TPU v7x, 32 devices: a whole 2x2x4 slice. The times are simulated.
32 devices in a mesh: clip: 4 (over z), frame: 2 (over y), row: 4 (over x, core).
Axes of the slice: x: 2, y: 2, z: 4, core: 2. Of those that a mesh axis runs over, the one named last changes fastest.
Arguments:
- tokens: bfloat16 [16, 256, 8, 1024], P('frame', 'row', 'clip'), may hold values from -6 to 6
- context: int32 [8], P('clip'), may hold values from 1 to 15
- noise_mod: float32 [16, 8, 6, 1024], P('frame', 'clip'), may hold values from -4 to 4
- clean_mod: float32 [6, 1024], replicated, may hold values from -4 to 4
- w_qkv: bfloat16 [1024, 3072], replicated, may hold values from -0.1875 to 0.1875
- b_qkv: float32 [3072], replicated, may hold values from -3 to 3
- w_out: bfloat16 [1024, 1024], replicated, may hold values from -1.5 to 1.5
- b_out: float32 [1024], replicated, may hold values from -3 to 3
- w_up: bfloat16 [1024, 4096], replicated, may hold values from -0.1875 to 0.1875
- b_up: float32 [4096], replicated, may hold values from -3 to 3
- w_down: bfloat16 [4096, 1024], replicated, may hold values from -0.09375 to 0.09375
- b_down: float32 [1024], replicated, may hold values from -3 to 3
- cotangent: bfloat16 [16, 256, 8, 1024], P('frame', 'row', 'clip'), may hold values from -6 to 6
Outputs:
- output: bfloat16 [16, 256, 8, 1024], P('frame', 'row', 'clip')
- grad_tokens: float32 [16, 256, 8, 1024], P('frame', 'row', 'clip')
- grad_noise_mod: float32 [16, 8, 6, 1024], P('frame', 'clip', None, 'row')
- grad_clean_mod: float32 [6, 1024], P(None, ('clip', 'frame', 'row'))
- grad_w_qkv: float32 [1024, 3072], P(('clip', 'frame', 'row'))
- grad_b_qkv: float32 [3072], P(('clip', 'frame', 'row'))
- grad_w_out: float32 [1024, 1024], P(('clip', 'frame', 'row'))
- grad_b_out: float32 [1024], P(('clip', 'frame', 'row'))
- grad_w_up: float32 [1024, 4096], P(('clip', 'frame', 'row'))
- grad_b_up: float32 [4096], P(('clip', 'frame', 'row'))
- grad_w_down: float32 [4096, 1024], P(('clip', 'frame', 'row'))
- grad_b_down: float32 [1024], P(('clip', 'frame', 'row'))
Inputs may be any that keep to these rules, and one draw needn't show every extreme that they name: The first context[c] frames of clip c are clean context.
All inputs are finite; a program needn't handle non-finite values.
Results may differ from a plain program's by a relative error of at most 0.017.
The roundings to bfloat16 on the way count: a program that leaves them out, or rounds other values in their place, can miss the bound.
Values may be sent and summed in bfloat16 or wider, within the bound.
A program may use at most 384 MiB of HBM per device.

v0:
```python
from functools import partial

import jax
import jax.numpy as jnp
from jax import lax
from jax.sharding import PartitionSpec as P

HEAD_DIM = 64
GRID = 16


def rope_angles(frame_pos, patch_pos):
    pair_index = jnp.arange(32)
    is_time = pair_index < 8
    is_height = (pair_index >= 8) & (pair_index < 20)
    exponent = jnp.where(
        is_time,
        pair_index / 8.0,
        jnp.where(is_height, (pair_index - 8) / 12.0, (pair_index - 20) / 12.0),
    ).astype(jnp.float32)
    frequency = jnp.power(jnp.float32(10000.0), -exponent)
    position = jnp.where(
        is_time[None, :],
        frame_pos[:, None],
        jnp.where(is_height[None, :], (patch_pos // GRID)[:, None], (patch_pos % GRID)[:, None]),
    ).astype(jnp.float32)
    angle = position * frequency[None, :]
    return (jnp.cos(angle), jnp.sin(angle))


def rotate(values_in, cosine, sine_table):
    half_dim = values_in.shape[-1] // 2
    shape_b = (cosine.shape[0],) + (1,) * (values_in.ndim - 2) + (half_dim,)
    cos_b = cosine.reshape(shape_b)
    sin_b = sine_table.reshape(shape_b)
    first_half = values_in[..., :half_dim]
    second_half = values_in[..., half_dim:]
    return jnp.concatenate(
        [first_half * cos_b - second_half * sin_b, first_half * sin_b + second_half * cos_b],
        axis=-1,
    )


def normalize(values_in):
    centre = values_in - jnp.mean(values_in, axis=-1, keepdims=True)
    inverse = lax.rsqrt(jnp.mean(centre * centre, axis=-1, keepdims=True) + 1e-06)
    return (centre * inverse, inverse)


def norm_back(grad_in, normed, inverse):
    first_mean = jnp.mean(grad_in, axis=-1, keepdims=True)
    second_mean = jnp.mean(grad_in * normed, axis=-1, keepdims=True)
    return inverse * (grad_in - first_mean - normed * second_mean)


def key_frames(row_ids, layout):
    shard_rows, row_split, shard_frames, patch_count = layout
    return row_ids // shard_rows // row_split * shard_frames + row_ids % shard_rows // patch_count


def fold_block(state_in, key_block, value_block, frames_k, queries, query_frames):
    running_max, weight_sum, accum = state_in
    q_count, clip_count, packed = queries.shape
    head_count = packed // HEAD_DIM
    row_count = key_block.shape[0]
    q_four = queries.reshape(q_count, clip_count, head_count, HEAD_DIM)
    k_four = key_block.reshape(row_count, clip_count, head_count, HEAD_DIM)
    v_four = value_block.reshape(row_count, clip_count, head_count, HEAD_DIM)
    scores = jnp.einsum(
        "qchd,kchd->chqk", q_four, k_four, preferred_element_type=jnp.float32
    ) * HEAD_DIM ** (-0.5)
    allowed = frames_k[None, :] <= query_frames[:, None]
    scores = jnp.where(allowed, scores, -jnp.inf)
    new_max = jnp.maximum(running_max, jnp.max(scores, axis=-1))
    factor = jnp.exp(running_max - new_max)
    weights = jnp.exp(scores - new_max[..., None])
    weight_sum = weight_sum * factor + jnp.sum(weights, axis=-1)
    accum = accum * factor[..., None] + jnp.einsum(
        "chqk,kchd->chqd", weights.astype(jnp.bfloat16), v_four, preferred_element_type=jnp.float32
    )
    return (new_max, weight_sum, accum)


def fold_piece(state_now, pieces_now, queries, query_frames, layout):
    key_piece, value_piece = pieces_now
    row_count = key_piece.shape[0]
    block_rows = 512
    latest = jnp.max(query_frames)

    def fold_advance(block_number, state_in):
        offset = block_number * block_rows
        key_block = lax.dynamic_slice_in_dim(key_piece, offset, block_rows, 0)
        value_block = lax.dynamic_slice_in_dim(value_piece, offset, block_rows, 0)
        frames_k = key_frames(offset + jnp.arange(block_rows), layout)
        return lax.cond(
            jnp.min(frames_k) <= latest,
            lambda carried: fold_block(
                carried, key_block, value_block, frames_k, queries, query_frames
            ),
            lambda carried: carried,
            state_in,
        )

    return lax.fori_loop(0, row_count // block_rows, fold_advance, state_now)


def fold_start(queries):
    q_count, clip_count, packed = queries.shape
    head_count = packed // HEAD_DIM
    return (
        jnp.full((clip_count, head_count, q_count), -1e30, jnp.float32),
        jnp.zeros((clip_count, head_count, q_count), jnp.float32),
        jnp.zeros((clip_count, head_count, q_count, HEAD_DIM), jnp.float32),
    )


def fold_finish(state_out):
    running_max, weight_sum, accum = state_out
    log_sums = running_max + jnp.log(weight_sum)
    attn_four = (accum / weight_sum[..., None]).transpose(2, 0, 1, 3)
    q_count, clip_count, head_count, head_size = attn_four.shape
    return (attn_four.reshape(q_count, clip_count, head_count * head_size), log_sums)


def block_terms(
    queries, grads_out, query_frames, log_sums, deltas, key_block, value_block, frames_k
):
    q_count, clip_count, packed = queries.shape
    head_count = packed // HEAD_DIM
    row_count = key_block.shape[0]
    q_four = queries.reshape(q_count, clip_count, head_count, HEAD_DIM)
    go_four = grads_out.reshape(q_count, clip_count, head_count, HEAD_DIM)
    k_four = key_block.reshape(row_count, clip_count, head_count, HEAD_DIM)
    v_four = value_block.reshape(row_count, clip_count, head_count, HEAD_DIM)
    scores = jnp.einsum(
        "qchd,kchd->chqk", q_four, k_four, preferred_element_type=jnp.float32
    ) * HEAD_DIM ** (-0.5)
    allowed = frames_k[None, :] <= query_frames[:, None]
    probs = jnp.exp(jnp.where(allowed, scores - log_sums[..., None], -jnp.inf))
    dprob = jnp.einsum("qchd,kchd->chqk", go_four, v_four, preferred_element_type=jnp.float32)
    dscore = (probs * (dprob - deltas[..., None])).astype(jnp.bfloat16)
    return (probs, dscore)


def query_grads(queries, grads_out, query_frames, log_sums, deltas, keys_all, values_all, layout):
    q_count, clip_count, packed = queries.shape
    head_count = packed // HEAD_DIM
    total_rows = keys_all.shape[0]
    block_rows = 512
    latest = jnp.max(query_frames)

    def query_advance(block_number, accum):
        offset = block_number * block_rows
        key_block = lax.dynamic_slice_in_dim(keys_all, offset, block_rows, 0)
        value_block = lax.dynamic_slice_in_dim(values_all, offset, block_rows, 0)
        frames_k = key_frames(offset + jnp.arange(block_rows), layout)

        def query_work(carried):
            probs, dscore = block_terms(
                queries, grads_out, query_frames, log_sums, deltas, key_block, value_block, frames_k
            )
            k_four = key_block.reshape(block_rows, clip_count, head_count, HEAD_DIM)
            return carried + jnp.einsum(
                "chqk,kchd->qchd", dscore, k_four, preferred_element_type=jnp.float32
            )

        return lax.cond(jnp.min(frames_k) <= latest, query_work, lambda carried: carried, accum)

    start_acc = jnp.zeros((q_count, clip_count, head_count, HEAD_DIM), jnp.float32)
    summed = lax.fori_loop(0, total_rows // block_rows, query_advance, start_acc) * HEAD_DIM ** (
        -0.5
    )
    return summed.reshape(q_count, clip_count, packed)


def kv_terms(
    first_row,
    row_count,
    queries,
    grads_out,
    query_frames,
    log_sums,
    deltas,
    keys_all,
    values_all,
    layout,
):
    q_count, clip_count, packed = queries.shape
    head_count = packed // HEAD_DIM
    block_rows = 512
    q_four = queries.reshape(q_count, clip_count, head_count, HEAD_DIM)
    go_four = grads_out.reshape(q_count, clip_count, head_count, HEAD_DIM)
    latest = jnp.max(query_frames)

    def one_block(block_number):
        offset = block_number * block_rows
        key_block = lax.dynamic_slice_in_dim(keys_all, offset, block_rows, 0)
        value_block = lax.dynamic_slice_in_dim(values_all, offset, block_rows, 0)
        frames_k = key_frames(offset + jnp.arange(block_rows), layout)

        def one_work(unused):
            probs, dscore = block_terms(
                queries, grads_out, query_frames, log_sums, deltas, key_block, value_block, frames_k
            )
            grad_value = jnp.einsum(
                "chqk,qchd->kchd",
                probs.astype(jnp.bfloat16),
                go_four,
                preferred_element_type=jnp.float32,
            )
            grad_key = jnp.einsum(
                "chqk,qchd->kchd", dscore, q_four, preferred_element_type=jnp.float32
            ) * HEAD_DIM ** (-0.5)
            return jnp.concatenate(
                [
                    grad_key.reshape(block_rows, clip_count, packed),
                    grad_value.reshape(block_rows, clip_count, packed),
                ],
                axis=-1,
            )

        def empty(unused):
            return jnp.zeros((block_rows, clip_count, 2 * packed), jnp.float32)

        return lax.cond(jnp.min(frames_k) <= latest, one_work, empty, jnp.int32(0))

    blocks = lax.map(one_block, jnp.arange(row_count // block_rows))
    return blocks.reshape(row_count, clip_count, 2 * packed)


def output_deltas(grads_out, attn_float):
    q_count, clip_count, packed = attn_float.shape
    head_count = packed // HEAD_DIM
    product = (grads_out.astype(jnp.float32) * attn_float).reshape(
        q_count, clip_count, head_count, HEAD_DIM
    )
    return jnp.sum(product, axis=-1).transpose(1, 2, 0)


def on_device(
    tokens,
    context,
    noise_mod,
    clean_mod,
    w_qkv,
    b_qkv,
    w_out,
    b_out,
    w_up,
    b_up,
    w_down,
    b_down,
    cotangent,
):
    frame_count, patch_local, clip_count, model_width = tokens.shape
    shard_rows = frame_count * patch_local
    row_total = shard_rows * clip_count
    heads_all = model_width // HEAD_DIM
    frame_index = lax.axis_index("frame")
    row_index = lax.axis_index("row")
    row_devices = lax.axis_size("row")
    local_frames = frame_index * frame_count + jnp.arange(frame_count)
    is_clean = local_frames[:, None] < context[None, :]
    modulation = jnp.where(is_clean[:, :, None, None], clean_mod[None, None], noise_mod)
    mod_tok = modulation[:, None]
    shift_one, scale_one, gate_one = (mod_tok[:, :, :, 0], mod_tok[:, :, :, 1], mod_tok[:, :, :, 2])
    shift_two, scale_two, gate_two = (mod_tok[:, :, :, 3], mod_tok[:, :, :, 4], mod_tok[:, :, :, 5])
    inputs = tokens.astype(jnp.float32)
    normed_one, inverse_one = normalize(inputs)
    hidden_one = (
        (normed_one * (1.0 + scale_one) + shift_one)
        .astype(jnp.bfloat16)
        .reshape(row_total, model_width)
    )
    projected = jnp.dot(hidden_one, w_qkv, preferred_element_type=jnp.float32) + b_qkv
    proj_four = projected.reshape(shard_rows, clip_count, 3 * heads_all, HEAD_DIM)
    tok_index = jnp.arange(shard_rows)
    tok_frames = frame_index * frame_count + tok_index // patch_local
    tok_patch = row_index * patch_local + tok_index % patch_local
    cosine, sine_table = rope_angles(tok_frames, tok_patch)
    query_rot = rotate(proj_four[:, :, :heads_all], cosine, sine_table).astype(jnp.bfloat16)
    key_rot = rotate(proj_four[:, :, heads_all : 2 * heads_all], cosine, sine_table).astype(
        jnp.bfloat16
    )
    value_low = proj_four[:, :, 2 * heads_all :].astype(jnp.bfloat16)
    queries_now = query_rot.reshape(shard_rows, clip_count, model_width)
    keys_now = key_rot.reshape(shard_rows, clip_count, model_width)
    values_now = value_low.reshape(shard_rows, clip_count, model_width)
    layout = (shard_rows, row_devices, frame_count, patch_local)
    state_out = fold_piece(
        fold_start(queries_now),
        (
            lax.all_gather(keys_now, ("frame", "row"), axis=0, tiled=True),
            lax.all_gather(values_now, ("frame", "row"), axis=0, tiled=True),
        ),
        queries=queries_now,
        query_frames=tok_frames,
        layout=layout,
    )
    attn_float, log_sums = fold_finish(state_out)
    attn_low = attn_float.astype(jnp.bfloat16).reshape(row_total, model_width)
    branch = (jnp.dot(attn_low, w_out, preferred_element_type=jnp.float32) + b_out).reshape(
        tokens.shape
    )
    mixed = inputs + gate_one * branch
    normed_two, inverse_two = normalize(mixed)
    hidden_two = (
        (normed_two * (1.0 + scale_two) + shift_two)
        .astype(jnp.bfloat16)
        .reshape(row_total, model_width)
    )
    pre_act = jnp.dot(hidden_two, w_up, preferred_element_type=jnp.float32) + b_up
    act_low = jax.nn.gelu(pre_act, approximate=True).astype(jnp.bfloat16)
    down_out = (jnp.dot(act_low, w_down, preferred_element_type=jnp.float32) + b_down).reshape(
        tokens.shape
    )
    result = mixed + gate_two * down_out
    grad_result = cotangent.astype(jnp.float32)
    grad_down = (grad_result * gate_two).astype(jnp.bfloat16).reshape(row_total, model_width)
    grad_gate_two = grad_result * down_out
    dw_down = jnp.einsum("nf,nd->fd", act_low, grad_down, preferred_element_type=jnp.float32)
    db_down = jnp.sum(grad_down, axis=0, dtype=jnp.float32)
    grad_act = jnp.einsum("nd,fd->nf", grad_down, w_down, preferred_element_type=jnp.float32)
    _, gelu_pull = jax.vjp(partial(jax.nn.gelu, approximate=True), pre_act)
    grad_pre = gelu_pull(grad_act)[0].astype(jnp.bfloat16)
    dw_up = jnp.einsum("nd,nf->df", hidden_two, grad_pre, preferred_element_type=jnp.float32)
    db_up = jnp.sum(grad_pre, axis=0, dtype=jnp.float32)
    grad_hidden_two = jnp.einsum(
        "nf,df->nd", grad_pre, w_up, preferred_element_type=jnp.float32
    ).reshape(tokens.shape)
    grad_mixed = grad_result + norm_back(
        grad_hidden_two * (1.0 + scale_two), normed_two, inverse_two
    )
    grad_gate_one = grad_mixed * branch
    grad_branch = (grad_mixed * gate_one).astype(jnp.bfloat16).reshape(row_total, model_width)
    dw_out = jnp.einsum("nd,ne->de", attn_low, grad_branch, preferred_element_type=jnp.float32)
    db_out = jnp.sum(grad_branch, axis=0, dtype=jnp.float32)
    grad_attn = jnp.einsum(
        "ne,de->nd", grad_branch, w_out, preferred_element_type=jnp.float32
    ).astype(jnp.bfloat16)
    grads_out = grad_attn.reshape(shard_rows, clip_count, model_width)
    deltas = output_deltas(grads_out, attn_float)
    keys_all, values_all = (
        lax.all_gather(keys_now, ("frame", "row"), axis=0, tiled=True),
        lax.all_gather(values_now, ("frame", "row"), axis=0, tiled=True),
    )
    grad_query = query_grads(
        queries_now, grads_out, tok_frames, log_sums, deltas, keys_all, values_all, layout
    )
    kv_fn = partial(
        kv_terms,
        queries=queries_now,
        grads_out=grads_out,
        query_frames=tok_frames,
        log_sums=log_sums,
        deltas=deltas,
        keys_all=keys_all,
        values_all=values_all,
        layout=layout,
    )
    kv_sum = lax.psum_scatter(
        kv_fn(jnp.int32(0), shard_rows * lax.axis_size(("frame", "row"))).astype(jnp.bfloat16),
        ("frame", "row"),
        scatter_dimension=0,
        tiled=True,
    ).astype(jnp.float32)
    tok_four = (shard_rows, clip_count, heads_all, HEAD_DIM)
    back_q = rotate(grad_query.reshape(tok_four), cosine, -sine_table)
    back_k = rotate(kv_sum[:, :, :model_width].reshape(tok_four), cosine, -sine_table)
    back_v = kv_sum[:, :, model_width:].reshape(tok_four)
    grad_proj = (
        jnp.concatenate([back_q, back_k, back_v], axis=2)
        .astype(jnp.bfloat16)
        .reshape(row_total, 3 * model_width)
    )
    dw_qkv = jnp.einsum("nd,ne->de", hidden_one, grad_proj, preferred_element_type=jnp.float32)
    db_qkv = jnp.sum(grad_proj, axis=0, dtype=jnp.float32)
    grad_hidden_one = jnp.einsum(
        "ne,de->nd", grad_proj, w_qkv, preferred_element_type=jnp.float32
    ).reshape(tokens.shape)
    grad_tokens = grad_mixed + norm_back(
        grad_hidden_one * (1.0 + scale_one), normed_one, inverse_one
    )
    mod_terms = [
        grad_hidden_one,
        grad_hidden_one * normed_one,
        grad_gate_one,
        grad_hidden_two,
        grad_hidden_two * normed_two,
        grad_gate_two,
    ]
    grad_mods = jnp.stack([jnp.sum(term, axis=1) for term in mod_terms], axis=2)
    noise_part = jnp.where(is_clean[:, :, None, None], 0.0, grad_mods)
    clean_part = jnp.sum(jnp.where(is_clean[:, :, None, None], grad_mods, 0.0), axis=(0, 1))
    grad_noise = lax.psum_scatter(
        noise_part.astype(jnp.bfloat16), "row", scatter_dimension=3, tiled=True
    ).astype(jnp.float32)
    gw_qkv, gb_qkv, gw_out, gb_out, gw_up, gb_up, gw_down, gb_down, grad_clean = (
        lax.psum_scatter(dw_qkv, ("clip", "frame", "row"), scatter_dimension=0, tiled=True),
        lax.psum_scatter(db_qkv, ("clip", "frame", "row"), scatter_dimension=0, tiled=True),
        lax.psum_scatter(dw_out, ("clip", "frame", "row"), scatter_dimension=0, tiled=True),
        lax.psum_scatter(db_out, ("clip", "frame", "row"), scatter_dimension=0, tiled=True),
        lax.psum_scatter(dw_up, ("clip", "frame", "row"), scatter_dimension=0, tiled=True),
        lax.psum_scatter(db_up, ("clip", "frame", "row"), scatter_dimension=0, tiled=True),
        lax.psum_scatter(dw_down, ("clip", "frame", "row"), scatter_dimension=0, tiled=True),
        lax.psum_scatter(db_down, ("clip", "frame", "row"), scatter_dimension=0, tiled=True),
        lax.psum_scatter(clean_part, ("clip", "frame", "row"), scatter_dimension=1, tiled=True),
    )
    return (
        result.astype(jnp.bfloat16),
        grad_tokens,
        grad_noise,
        grad_clean,
        gw_qkv,
        gb_qkv,
        gw_out,
        gb_out,
        gw_up,
        gb_up,
        gw_down,
        gb_down,
    )


def solution(mesh):
    placed = (
        P("frame", "row", "clip", None),
        P("clip"),
        P("frame", "clip", None, None),
        P(),
        P(),
        P(),
        P(),
        P(),
        P(),
        P(),
        P(),
        P(),
        P("frame", "row", "clip", None),
    )
    return jax.shard_map(
        on_device,
        mesh=mesh,
        in_specs=placed,
        out_specs=(
            P("frame", "row", "clip", None),
            P("frame", "row", "clip", None),
            P("frame", "clip", None, "row"),
            P(None, ("clip", "frame", "row")),
            P(("clip", "frame", "row"), None),
            P(("clip", "frame", "row")),
            P(("clip", "frame", "row"), None),
            P(("clip", "frame", "row")),
            P(("clip", "frame", "row"), None),
            P(("clip", "frame", "row")),
            P(("clip", "frame", "row"), None),
            P(("clip", "frame", "row")),
        ),
        check_vma=False,
    )
```

profile of v0, /device:TPU:1, one launch (start us, length us, event | category | flops | bytes accessed | tf_op | source)
XLA Modules:
  0.0 2922.3 jit_solution(3532392246752427041)
XLA Ops:
  116.4 44.3 %all-gather.5.cloned.1.call-done = bf16[4096,2,1024]{0,2,1:T(8,128)(2,1)} async-done(((bf16[512,2,1024]{0,2,1:T(8,128)(2,1)}), bf16[4096,2,1024]{0,2,1:T(8,128)(2,1)}) %all-gather.5.cloned.1.call-update) | async-done | bytes 16777232 | tf_op jit(solution)/shard_map/all_gather | solution.py:294
  160.7 95.6 %all-gather.3.cloned.1.call-done = bf16[4096,2,1024]{0,2,1:T(8,128)(2,1)} async-done(((bf16[512,2,1024]{0,2,1:T(8,128)(2,1)}), bf16[4096,2,1024]{0,2,1:T(8,128)(2,1)}) %all-gather.3.cloned.1.call-update) | async-done | bytes 16777232 | tf_op jit(solution)/shard_map/all_gather | solution.py:293
  258.9 218.7 %while.55 = (s32[]{:T(128)}, f32[2,16,512]{2,1,0:T(8,128)S(1)}, f32[2,16,512]{2,1,0:T(8,128)S(1)}, f32[2,16,512,64]{2,3,1,0:T(8,128)}, s32[]{:T(128)}, /*index=5...) while((s32[]{:T(128)}, f32[2,16,512]{2,1,0:T(8,128)S(1)}, ...), condition=%wide.region_9.10_spmd.clone, body=%wide.region_3.9_spmd.clone.sunk | while | flops 2242182144 | bytes 134250944 | solution.py:104
  260.9 50.6 %conditional.9 = ((f32[2,16,512]{2,1,0:T(8,128)S(1)}, f32[2,16,512]{2,1,0:T(8,128)S(1)}, f32[2,16,512,64]{2,3,1,0:T(8,128)})) conditional(s32[]{:T(128)} %convert_element_type.328, (f32[2,16,512]{2,1,0:T(8,128)S(1)}, f32[2,16,512]{2,1,0:T(8,128)S(1)}, f32[2,16,512,64]{2,3,1,0:T(8,128)}) %tuple.237, (s32[512]{0:T(512)S(1)}, s32[]{:T(128)}, s32[]{:T(128)}, ...), branch_computations={%region_5.5_spmd, %region_6.8_spmd} | conditional | flops 2242154496 | bytes 134238304 | solution.py:95
  313.5 50.6 %conditional.9 = ((f32[2,16,512]{2,1,0:T(8,128)S(1)}, f32[2,16,512]{2,1,0:T(8,128)S(1)}, f32[2,16,512,64]{2,3,1,0:T(8,128)})) conditional(s32[]{:T(128)} %convert_element_type.328, (f32[2,16,512]{2,1,0:T(8,128)S(1)}, f32[2,16,512]{2,1,0:T(8,128)S(1)}, f32[2,16,512,64]{2,3,1,0:T(8,128)}) %tuple.237, (s32[512]{0:T(512)S(1)}, s32[]{:T(128)}, s32[]{:T(128)}, ...), branch_computations={%region_5.5_spmd, %region_6.8_spmd} | conditional | flops 2242154496 | bytes 134238304 | solution.py:95
  366.2 50.6 %conditional.9 = ((f32[2,16,512]{2,1,0:T(8,128)S(1)}, f32[2,16,512]{2,1,0:T(8,128)S(1)}, f32[2,16,512,64]{2,3,1,0:T(8,128)})) conditional(s32[]{:T(128)} %convert_element_type.328, (f32[2,16,512]{2,1,0:T(8,128)S(1)}, f32[2,16,512]{2,1,0:T(8,128)S(1)}, f32[2,16,512,64]{2,3,1,0:T(8,128)}) %tuple.237, (s32[512]{0:T(512)S(1)}, s32[]{:T(128)}, s32[]{:T(128)}, ...), branch_computations={%region_5.5_spmd, %region_6.8_spmd} | conditional | flops 2242154496 | bytes 134238304 | solution.py:95
  418.8 50.6 %conditional.9 = ((f32[2,16,512]{2,1,0:T(8,128)S(1)}, f32[2,16,512]{2,1,0:T(8,128)S(1)}, f32[2,16,512,64]{2,3,1,0:T(8,128)})) conditional(s32[]{:T(128)} %convert_element_type.328, (f32[2,16,512]{2,1,0:T(8,128)S(1)}, f32[2,16,512]{2,1,0:T(8,128)S(1)}, f32[2,16,512,64]{2,3,1,0:T(8,128)}) %tuple.237, (s32[512]{0:T(512)S(1)}, s32[]{:T(128)}, s32[]{:T(128)}, ...), branch_computations={%region_5.5_spmd, %region_6.8_spmd} | conditional | flops 2242154496 | bytes 134238304 | solution.py:95
  579.8 26.8 convert_reduce_fusion.1
  678.2 399.3 %while.57 = (s32[]{:T(128)}, bf16[8,512,2,2048]{3,1,0,2:T(8,128)(2,1)}, s32[8]{0:T(128)S(1)}, s32[]{:T(128)}, bf16[4096,2,1024]{0,2,1:T(8,128)(2,1)}, /*index=5*...) while((s32[]{:T(128)}, ...), condition=%wide.region_24.25_spmd.clone, body=%wide.region_20.24_spmd.clone.sunk | while | flops 4389633024 | bytes 156205488 | solution.py:227
  681.9 68.6 %conditional.11 = (bf16[1,512,2,2048]{1,3,2,0:T(8,128)(2,1)}) conditional(s32[]{:T(128)} %convert_element_type.330, () %tuple.244, (s32[512]{0:T(512)S(1)}, s32[]{:T(128)}, s32[]{:T(128)}, bf16[4096,2,1024]{0,2,1:T(8,128)(2,1)}, bf16[512,2,16,64]{0,3,2,1:T(8,128)(2,1)S(1)}, /*index=5*/f32[2,16,512]{2,1,0:T(8,128)S(1)}, ...), branch_computations={%region_22.22_spmd, %region_23.23_spmd} | conditional | flops 4389605376 | bytes 139415616 | solution.py:225
  764.9 68.6 %conditional.11 = (bf16[1,512,2,2048]{1,3,2,0:T(8,128)(2,1)}) conditional(s32[]{:T(128)} %convert_element_type.330, () %tuple.244, (s32[512]{0:T(512)S(1)}, s32[]{:T(128)}, s32[]{:T(128)}, bf16[4096,2,1024]{0,2,1:T(8,128)(2,1)}, bf16[512,2,16,64]{0,3,2,1:T(8,128)(2,1)S(1)}, /*index=5*/f32[2,16,512]{2,1,0:T(8,128)S(1)}, ...), branch_computations={%region_22.22_spmd, %region_23.23_spmd} | conditional | flops 4389605376 | bytes 139415616 | solution.py:225
  847.9 68.6 %conditional.11 = (bf16[1,512,2,2048]{1,3,2,0:T(8,128)(2,1)}) conditional(s32[]{:T(128)} %convert_element_type.330, () %tuple.244, (s32[512]{0:T(512)S(1)}, s32[]{:T(128)}, s32[]{:T(128)}, bf16[4096,2,1024]{0,2,1:T(8,128)(2,1)}, bf16[512,2,16,64]{0,3,2,1:T(8,128)(2,1)S(1)}, /*index=5*/f32[2,16,512]{2,1,0:T(8,128)S(1)}, ...), branch_computations={%region_22.22_spmd, %region_23.23_spmd} | conditional | flops 4389605376 | bytes 139415616 | solution.py:225
  930.8 68.6 %conditional.11 = (bf16[1,512,2,2048]{1,3,2,0:T(8,128)(2,1)}) conditional(s32[]{:T(128)} %convert_element_type.330, () %tuple.244, (s32[512]{0:T(512)S(1)}, s32[]{:T(128)}, s32[]{:T(128)}, bf16[4096,2,1024]{0,2,1:T(8,128)(2,1)}, bf16[512,2,16,64]{0,3,2,1:T(8,128)(2,1)S(1)}, /*index=5*/f32[2,16,512]{2,1,0:T(8,128)S(1)}, ...), branch_computations={%region_22.22_spmd, %region_23.23_spmd} | conditional | flops 4389605376 | bytes 139415616 | solution.py:225
  1084.1 205.3 %while.56 = (s32[]{:T(128)}, f32[512,2,16,64]{0,3,2,1:T(8,128)}, s32[]{:T(128)}, bf16[4096,2,1024]{0,2,1:T(8,128)(2,1)}, bf16[512,2,16,64]{0,3,2,1:T(8,128)(2,1)...) while((s32[]{:T(128)}, f32[512,2,16,64]{0,3,2,1:T(8,128)}, ...), condition=%wide.region_19.20_spmd.clone, body=%wide.region_15.19_spmd.clone.sunk | while | flops 3272899584 | bytes 99254656 | solution.py:170
  1086.2 47.1 %conditional.10 = (f32[512,2,16,64]{0,3,2,1:T(8,128)}) conditional(s32[]{:T(128)} %convert_element_type.329, f32[512,2,16,64]{0,3,2,1:T(8,128)} %get-tuple-element.1869, (s32[512]{0:T(512)S(1)}, s32[]{:T(128)}, s32[]{:T(128)}, bf16[4096,2,1024]{0,2,1:T(8,128)(2,1)}, bf16[512,2,16,64]{0,3,2,1:T(8,128)(2,1)S(1)}, ...), branch_computations={%region_17.17_spmd, %region_18.18_spmd} | conditional | flops 3272871936 | bytes 99242040 | solution.py:167
  1135.3 47.1 %conditional.10 = (f32[512,2,16,64]{0,3,2,1:T(8,128)}) conditional(s32[]{:T(128)} %convert_element_type.329, f32[512,2,16,64]{0,3,2,1:T(8,128)} %get-tuple-element.1869, (s32[512]{0:T(512)S(1)}, s32[]{:T(128)}, s32[]{:T(128)}, bf16[4096,2,1024]{0,2,1:T(8,128)(2,1)}, bf16[512,2,16,64]{0,3,2,1:T(8,128)(2,1)S(1)}, ...), branch_computations={%region_17.17_spmd, %region_18.18_spmd} | conditional | flops 3272871936 | bytes 99242040 | solution.py:167
  1184.5 47.1 %conditional.10 = (f32[512,2,16,64]{0,3,2,1:T(8,128)}) conditional(s32[]{:T(128)} %convert_element_type.329, f32[512,2,16,64]{0,3,2,1:T(8,128)} %get-tuple-element.1869, (s32[512]{0:T(512)S(1)}, s32[]{:T(128)}, s32[]{:T(128)}, bf16[4096,2,1024]{0,2,1:T(8,128)(2,1)}, bf16[512,2,16,64]{0,3,2,1:T(8,128)(2,1)S(1)}, ...), branch_computations={%region_17.17_spmd, %region_18.18_spmd} | conditional | flops 3272871936 | bytes 99242040 | solution.py:167
  1233.7 47.1 %conditional.10 = (f32[512,2,16,64]{0,3,2,1:T(8,128)}) conditional(s32[]{:T(128)} %convert_element_type.329, f32[512,2,16,64]{0,3,2,1:T(8,128)} %get-tuple-element.1869, (s32[512]{0:T(512)S(1)}, s32[]{:T(128)}, s32[]{:T(128)}, bf16[4096,2,1024]{0,2,1:T(8,128)(2,1)}, bf16[512,2,16,64]{0,3,2,1:T(8,128)(2,1)S(1)}, ...), branch_computations={%region_17.17_spmd, %region_18.18_spmd} | conditional | flops 3272871936 | bytes 99242040 | solution.py:167
  1306.3 443.4 %reduce-scatter.12.cloned.1.call-done = bf16[512,2,2048]{2,0,1:T(8,128)(2,1)} async-done(((bf16[4096,2,2048]{2,0,1:T(8,128)(2,1)}), bf16[512,2,2048]{2,0,1:T(8,128)(2,1)}) %reduce-scatter.12.cloned.1.call-update) | async-done | bytes 4194320 | tf_op jit(solution)/shard_map/reduce_scatter | solution.py:361
  1981.9 267.0 %all-reduce.4 = (f32[3072]{0:T(1024)S(1)}, f32[1024]{0:T(1024)S(1)}, f32[4096]{0:T(1024)S(1)}, f32[1024]{0:T(1024)S(1)}) all-reduce(f32[3072]{0:T(1024)S(1)} %reduce_sum.211, f32[1024]{0:T(1024)S(1)} %copy-done.47, f32[4096]{0:T(1024)S(1)} %copy-done.48, ...), channel_id=6, replica_groups=mesh['clip'=4,'frame'=2,'row'=4] {'clip','frame','row'}, use_global_device_ids=true, to_apply=%region_39.40.clone | all-reduce | flops 9216 | bytes 73728
  2274.6 102.9 %reduce-scatter.16.cloned.1.call-done = f32[32,1024]{1,0:T(8,128)} async-done(((f32[1024,1024]{1,0:T(8,128)}), f32[32,1024]{1,0:T(8,128)}) %reduce-scatter.16.cloned.1.call-update) | async-done | bytes 131088 | tf_op jit(solution)/shard_map/reduce_scatter | solution.py:401
  2377.5 187.5 %reduce-scatter.20.cloned.1.call-done = f32[128,1024]{1,0:T(8,128)} async-done(((f32[4096,1024]{1,0:T(8,128)}), f32[128,1024]{1,0:T(8,128)}) %reduce-scatter.20.cloned.1.call-update) | async-done | bytes 524304 | tf_op jit(solution)/shard_map/reduce_scatter | solution.py:405
  2565.0 187.5 %reduce-scatter.18.cloned.1.call-done = f32[32,4096]{1,0:T(8,128)} async-done(((f32[1024,4096]{1,0:T(8,128)}), f32[32,4096]{1,0:T(8,128)}) %reduce-scatter.18.cloned.1.call-update) | async-done | bytes 524304 | tf_op jit(solution)/shard_map/reduce_scatter | solution.py:403
  2752.5 163.0 %reduce-scatter.14.cloned.1.call-done = f32[32,3072]{1,0:T(8,128)} async-done(((f32[1024,3072]{1,0:T(8,128)}), f32[32,3072]{1,0:T(8,128)}) %reduce-scatter.14.cloned.1.call-update) | async-done | bytes 393232 | tf_op jit(solution)/shard_map/reduce_scatter | solution.py:399
  (530 shorter events, 1359.4 us)
Async XLA Ops:
  7.2 493.6 %copy-start = (bf16[1024,1024]{1,0:T(8,128)(2,1)S(1)}, bf16[1024,1024]{1,0:T(8,128)(2,1)}, u32[]{:S(2)}) copy-start(bf16[1024,1024]{1,0:T(8,128)(2,1)} %param.31) | copy-start | bytes 6291460
  7.2 153.5 %all-gather.5.cloned.1.call-start = ((), (), s32[]{:S(2)}) async-start(), calls=%async_computation.8 | async-start | bytes 18874368 | tf_op jit(solution)/shard_map/all_gather | solution.py:294
  12.9 81.8 %copy-start.27 = (f32[8,2,1024]{2,1,0:T(2,128)}, f32[8,2,1024]{2,1,0:T(2,128)S(1)}, u32[]{:S(2)}) copy-start(f32[8,2,1024]{2,1,0:T(2,128)S(1)} %get-tuple-element.1536) | copy-start | bytes 196612
  65.0 191.4 %all-gather.3.cloned.1.call-start = ((), (), s32[]{:S(2)}) async-start(), calls=%async_computation.7 | async-start | bytes 18874368 | tf_op jit(solution)/shard_map/all_gather | solution.py:293
  67.3 18.1 copy-start.21
  94.6 1655.1 %reduce-scatter.12.cloned.1.call-start = ((), (), s32[]{:S(2)}) async-start(), calls=%async_computation.9 | async-start | bytes 37748736 | tf_op jit(solution)/shard_map/reduce_scatter | solution.py:361
  477.6 9.8 copy-start.11
  540.4 17.8 copy-start.50
  540.4 17.8 copy-start.54
  1077.6 1181.1 %reduce-scatter.24.cloned.1.call-start = ((), (), s32[]{:S(2)}) async-start(), calls=%async_computation.15 | async-start | bytes 540672
  1820.7 20.1 copy-start.8
  1820.7 20.1 copy-start.31
  1820.7 20.1 copy-start.40
  1820.7 20.1 copy-start.42
  1840.8 12.8 copy-start.9
  1840.8 12.8 copy-start.10
  1859.4 400.7 %reduce-scatter.22.cloned.1.call-start = ((), (), s32[]{:S(2)}) async-start(), calls=%async_computation.14 | async-start | bytes 327680
  1883.0 21.1 copy-start.23
  1904.0 473.5 %reduce-scatter.16.cloned.1.call-start = ((), (), s32[]{:S(2)}) async-start(), calls=%async_computation.11 | async-start | bytes 4325376 | tf_op jit(solution)/shard_map/reduce_scatter | solution.py:401
  1910.1 654.9 %reduce-scatter.20.cloned.1.call-start = ((), (), s32[]{:S(2)}) async-start(), calls=%async_computation.13 | async-start | bytes 17301504 | tf_op jit(solution)/shard_map/reduce_scatter | solution.py:405
  1931.4 821.1 %reduce-scatter.18.cloned.1.call-start = ((), (), s32[]{:S(2)}) async-start(), calls=%async_computation.12 | async-start | bytes 17301504 | tf_op jit(solution)/shard_map/reduce_scatter | solution.py:403
  1947.6 16.7 copy-start.24
  1947.6 967.9 %reduce-scatter.14.cloned.1.call-start = ((), (), s32[]{:S(2)}) async-start(), calls=%async_computation.10 | async-start | bytes 12976128 | tf_op jit(solution)/shard_map/reduce_scatter | solution.py:399
  2258.6 656.9 %copy-start.1 = (bf16[1024,1024]{1,0:T(8,128)(2,1)S(1)}, bf16[1024,1024]{1,0:T(8,128)(2,1)}, u32[]{:S(2)}) copy-start(bf16[1024,1024]{1,0:T(8,128)(2,1)} %param.31) | copy-start | bytes 6291460
  (45 other events, 213.5 us)
Sparse Core Ops, SparseCore 0:
  65.1 95.6 all-gather.4
  163.2 93.1 all-gather.2
  1077.7 671.9 reduce-scatter.11
  1859.5 356.0 reduce-scatter.23
  2218.0 21.0 reduce-scatter.21
  2241.9 135.5 reduce-scatter.15
  2380.5 184.4 reduce-scatter.19
  2568.0 184.4 reduce-scatter.17
  2760.2 155.3 reduce-scatter.13
where the time goes:
time: 2940 us; the launch traced here: 2920 us
  waiting for transfers between devices  1220 us (41%)
  matrix products  632 us (21%)
  local copies, waits for them, and re-layouts  526 us (18%)
  blocking collectives  267 us (9%)
  other arithmetic  218 us (7%)
  loops' own time  39.3 us (1%)
    reduce_scatter x1, waiting for transfers between devices, on_device(): lax.psum_scatter(kv_fn(jnp.int32(0), shard_rows * lax.axis_size(('frame',...  443 us
    unnamed x1, blocking collectives  267 us
    reduce_scatter x1, waiting for transfers between devices, on_device(): lax.psum_scatter(dw_up, ('clip', 'frame', 'row'), scatter_dimension=0, ti...  187 us
    reduce_scatter x1, waiting for transfers between devices, on_device(): lax.psum_scatter(dw_down, ('clip', 'frame', 'row'), scatter_dimension=0,...  187 us
    reduce_scatter x1, waiting for transfers between devices, on_device(): lax.psum_scatter(dw_qkv, ('clip', 'frame', 'row'), scatter_dimension=0, t...  163 us
    dot_general x8, matrix products, block_terms(): jnp.einsum('qchd,kchd->chqk', q_four, k_four, preferred_element_type=jnp....  118 us
    unnamed x132, local copies, waits for them, and re-layouts  115 us
    reduce_scatter x1, waiting for transfers between devices, on_device(): lax.psum_scatter(dw_out, ('clip', 'frame', 'row'), scatter_dimension=0, t...  103 us
  transfers between devices with their start and end apart: 9, of which 7 were waited for; matrix products, arithmetic and copies ran while one was open for 14% of the time, Pallas kernels for 0%

commit v1 on v0

v1 whole, which is shorter than its diff:
```python
import functools
import jax, jax.numpy as jnp
from jax import lax
from jax.experimental import pallas as pl
from jax.experimental.pallas import tpu as pltpu
from jax.sharding import PartitionSpec as P
HD = 64
NN = (((1,), (0,)), ((), ()))
NT = (((1,), (1,)), ((), ()))
def dot(a, b, dims):
    return lax.dot_general(a, b, dims, preferred_element_type=jnp.float32)

def head_mask(values, head, heads):
    if heads == 1:
        return values
    lane = lax.broadcasted_iota(jnp.int32, values.shape, 1)
    return jnp.where(lane // HD == head, values, jnp.zeros_like(values))


def fwd_kernel(x_ref, o_ref, ot_ref, lse_ref, qm, kf, vt, sb, acc, mrow):
    nf, nr, fl, pt, width = x_ref.shape
    lw = width // 3
    nh = lw // HD
    tok = nr * pt
    frames = nf * fl
    blk = 2 * tok
    nblk = frames // 2
    def load(f, _):
        part = x_ref[f // fl, :, f % fl].reshape(tok, width)
        rows = pl.ds(pl.multiple_of(f * tok, tok), tok)
        q = part[:, :lw] * jnp.bfloat16(HD ** -0.5)
        for h in range(nh):
            qm[h, rows, :] = head_mask(q, h, nh)
        kf[rows, :] = part[:, lw:2 * lw]
        vt[:, rows] = part[:, 2 * lw:].T
        return 0
    lax.fori_loop(0, frames, load, 0)

    def fold(v, op):
        return op(v.reshape(v.shape[0] // 8, 8, v.shape[1]), axis=0)

    def stage(cur, nxt, grow):
        zero8 = jnp.zeros((8, blk), jnp.float32)
        if nxt is not None:
            na, nhd, ns = nxt
            n0 = pl.multiple_of(na * blk, blk)
            n1 = pl.multiple_of(na * blk + tok, tok)
            ncols = pl.ds(n0, blk)
            s0 = dot(kf[pl.ds(n0, tok), :], qm[nhd, ncols, :], NT)
            s1 = dot(kf[pl.ds(n1, tok), :], qm[nhd, pl.ds(n1, tok), :], NT)
            sb[ns, pl.ds(n0, tok), :] = s0
            sb[ns, pl.ds(n1, tok), tok:] = s1
            m0 = fold(s0, jnp.max)
            mm = jnp.concatenate([m0[:, :tok], jnp.maximum(m0[:, tok:], fold(s1, jnp.max))], axis=1)
        else:
            mm = zero8
        if cur is not None:
            ca, chd, cs = cur
            hs = slice(chd * HD, (chd + 1) * HD)
            c0 = pl.multiple_of(ca * blk, blk)
            c1 = pl.multiple_of(ca * blk + tok, tok)
            m = mrow[cs]
            p0 = jnp.exp(sb[cs, pl.ds(c0, tok), :] - m)
            p1 = jnp.exp(sb[cs, pl.ds(c1, tok), tok:] - m[:, tok:])
            l0 = fold(p0, jnp.sum)
            ll = jnp.concatenate([l0[:, :tok], l0[:, tok:] + fold(p1, jnp.sum)], axis=1)
            a0 = dot(vt[hs, pl.ds(c0, tok)], p0.astype(jnp.bfloat16), NN)
            a1 = dot(vt[hs, pl.ds(c1, tok)], p1.astype(jnp.bfloat16), NN)
            acc[hs, :tok] = a0[:, :tok]
            acc[hs, tok:] = a0[:, tok:] + a1
        else:
            ll = zero8
        def score(b, mm):
            rows = pl.ds(pl.multiple_of(b * blk, blk), blk)
            s = dot(kf[rows, :], qm[nhd, ncols, :], NT)
            sb[ns, rows, :] = s
            return jnp.maximum(mm, fold(s, jnp.max))
        def body(b, carry):
            mm, ll = carry
            if nxt is not None:
                mm = score(b, mm)
            if cur is not None:
                rows = pl.ds(pl.multiple_of(b * blk, blk), blk)
                p = jnp.exp(sb[cs, rows, :] - m)
                ll = ll + fold(p, jnp.sum)
                acc[hs, :] += dot(vt[hs, rows], p.astype(jnp.bfloat16), NN)
            return mm, ll
        trip = nxt[0] if cur is None else cur[0]
        mm, ll = lax.fori_loop(0, trip, body, (mm, ll))
        if grow and nxt is not None:
            mm = score(cur[0], mm)
        if nxt is not None:
            mrow[ns] = jnp.max(mm, axis=0, keepdims=True)
        if cur is not None:
            l = jnp.sum(ll, axis=0, keepdims=True)
            ot = acc[hs, :] / l
            acc[hs, :] = ot
            cols = pl.ds(c0, blk)
            ot_ref[hs, cols] = ot
            lse_ref[chd:chd + 1, cols] = m + jnp.log(l)

    def finish(a):
        o = acc[...].T.astype(jnp.bfloat16)
        for j in range(2):
            f = 2 * a + j
            o_ref[f // fl, :, f % fl] = o[j * tok:(j + 1) * tok].reshape(nr, pt, lw)

    slots = sb.shape[0]
    def q_block(a, last):
        par = (a * nh) % slots if nh % slots else 0
        for h in range(nh):
            cs = (par + h) % slots
            cur = (a, h, cs)
            ns = (par + h + 1) % slots
            if h + 1 < nh:
                stage(cur, (a, h + 1, ns), False)
            else:
                stage(cur, None if last else (a + 1, 0, ns), True)
        finish(a)
    stage(None, (0, 0, 0), False)
    def step(a, _):
        q_block(a, False)
        return 0
    lax.fori_loop(0, nblk - 1, step, 0)
    q_block(nblk - 1, True)

def attn_fwd(x):
    nf, nr, fl, pt, width = x.shape
    lw = width // 3
    nh = lw // HD
    seq = nf * nr * fl * pt
    blk = 2 * nr * pt
    return pl.pallas_call(
        fwd_kernel,
        out_shape=(jax.ShapeDtypeStruct((nf, nr, fl, pt, lw), jnp.bfloat16),
                   jax.ShapeDtypeStruct((lw, seq), jnp.float32),
                   jax.ShapeDtypeStruct((nh, seq), jnp.float32)),
        scratch_shapes=[pltpu.VMEM((nh, seq, lw), jnp.bfloat16), pltpu.VMEM((seq, lw), jnp.bfloat16),
                        pltpu.VMEM((lw, seq), jnp.bfloat16), pltpu.VMEM((2, seq, blk), jnp.float32),
                        pltpu.VMEM((lw, blk), jnp.float32), pltpu.VMEM((2, 1, blk), jnp.float32)],
        compiler_params=pltpu.CompilerParams(vmem_limit_bytes=48 << 20),
        cost_estimate=pl.CostEstimate(flops=seq * seq * lw * 2, bytes_accessed=seq * lw * 12, transcendentals=seq * seq * nh // 2),
        name="attn_fwd",
    )(x)

def rotate_back(t, cos, sin, nh):
    out = []
    for h in range(nh):
        a = t[h * HD:h * HD + HD // 2]
        b = t[h * HD + HD // 2:(h + 1) * HD]
        out += [a * cos + b * sin, b * cos - a * sin]
    return jnp.concatenate(out, axis=0)

def bwd_kernel(x_ref, go_ref, ot_ref, lse_ref, cos_ref, sin_ref, g_ref, qm, dom, kf, vf, kt, delta, dqt, dka, dva):
    nf, nr, fl, pt, width = x_ref.shape
    lw = width // 3
    nh = lw // HD
    tok = nr * pt
    frames = nf * fl
    blk = 2 * tok
    def load(f, _):
        part = x_ref[f // fl, :, f % fl].reshape(tok, width)
        go = go_ref[f // fl, :, f % fl].reshape(tok, lw)
        rows = pl.ds(pl.multiple_of(f * tok, tok), tok)
        q = part[:, :lw] * jnp.bfloat16(HD ** -0.5)
        k = part[:, lw:2 * lw]
        prod = go.T.astype(jnp.float32) * ot_ref[:, rows]
        for h in range(nh):
            qm[h, rows, :] = head_mask(q, h, nh)
            dom[h, rows, :] = head_mask(go, h, nh)
            delta[h:h + 1, rows] = jnp.sum(prod[h * HD:(h + 1) * HD], axis=0, keepdims=True)
        kf[rows, :] = k
        kt[:, rows] = k.T
        vf[rows, :] = part[:, 2 * lw:]
        dqt[:, rows] = jnp.zeros((lw, tok), jnp.float32)
        return 0
    lax.fori_loop(0, frames, load, 0)

    def work(k0, kn, q0, qn):
        rows, cols = pl.ds(k0, kn), pl.ds(q0, qn)
        dv, dk = [], []
        for h in range(nh):
            hs = slice(h * HD, (h + 1) * HD)
            qh, dh = qm[h, cols, :], dom[h, cols, :]
            p = jnp.exp(dot(kf[rows, :], qh, NT) - lse_ref[h:h + 1, cols])
            ds = (p * (dot(vf[rows, :], dh, NT) - delta[h:h + 1, cols])).astype(jnp.bfloat16)
            dv.append(dot(p.astype(jnp.bfloat16), dh, NN))
            dk.append(dot(ds, qh, NN))
            dqt[hs, cols] += dot(kt[hs, rows], ds, NN)
        return sum(dk[1:], dk[0]), sum(dv[1:], dv[0])

    def k_block(b, _):
        k0 = pl.multiple_of(b * blk, blk)
        k1 = pl.multiple_of(b * blk + tok, tok)
        dk, dv = work(k0, tok, k0, blk)
        dka[:tok, :] = dk
        dva[:tok, :] = dv
        dk, dv = work(k1, tok, k1, tok)
        dka[tok:, :] = dk
        dva[tok:, :] = dv
        def q_block(a, _):
            dk, dv = work(k0, blk, pl.multiple_of(a * blk, blk), blk)
            dka[...] += dk
            dva[...] += dv
            return 0
        lax.fori_loop(b + 1, frames // 2, q_block, 0)
        cols = pl.ds(k0, blk)
        dk = rotate_back(dka[...].T, cos_ref[:, cols], sin_ref[:, cols], nh).T.astype(jnp.bfloat16)
        dv = dva[...].astype(jnp.bfloat16)
        for j in range(2):
            f = 2 * b + j
            g_ref[f // fl, :, f % fl, :, lw:2 * lw] = dk[j * tok:(j + 1) * tok].reshape(nr, pt, lw)
            g_ref[f // fl, :, f % fl, :, 2 * lw:] = dv[j * tok:(j + 1) * tok].reshape(nr, pt, lw)
        return 0
    lax.fori_loop(0, frames // 2, k_block, 0)
    def store(f, _):
        cols = pl.ds(pl.multiple_of(f * tok, tok), tok)
        dq = rotate_back(dqt[:, cols] * HD ** -0.5, cos_ref[:, cols], sin_ref[:, cols], nh).T.astype(jnp.bfloat16)
        g_ref[f // fl, :, f % fl, :, :lw] = dq.reshape(nr, pt, lw)
        return 0
    lax.fori_loop(0, frames, store, 0)

def attn_bwd(x, go, ot, lse, cos, sin):
    nf, nr, fl, pt, width = x.shape
    lw = width // 3
    nh = lw // HD
    seq = nf * nr * fl * pt
    blk = 2 * nr * pt
    b16, f32 = jnp.bfloat16, jnp.float32
    return pl.pallas_call(
        bwd_kernel,
        out_shape=jax.ShapeDtypeStruct(x.shape, b16),
        scratch_shapes=[pltpu.VMEM((nh, seq, lw), b16), pltpu.VMEM((nh, seq, lw), b16), pltpu.VMEM((seq, lw), b16),
                        pltpu.VMEM((seq, lw), b16), pltpu.VMEM((lw, seq), b16), pltpu.VMEM((nh, seq), f32),
                        pltpu.VMEM((lw, seq), f32), pltpu.VMEM((blk, lw), f32), pltpu.VMEM((blk, lw), f32)],
        compiler_params=pltpu.CompilerParams(vmem_limit_bytes=52 << 20),
        cost_estimate=pl.CostEstimate(flops=seq * seq * lw * 5, bytes_accessed=seq * lw * 24, transcendentals=seq * seq * nh // 2),
        name="attn_bwd",
    )(x, go, ot, lse, cos, sin)

ALL = ("clip", "frame", "row")
B16, F32 = jnp.bfloat16, jnp.float32


def rope_angles(frame_pos, patch_pos, grid):
    pair_index = jnp.arange(32)
    is_time = pair_index < 8
    is_height = (pair_index >= 8) & (pair_index < 20)
    exponent = jnp.where(
        is_time,
        pair_index / 8.0,
        jnp.where(is_height, (pair_index - 8) / 12.0, (pair_index - 20) / 12.0),
    ).astype(F32)
    frequency = jnp.power(F32(10000.0), -exponent)
    position = jnp.where(
        is_time[None, :],
        frame_pos[:, None],
        jnp.where(is_height[None, :], (patch_pos // grid)[:, None], (patch_pos % grid)[:, None]),
    ).astype(F32)
    angle = position * frequency[None, :]
    return (jnp.cos(angle), jnp.sin(angle))


def rotate(values_in, cosine, sine):
    half = values_in.shape[-1] // 2
    cos_b, sin_b = cosine[:, None, :], sine[:, None, :]
    a, b = values_in[..., :half], values_in[..., half:]
    return jnp.concatenate([a * cos_b - b * sin_b, a * sin_b + b * cos_b], axis=-1)


def normalize(values_in):
    centre = values_in - jnp.mean(values_in, axis=-1, keepdims=True)
    inverse = lax.rsqrt(jnp.mean(centre * centre, axis=-1, keepdims=True) + 1e-06)
    return (centre * inverse, inverse)


def norm_back(grad_in, normed, inverse):
    first_mean = jnp.mean(grad_in, axis=-1, keepdims=True)
    second_mean = jnp.mean(grad_in * normed, axis=-1, keepdims=True)
    return inverse * (grad_in - first_mean - normed * second_mean)


def swap(block, axis, bit):
    size = lax.axis_size(axis)
    return lax.ppermute(block, axis, [(i, i ^ bit) for i in range(size)])


def half_step(array, dim, axis, bit):
    mine = (lax.axis_index(axis) // bit) % 2
    send = lax.dynamic_index_in_dim(array, 1 - mine, dim, keepdims=False)
    keep = lax.dynamic_index_in_dim(array, mine, dim, keepdims=False)
    got = swap(send, axis, bit)
    return (keep.astype(F32) + got.astype(F32)).astype(array.dtype)


def bits_of(size):
    out, bit = [], 1
    while bit < size:
        out.append(bit)
        bit *= 2
    return out


def scatter_sum(grad):
    rows, cols = grad.shape
    nc, nf, nr = (lax.axis_size(a) for a in ALL)
    sizes = {"clip": nc, "frame": nf, "row": nr // 2}
    array = half_step(grad.reshape(rows, 2, cols // 2), 1, "row", 1)
    left = rows
    shape = [nc, nf, nr // 2]
    array = array.reshape(shape + [rows // (nc * nf * (nr // 2)), cols // 2])
    for position, axis in ((0, "clip"), (2, "row"), (1, "frame")):
        base = 2 if axis == "row" else 1
        for bit in bits_of(sizes[axis]):
            now = list(array.shape)
            rest = now[position] // 2
            view = array.reshape(now[:position] + [rest, 2] + now[position + 1:])
            array = half_step(view, position + 1, axis, bit * base)
            array = array.reshape(now[:position] + [rest] + now[position + 1:])
    per = array.shape[3]
    array = array.reshape(2, per // 2, cols // 2)
    mine = lax.axis_index("row") % 2
    keep = lax.dynamic_index_in_dim(array, mine, 0, keepdims=False)
    got = swap(lax.dynamic_index_in_dim(array, 1 - mine, 0, keepdims=False), "row", 1)
    return jnp.where(mine == 0, jnp.concatenate([keep, got], axis=1), jnp.concatenate([got, keep], axis=1)).astype(F32)


def on_device(tokens, context, noise_mod, clean_mod, w_qkv, b_qkv, w_out, b_out, w_up, b_up, w_down, b_down, cotangent):
    frames, patches, clips, width = tokens.shape
    count = frames * patches
    heads = width // HD
    nf, nr = lax.axis_size("frame"), lax.axis_size("row")
    group = nf * nr
    nh = max(1, heads // group)
    lw = nh * HD
    hg = heads // nh
    cs = group // hg
    calls = clips // cs
    grid = round((patches * nr) ** 0.5)
    fi, ri = lax.axis_index("frame"), lax.axis_index("row")

    is_clean = (fi * frames + jnp.arange(frames))[None, :] < context[:, None]
    mods = jnp.where(is_clean[:, :, None, None], clean_mod[None, None], noise_mod.transpose(1, 0, 2, 3))
    mods = mods[:, :, :, None]
    shift1, scale1, gate1, shift2, scale2, gate2 = (mods[:, :, i] for i in range(6))
    full = (clips, frames, patches, width)
    inputs = tokens.transpose(2, 0, 1, 3).astype(F32)
    normed1, inv1 = normalize(inputs)
    h1 = (normed1 * (1.0 + scale1) + shift1).astype(B16).reshape(clips, count, width)

    tok = jnp.arange(count)
    cos, sin = rope_angles(fi * frames + tok // patches, ri * patches + tok % patches, grid)
    every = jnp.arange(nf * frames * nr * patches)
    cos_all, sin_all = rope_angles(every // (nr * patches), every % (nr * patches), grid)
    cos_t, sin_t = cos_all.T, sin_all.T

    def exchange(blocks):
        return lax.all_to_all(blocks, ("frame", "row"), 0, 0, tiled=True)

    def to_heads(parts):
        m = parts[0].shape[1]
        return jnp.concatenate(
            [p.reshape(count, m, hg, lw).transpose(2, 0, 1, 3).reshape(hg, count, m * lw) for p in parts], axis=0)

    def from_heads(blocks, m):
        v = blocks.reshape(cs, hg, count, m, lw).transpose(0, 2, 3, 1, 4).reshape(cs, count, m, width)
        return [v[i] for i in range(cs)]

    lead = (nf, nr, frames, patches)
    saved = []
    attn = []
    for i in range(calls):
        parts = []
        for c in range(i * cs, (i + 1) * cs):
            proj = jnp.dot(h1[c], w_qkv, preferred_element_type=F32) + b_qkv
            four = proj.reshape(count, 3 * heads, HD)
            q = rotate(four[:, :heads], cos, sin)
            k = rotate(four[:, heads:2 * heads], cos, sin)
            parts.append(jnp.concatenate([q, k, four[:, 2 * heads:]], axis=1).astype(B16).reshape(count, 3, width))
        x = exchange(to_heads(parts)).reshape(lead + (3 * lw,))
        o, ot, lse = attn_fwd(x)
        saved.append((x, ot, lse))
        attn += from_heads(exchange(o.reshape(group, count, lw)), 1)
    attn = jnp.concatenate(attn, axis=0).reshape(clips * count, width)

    branch = (jnp.dot(attn, w_out, preferred_element_type=F32) + b_out).reshape(full)
    mixed = inputs + gate1 * branch
    normed2, inv2 = normalize(mixed)
    h2 = (normed2 * (1.0 + scale2) + shift2).astype(B16).reshape(clips * count, width)
    pre = jnp.dot(h2, w_up, preferred_element_type=F32) + b_up
    act = jax.nn.gelu(pre, approximate=True).astype(B16)
    down = (jnp.dot(act, w_down, preferred_element_type=F32) + b_down).reshape(full)
    result = mixed + gate2 * down
    g = cotangent.transpose(2, 0, 1, 3).astype(F32)
    gdown = (g * gate2).astype(B16).reshape(clips * count, width)
    tn = (((0,), (0,)), ((), ()))
    dw_down = dot(act, gdown, tn).astype(B16)
    db_down = jnp.sum(gdown, axis=0, dtype=F32)
    gact = dot(gdown, w_down, NT)
    _, pull = jax.vjp(functools.partial(jax.nn.gelu, approximate=True), pre)
    gpre = pull(gact)[0].astype(B16)
    dw_up = dot(h2, gpre, tn).astype(B16)
    db_up = jnp.sum(gpre, axis=0, dtype=F32)
    gh2 = dot(gpre, w_up, NT).reshape(full)
    gmixed = g + norm_back(gh2 * (1.0 + scale2), normed2, inv2)
    gbranch = (gmixed * gate1).astype(B16).reshape(clips * count, width)
    dw_out = dot(attn, gbranch, tn).astype(B16)
    db_out = jnp.sum(gbranch, axis=0, dtype=F32)
    gattn = dot(gbranch, w_out, NT).astype(B16).reshape(clips, count, 1, width)

    gw_down, gw_up, gw_out = scatter_sum(dw_down), scatter_sum(dw_up), scatter_sum(dw_out)

    grads = []
    for i in range(calls):
        go = exchange(to_heads([gattn[c] for c in range(i * cs, (i + 1) * cs)])).reshape(lead + (lw,))
        x, ot, lse = saved[i]
        gx = attn_bwd(x, go, ot, lse, cos_t, sin_t)
        grads += from_heads(exchange(gx.reshape(group, count, 3 * lw)), 3)
    gproj = jnp.concatenate(grads, axis=0).reshape(clips * count, 3 * width)
    dw_qkv = dot(h1.reshape(clips * count, width), gproj, tn).astype(B16)
    db_qkv = jnp.sum(gproj, axis=0, dtype=F32)
    gh1 = dot(gproj, w_qkv, NT).reshape(full)
    gtokens = gmixed + norm_back(gh1 * (1.0 + scale1), normed1, inv1)
    gw_qkv = scatter_sum(dw_qkv)

    terms = [gh1, gh1 * normed1, gmixed * branch.reshape(full), gh2, gh2 * normed2, g * down]
    gmods = jnp.stack([jnp.sum(t, axis=2) for t in terms], axis=2)
    clean = is_clean[:, :, None, None]
    noise_part = jnp.where(clean, 0.0, gmods).transpose(1, 0, 2, 3).astype(B16)
    quarter = width // nr
    sent = noise_part.reshape(frames, clips, 6, nr, quarter).transpose(3, 0, 1, 2, 4)
    grad_noise = jnp.sum(lax.all_to_all(sent, "row", 0, 0, tiled=True).astype(F32), axis=0)
    clean_part = jnp.sum(jnp.where(clean, gmods, 0.0), axis=(0, 1))
    total = lax.axis_size(ALL)
    small = jnp.concatenate([v.reshape(total, -1) for v in (db_qkv, db_out, db_up, db_down)]
                            + [clean_part.reshape(6, total, -1).transpose(1, 0, 2).reshape(total, -1)], axis=1)
    small = jnp.sum(lax.all_to_all(small, ALL, 0, 0, tiled=True), axis=0)
    ends = []
    at = 0
    for size in (3 * width, width, 4 * width, width):
        ends.append(small[at:at + size // total])
        at += size // total
    gb_qkv, gb_out, gb_up, gb_down = ends
    grad_clean = small[at:].reshape(6, -1)
    back = lambda v: v.reshape(full).transpose(1, 2, 0, 3)
    return (back(result).astype(B16), back(gtokens), grad_noise, grad_clean, gw_qkv, gb_qkv, gw_out, gb_out, gw_up, gb_up, gw_down, gb_down)


def solution(mesh):
    token = P("frame", "row", "clip", None)
    rows = P(ALL, None)
    return jax.shard_map(
        on_device,
        mesh=mesh,
        in_specs=(token, P("clip"), P("frame", "clip", None, None)) + (P(),) * 9 + (token,),
        out_specs=(token, token, P("frame", "clip", None, "row"), P(None, ALL), rows, P(ALL), rows, P(ALL), rows, P(ALL), rows, P(ALL)),
        check_vma=False,
    )
```

time: 2940 us -> 952 us (0.32)
  waiting for transfers between devices: 1220 us -> 233 us
  matrix products: 632 us -> 150 us
  local copies, waits for them, and re-layouts: 526 us -> 200 us
  blocking collectives: 267 us -> 0 us
  Pallas kernels: 0 us -> 200 us
  other arithmetic: 218 us -> 79.6 us
  starting transfers between devices: 0.55 us -> 76.4 us
  loops' own time: 39.3 us -> 0 us
    reduce_scatter x5 -> x0, waiting for transfers between devices: 1080 us -> none  [the longest x1 443 us: on_device(): lax.psum_scatter(kv_fn(jnp.int32(0), shard_rows * lax.axis_size(('frame',...]
    dot_general x40 -> x13, matrix products: 632 us -> 150 us  [the longest x8 103 us: dot(): return lax.dot_general(a, b, dims, preferred_element_type=jnp.float32)]
    unnamed x1 -> x0, blocking collectives: 267 us -> none
    pallas_call x0 -> x4, Pallas kernels: none -> 200 us  [the longest x2 131 us: attn_bwd(): pl.pallas_call(bwd_kernel, out_shape=jax.ShapeDtypeStruct(x.shape, b16),...]
    all_gather x2 -> x0, waiting for transfers between devices: 140 us -> none  [the longest x1 95.6 us: on_device(): lax.all_gather(keys_now, ('frame', 'row'), axis=0, tiled=True)]
    ppermute x0 -> x24, waiting for transfers between devices: none -> 123 us  [swap(): return lax.ppermute(block, axis, [(i, i ^ bit) for i in range(size)])]
    all_to_all x0 -> x10, waiting for transfers between devices: none -> 109 us  [the longest x1 70 us: on_device(): small = jnp.sum(lax.all_to_all(small, ALL, 0, 0, tiled=True), axis=0)]
    dynamic_update_slice x16 -> x0, local copies, waits for them, and re-layouts: 89.5 us -> none  [kv_terms(): blocks = lax.map(one_block, jnp.arange(row_count // block_rows))]
  transfers between devices with their start and end apart: 9 -> 34, of which waited for: 7 -> 10; matrix products, arithmetic and copies ran while one was open for 14% -> 28% of each run, Pallas kernels for 0% -> 21%
where the time goes in v1:
time: 952 us; the launch traced here: 941 us
  waiting for transfers between devices  233 us (24%)
  local copies, waits for them, and re-layouts  200 us (21%)
  Pallas kernels  200 us (21%)
  matrix products  150 us (16%)
  other arithmetic  79.6 us (8%)
  starting transfers between devices  76.4 us (8%)
    pallas_call x2, Pallas kernels, attn_bwd(): pl.pallas_call(bwd_kernel, out_shape=jax.ShapeDtypeStruct(x.shape, b16),...  131 us
    ppermute x24, waiting for transfers between devices, swap(): return lax.ppermute(block, axis, [(i, i ^ bit) for i in range(size)])  123 us
    dot_general x8, matrix products, dot(): return lax.dot_general(a, b, dims, preferred_element_type=jnp.float32)  103 us
    all_to_all x1, waiting for transfers between devices, on_device(): small = jnp.sum(lax.all_to_all(small, ALL, 0, 0, tiled=True), axis=0)  70 us
    pallas_call x2, Pallas kernels, attn_fwd(): pl.pallas_call(fwd_kernel, out_shape=(jax.ShapeDtypeStruct((nf, nr, fl, p...  68.9 us
    all_to_all x8, starting transfers between devices, exchange(): return lax.all_to_all(blocks, ('frame', 'row'), 0, 0, tiled=True)  45.7 us
    dynamic_slice x4, local copies, waits for them, and re-layouts, half_step(): keep = lax.dynamic_index_in_dim(array, mine, dim, keepdims=False)  45.1 us
    unnamed x137, local copies, waits for them, and re-layouts  43.7 us
  transfers between devices with their start and end apart: 34, of which 10 were waited for; matrix products, arithmetic and copies ran while one was open for 28% of the time, Pallas kernels for 21%

profile of v1, /device:TPU:1, one launch (start us, length us, event | category | flops | bytes accessed | tf_op | source)
XLA Modules:
  0.0 940.8 jit_solution(1009565819243795250)
XLA Ops:
  24.3 9.2 convolution_add_fusion.1
  59.3 29.3 %all-to-all-done.2 = bf16[8,512,384]{1,2,0:T(8,128)(2,1)} async-done(((bf16[8,512,384]{1,2,0:T(8,128)(2,1)}), bf16[8,512,384]{1,2,0:T(8,128)(2,1)}, u32[]{:S(2)}, u32[]{:S(2)}) %all-to-all-start.2) | async-done | bytes 3145760 | tf_op jit(solution)/shard_map/all_to_all | solution.py:358
  101.4 34.5 %attn_fwd.3 = (bf16[2,4,8,64,128]{4,3,2,1,0:T(8,128)(2,1)S(1)}, f32[128,4096]{1,0:T(8,128)S(1)}, f32[2,4096]{1,0:T(2,128)S(1)}) custom-call(bf16[2,4,8,64,384]{4,3,2,1,0:T(8,128)(2,1)} %bitcast.294), custom_call_target="tpu_custom_call" | custom-call | flops 4294967296 | bytes 6291456 | tf_op jit(solution)/shard_map/attn_fwd/pallas_call | solution.py:133
  147.5 34.5 %attn_fwd.2 = (bf16[2,4,8,64,128]{4,3,2,1,0:T(8,128)(2,1)S(1)}, f32[128,4096]{1,0:T(8,128)S(1)}, f32[2,4096]{1,0:T(2,128)S(1)}) custom-call(bf16[2,4,8,64,384]{4,3,2,1,0:T(8,128)(2,1)} %bitcast.296), custom_call_target="tpu_custom_call" | custom-call | flops 4294967296 | bytes 6291456 | tf_op jit(solution)/shard_map/attn_fwd/pallas_call | solution.py:133
  191.3 9.9 %all-to-all-done.1 = bf16[8,512,128]{1,2,0:T(8,128)(2,1)} async-done(((bf16[8,512,128]{1,2,0:T(8,128)(2,1)}), bf16[8,512,128]{1,2,0:T(8,128)(2,1)}, u32[]{:S(2)}, u32[]{:S(2)}) %all-to-all-start.1) | async-done | bytes 1048608 | tf_op jit(solution)/shard_map/all_to_all | solution.py:358
  216.2 12.1 %fusion.85 = f32[1024,4096]{1,0:T(8,128)} fusion(bf16[1024,1024]{1,0:T(8,128)(2,1)S(1)} %bitcast.300, bf16[1024,4096]{1,0:T(8,128)(2,1)S(1)} %bitcast.321), kind=kOutput, calls=%fused_computation.245 | convolution fusion | flops 8589934592 | bytes 27262976 | tf_op jit(solution)/shard_map/dot_general | solution.py:390
  228.3 16.1 %broadcast_add_fusion = f32[1024,1024]{1,0:T(8,128)} fusion(f32[1024]{0:T(1024)S(1)} %copy-done.51, bf16[4096,1024]{1,0:T(8,128)(2,1)S(1)} %bitcast.319, f32[1024,4096]{1,0:T(8,128)} %fusion.85, f32[4096]{0:T(1024)S(1)} %copy-done.48), kind=kOutput, calls=%fused_computation.86 | convolution fusion | flops 8632926208 | bytes 29380608 | tf_op jit(solution)/shard_map/dot_general | solution.py:392
  244.4 26.4 %convert_reduce_fusion = (f32[4096]{0:T(1024)}, bf16[1024,4096]{1,0:T(8,128)(2,1)}) fusion(f32[1024,4096]{1,0:T(8,128)} %fusion.85, f32[4096]{0:T(1024)S(1)} %copy-done.48, bf16[1024,1024]{1,0:T(8,128)(2,1)} %bitcast.302, bf16[4096,1024]{1,0:T(8,128)(2,1)} %param.23), kind=kOutput, calls=%fused_computation.9 | convolution fusion | flops 8686399488 | bytes 35684352 | tf_op jit(solution)/shard_map/dot_general | solution.py:11
  270.8 15.3 %fusion.14 = (f32[1024]{0:T(1024)S(1)}, f32[1024,1024]{1,0:T(8,128)}) fusion(f32[2,8,1024]{2,1,0:T(8,128)S(1)} %get-tuple-element.126, bf16[1024,4096]{1,0:T(8,128)(2,1)} %get-tuple-element.94, bf16[1024,4096]{1,0:T(8,128)(2,1)} %param.21), kind=kOutput, calls=%fused_computation.33 | convolution fusion | flops 8592030720 | bytes 21041152 | tf_op jit(solution)/shard_map/dot_general | solution.py:11
  322.7 15.8 %convolution_convert_fusion = bf16[4096,1024]{0,1:T(8,128)(2,1)} fusion(bf16[1024,1024]{1,0:T(8,128)(2,1)} %bitcast.303, f32[1024,4096]{1,0:T(8,128)} %fusion.85, f32[4096]{0:T(1024)S(1)} %copy-done.48), kind=kOutput, calls=%fused_computation.16 | convolution fusion | flops 8636071936 | bytes 27279360 | tf_op jit(solution)/shard_map/dot_general | solution.py:11
  349.7 65.6 %attn_bwd.3 = bf16[2,4,8,64,384]{4,3,2,1,0:T(8,128)(2,1)} custom-call(bf16[2,4,8,64,384]{4,3,2,1,0:T(8,128)(2,1)} %bitcast.295, bf16[2,4,8,64,128]{4,3,2,1,0:T(8,128)(2,1)} %bitcast.50.go_ref, f32[128,4096]{1,0:T(8,128)} %copy-done.2, f32[2,4096]{1,0:T(2,128)S(1)} %get-tuple-element.23.lse_ref, f32[32,4096]{1,0:T(8,128)S(1)} %get-tuple-element.143.cos_ref, ...), custom_call_target="tpu_custom_call" | custom-call | flops 10737418240 | bytes 12582912 | tf_op jit(solution)/shard_map/attn_bwd/pallas_call | solution.py:230
  428.4 14.6 %convolution_convert_fusion.1 = bf16[1024,4096]{1,0:T(8,128)(2,1)} fusion(bf16[1024,1024]{1,0:T(8,128)(2,1)S(1)} %bitcast.301, bf16[1024,4096]{1,0:T(8,128)(2,1)} %get-tuple-element.94), kind=kOutput, calls=%fused_computation.17 | convolution fusion | flops 8594128896 | bytes 18874368 | tf_op jit(solution)/shard_map/dot_general | solution.py:11
  445.5 65.6 %attn_bwd.2 = bf16[2,4,8,64,384]{4,3,2,1,0:T(8,128)(2,1)} custom-call(bf16[2,4,8,64,384]{4,3,2,1,0:T(8,128)(2,1)} %bitcast.297, bf16[2,4,8,64,128]{4,3,2,1,0:T(8,128)(2,1)} %bitcast.42.go_ref, f32[128,4096]{1,0:T(8,128)} %copy-done.3, f32[2,4096]{1,0:T(2,128)S(1)} %get-tuple-element.21.lse_ref, f32[32,4096]{1,0:T(8,128)S(1)} %get-tuple-element.143.cos_ref, ...), custom_call_target="tpu_custom_call" | custom-call | flops 10737418240 | bytes 12582912 | tf_op jit(solution)/shard_map/attn_bwd/pallas_call | solution.py:230
  543.5 14.7 %reshape.691 = bf16[1024,2,2048]{2,1,0:T(2,128)(2,1)} reshape(bf16[1024,4096]{1,0:T(8,128)(2,1)} %convolution_convert_fusion.1) | data formatting | bytes 16777216 | tf_op jit(solution)/shard_map/reshape | solution.py:308
  562.6 20.1 %constant_dynamic-slice_fusion.9 = (bf16[1024,1,2048]{2,1,0:T(2,128)(2,1)}, bf16[1024,1,2048]{2,1,0:T(2,128)(2,1)S(1)}) fusion(bf16[1024,2,2048]{2,1,0:T(2,128)(2,1)} %reshape.691, s32[]{:T(128)S(6)} %select_n.418, s32[]{:T(128)S(6)} %select_n.419), kind=kLoop, calls=%fused_computation.183 | loop fusion | bytes 16777224 | tf_op jit(solution)/shard_map/jit(dynamic_index_in_dim)/dynamic_slice | solution.py:291
  600.0 12.0 %convolution_convert_fusion.2 = bf16[1024,3072]{1,0:T(8,128)(2,1)} fusion(bf16[1024,1024]{1,0:T(8,128)(2,1)S(1)} %bitcast.287, bf16[512,3072]{0,1:T(8,128)(2,1)} %bitcast.263, bf16[512,3072]{0,1:T(8,128)(2,1)} %bitcast.268), kind=kOutput, calls=%fused_computation.23 | convolution fusion | flops 6458179584 | bytes 14680064 | tf_op jit(solution)/shard_map/dot_general | solution.py:11
  620.6 14.9 %reshape.687 = bf16[1024,2,1536]{2,1,0:T(2,128)(2,1)} reshape(bf16[1024,3072]{1,0:T(8,128)(2,1)} %convolution_convert_fusion.2) | data formatting | bytes 12582912 | tf_op jit(solution)/shard_map/reshape | solution.py:308
  635.6 15.4 %constant_dynamic-slice_fusion.19 = (bf16[1024,1,1536]{2,1,0:T(2,128)(2,1)}, bf16[1024,1,1536]{2,1,0:T(2,128)(2,1)S(1)}) fusion(bf16[1024,2,1536]{2,1,0:T(2,128)(2,1)} %reshape.687, s32[]{:T(128)S(6)} %select_n.418, s32[]{:T(128)S(6)} %select_n.419), kind=kLoop, calls=%fused_computation.193 | loop fusion | bytes 12582920 | tf_op jit(solution)/shard_map/jit(dynamic_index_in_dim)/dynamic_slice | solution.py:291
  655.6 11.6 %fusion.31 = (f32[2,8,1024]{2,1,0:T(8,128)S(1)}, f32[2,8,64]{2,1,0:T(8,128)S(1)}, f32[2,8,64]{2,1,0:T(8,128)S(1)}, f32[2,8,1024]{2,1,0:T(8,128)S(1)}, f32[2,8,64,1024]{3,2,1,0:T(8,128)}) fusion(f32[2,8,64]{2,1,0:T(8,128)S(1)} %copy-done.42, f32[2,8,64]{2,1,0:T(8,128)S(1)} %copy-done.40, bf16[8,64,2,1024]{3,2,1,0:T(2,128)(2,1)S(1)} %copy-done.8, ...), kind=kOutput, calls=%fused_computation.58 | convolution fusion | flops 6452901888 | bytes 19087360 | tf_op jit(solution)/shard_map/dot_general | solution.py:11
  704.2 70.0 %all-to-all-done.9 = f32[32,1,480]{2,1,0:T(1,128)S(1)} async-done(((f32[32,1,480]{2,1,0:T(1,128)}), f32[32,1,480]{2,1,0:T(1,128)S(1)}, u32[]{:S(2)}, u32[]{:S(2)}) %all-to-all-start.9) | async-done | bytes 61472 | tf_op jit(solution)/shard_map/all_to_all | solution.py:437
  797.4 57.2 %collective-permute-done.20 = bf16[1,2,2,256,512]{4,3,2,1,0:T(8,128)(2,1)} collective-permute-done((bf16[1,2,2,256,512]{4,3,2,1,0:T(8,128)(2,1)S(1)}, bf16[1,2,2,256,512]{4,3,2,1,0:T(8,128)(2,1)}, u32[]{:S(2)}, u32[]{:S(2)}) %collective-permute-start.20) | collective-permute-done | bytes 1048608 | tf_op jit(solution)/shard_map/ppermute | solution.py:285
  857.7 19.5 %collective-permute-done.14 = bf16[1,2,2,64,2048]{4,3,2,1,0:T(8,128)(2,1)} collective-permute-done((bf16[1,2,2,64,2048]{4,3,2,1,0:T(8,128)(2,1)}, bf16[1,2,2,64,2048]{4,3,2,1,0:T(8,128)(2,1)}, u32[]{:S(2)}, u32[]{:S(2)}) %collective-permute-start.14) | collective-permute-done | bytes 1048608 | tf_op jit(solution)/shard_map/ppermute | solution.py:285
  895.2 25.4 %collective-permute-done.2 = bf16[1,2,2,64,1536]{4,3,2,1,0:T(8,128)(2,1)S(1)} collective-permute-done((bf16[1,2,2,64,1536]{4,3,2,1,0:T(8,128)(2,1)S(1)}, bf16[1,2,2,64,1536]{4,3,2,1,0:T(8,128)(2,1)S(1)}, u32[]{:S(2)}, u32[]{:S(2)}) %collective-permute-start.2) | collective-permute-done | bytes 786464 | tf_op jit(solution)/shard_map/ppermute | solution.py:285
  922.0 9.1 collective-permute-done.3
  (330 shorter events, 319.9 us)
Async XLA Ops:
  48.8 39.8 %all-to-all-start.2 = ((bf16[8,512,384]{1,2,0:T(8,128)(2,1)}), bf16[8,512,384]{1,2,0:T(8,128)(2,1)}, u32[]{:S(2)}, u32[]{:S(2)}) async-start(bf16[8,512,384]{1,2,0:T(8,128)(2,1)} %bitcast.281), calls=%async_computation.2 | async-start | bytes 6291456 | tf_op jit(solution)/shard_map/all_to_all | solution.py:358
  88.6 49.9 %all-to-all-start = ((bf16[8,512,384]{1,2,0:T(8,128)(2,1)}), bf16[8,512,384]{1,2,0:T(8,128)(2,1)}, u32[]{:S(2)}, u32[]{:S(2)}) async-start(bf16[8,512,384]{1,2,0:T(8,128)(2,1)} %bitcast.280), calls=%async_computation | async-start | bytes 6291456 | tf_op jit(solution)/shard_map/all_to_all | solution.py:358
  138.5 46.1 %all-to-all-start.3 = ((bf16[8,512,128]{1,2,0:T(8,128)(2,1)}), bf16[8,512,128]{1,2,0:T(8,128)(2,1)}, u32[]{:S(2)}, u32[]{:S(2)}) async-start(bf16[8,512,128]{1,2,0:T(8,128)(2,1)} %copy.146), calls=%async_computation.3 | async-start | bytes 2097152 | tf_op jit(solution)/shard_map/all_to_all | solution.py:358
  311.4 33.5 %all-to-all-start.6 = ((bf16[8,512,128]{2,1,0:T(8,128)(2,1)}), bf16[8,512,128]{2,1,0:T(8,128)(2,1)}, u32[]{:S(2)}, u32[]{:S(2)}) async-start(bf16[8,512,128]{2,1,0:T(8,128)(2,1)} %bitcast.49), calls=%async_computation.6 | async-start | bytes 2097152 | tf_op jit(solution)/shard_map/all_to_all | solution.py:358
  342.9 77.1 %collective-permute-start.7 = (bf16[2,2,2,64,512]{4,3,2,1,0:T(8,128)(2,1)S(1)}, bf16[2,2,2,64,512]{4,3,2,1,0:T(8,128)(2,1)S(1)}, u32[]{:S(2)}, u32[]{:S(2)}) collective-permute-start(bf16[2,2,2,64,512]{4,3,2,1,0:T(8,128)(2,1)S(1)} %dynamic-slice_bitcast_fusion.3), channel_id=1, source_target_pairs={{0,8},{8,0},{16,24},{24,16},{1,9},{9,1},{17,25},{25,17},{2,10},{10... | collective-permute-start | bytes 1572872 | tf_op jit(solution)/shard_map/ppermute | solution.py:285
  344.9 78.5 %all-to-all-start.4 = ((bf16[8,512,128]{2,1,0:T(8,128)(2,1)}), bf16[8,512,128]{2,1,0:T(8,128)(2,1)}, u32[]{:S(2)}, u32[]{:S(2)}) async-start(bf16[8,512,128]{2,1,0:T(8,128)(2,1)} %bitcast.291), calls=%async_computation.4 | async-start | bytes 2097152 | tf_op jit(solution)/shard_map/all_to_all | solution.py:358
  423.3 92.4 %all-to-all-start.7 = ((bf16[8,512,384]{1,2,0:T(8,128)(2,1)}), bf16[8,512,384]{1,2,0:T(8,128)(2,1)}, u32[]{:S(2)}, u32[]{:S(2)}) async-start(bf16[8,512,384]{1,2,0:T(8,128)(2,1)} %copy.153), calls=%async_computation.7 | async-start | bytes 6291456 | tf_op jit(solution)/shard_map/all_to_all | solution.py:358
  444.0 77.0 %collective-permute-start.9 = (bf16[1,2,1,64,512]{4,3,2,1,0:T(8,128)(2,1)S(1)}, bf16[1,2,1,64,512]{4,3,2,1,0:T(8,128)(2,1)S(1)}, u32[]{:S(2)}, u32[]{:S(2)}) collective-permute-start(bf16[1,2,1,64,512]{4,3,2,1,0:T(8,128)(2,1)S(1)} %constant_dynamic-slice_fusion.11), channel_id=1, source_target_pairs={{0,2},{1,3},{2,0},{3,1},{4,6},{5,7},{6,4},{7,5},{8,10},{9,11},{10,... | collective-permute-start | bytes 393224 | tf_op jit(solution)/shard_map/ppermute | solution.py:285
  515.7 76.5 %all-to-all-start.5 = ((bf16[8,512,384]{1,2,0:T(8,128)(2,1)}), bf16[8,512,384]{1,2,0:T(8,128)(2,1)}, u32[]{:S(2)}, u32[]{:S(2)}) async-start(bf16[8,512,384]{1,2,0:T(8,128)(2,1)} %copy.150), calls=%async_computation.5 | async-start | bytes 6291456 | tf_op jit(solution)/shard_map/all_to_all | solution.py:358
  521.1 41.4 %collective-permute-start.10 = (bf16[1,1,1,64,512]{4,3,2,1,0:T(8,128)(2,1)S(1)}, bf16[1,1,1,64,512]{4,3,2,1,0:T(8,128)(2,1)S(1)}, u32[]{:S(2)}, u32[]{:S(2)}) collective-permute-start(bf16[1,1,1,64,512]{4,3,2,1,0:T(8,128)(2,1)S(1)} %constant_dynamic-slice_fusion.10), channel_id=1, source_target_pairs={{0,4},{4,0},{1,5},{5,1},{2,6},{6,2},{3,7},{7,3},{8,12},{12,8},{9,1... | collective-permute-start | bytes 196616 | tf_op jit(solution)/shard_map/ppermute | solution.py:285
  561.8 111.0 %collective-permute-start.18 = (bf16[4096,512]{1,0:T(8,128)(2,1)}, bf16[4096,512]{1,0:T(8,128)(2,1)}, u32[]{:S(2)}, u32[]{:S(2)}) collective-permute-start(bf16[4096,512]{1,0:T(8,128)(2,1)} %bitcast.99), channel_id=1, source_target_pairs={{0,1},{1,0},{2,3},{3,2},{4,5},{5,4},{6,7},{7,6},{8,9},{9,8},{10,11... | collective-permute-start | bytes 12582920 | tf_op jit(solution)/shard_map/ppermute | solution.py:285
  562.5 25.3 %collective-permute-start.11 = (bf16[32,512]{1,0:T(8,128)(2,1)S(1)}, bf16[32,512]{1,0:T(8,128)(2,1)S(1)}, u32[]{:S(2)}, u32[]{:S(2)}) collective-permute-start(bf16[32,512]{1,0:T(8,128)(2,1)S(1)} %get-tuple-element.141), channel_id=1, source_target_pairs={{0,1},{1,0},{2,3},{3,2},{4,5},{5,4},{6,7},{7,6},{8,9},{9,8},{10,11... | collective-permute-start | bytes 98312 | tf_op jit(solution)/shard_map/ppermute | solution.py:285
  587.3 92.6 %collective-permute-start.12 = (bf16[1024,2048]{1,0:T(8,128)(2,1)}, bf16[1024,2048]{1,0:T(8,128)(2,1)}, u32[]{:S(2)}, u32[]{:S(2)}) collective-permute-start(bf16[1024,2048]{1,0:T(8,128)(2,1)} %bitcast.255), channel_id=1, source_target_pairs={{0,1},{1,0},{2,3},{3,2},{4,5},{5,4},{6,7},{7,6},{8,9},{9,8},{10,11... | collective-permute-start | bytes 12582920 | tf_op jit(solution)/shard_map/ppermute | solution.py:285
  653.5 136.2 %collective-permute-start = (bf16[1024,1536]{1,0:T(8,128)(2,1)}, bf16[1024,1536]{1,0:T(8,128)(2,1)}, u32[]{:S(2)}, u32[]{:S(2)}) collective-permute-start(bf16[1024,1536]{1,0:T(8,128)(2,1)} %bitcast.256), channel_id=1, source_target_pairs={{0,1},{1,0},{2,3},{3,2},{4,5},{5,4},{6,7},{7,6},{8,9},{9,8},{10,11... | collective-permute-start | bytes 9437192 | tf_op jit(solution)/shard_map/ppermute | solution.py:285
  679.6 100.9 %collective-permute-start.19 = (bf16[2,2,2,256,512]{4,3,2,1,0:T(8,128)(2,1)S(1)}, bf16[2,2,2,256,512]{4,3,2,1,0:T(8,128)(2,1)}, u32[]{:S(2)}, u32[]{:S(2)}) collective-permute-start(bf16[2,2,2,256,512]{4,3,2,1,0:T(8,128)(2,1)S(1)} %dynamic-slice_bitcast_fusion), channel_id=1, source_target_pairs={{0,8},{8,0},{16,24},{24,16},{1,9},{9,1},{17,25},{25,17},{2,10},{10... | collective-permute-start | bytes 6291464 | tf_op jit(solution)/shard_map/ppermute | solution.py:285
  690.4 94.3 %collective-permute-start.13 = (bf16[2,2,2,64,2048]{4,3,2,1,0:T(8,128)(2,1)}, bf16[2,2,2,64,2048]{4,3,2,1,0:T(8,128)(2,1)}, u32[]{:S(2)}, u32[]{:S(2)}) collective-permute-start(bf16[2,2,2,64,2048]{4,3,2,1,0:T(8,128)(2,1)} %dynamic-slice_bitcast_fusion.1), channel_id=1, source_target_pairs={{0,8},{8,0},{16,24},{24,16},{1,9},{9,1},{17,25},{25,17},{2,10},{10... | collective-permute-start | bytes 6291464 | tf_op jit(solution)/shard_map/ppermute | solution.py:285
  693.0 81.2 %all-to-all-start.9 = ((f32[32,1,480]{2,1,0:T(1,128)}), f32[32,1,480]{2,1,0:T(1,128)S(1)}, u32[]{:S(2)}, u32[]{:S(2)}) async-start(f32[32,1,480]{2,1,0:T(1,128)} %copy.158), calls=%async_computation.9 | async-start | bytes 131072 | tf_op jit(solution)/shard_map/all_to_all | solution.py:437
  783.7 70.9 %collective-permute-start.20 = (bf16[1,2,2,256,512]{4,3,2,1,0:T(8,128)(2,1)S(1)}, bf16[1,2,2,256,512]{4,3,2,1,0:T(8,128)(2,1)}, u32[]{:S(2)}, u32[]{:S(2)}) collective-permute-start(bf16[1,2,2,256,512]{4,3,2,1,0:T(8,128)(2,1)S(1)} %constant_dynamic-slice_fusion.2), channel_id=1, source_target_pairs={{0,16},{8,24},{16,0},{24,8},{1,17},{9,25},{17,1},{25,9},{2,18},{10... | collective-permute-start | bytes 3145736 | tf_op jit(solution)/shard_map/ppermute | solution.py:285
  788.4 88.7 %collective-permute-start.14 = (bf16[1,2,2,64,2048]{4,3,2,1,0:T(8,128)(2,1)}, bf16[1,2,2,64,2048]{4,3,2,1,0:T(8,128)(2,1)}, u32[]{:S(2)}, u32[]{:S(2)}) collective-permute-start(bf16[1,2,2,64,2048]{4,3,2,1,0:T(8,128)(2,1)} %constant_dynamic-slice_fusion.7), channel_id=1, source_target_pairs={{0,16},{8,24},{16,0},{24,8},{1,17},{9,25},{17,1},{25,9},{2,18},{10... | collective-permute-start | bytes 3145736 | tf_op jit(solution)/shard_map/ppermute | solution.py:285
  795.8 85.9 %collective-permute-start.1 = (bf16[2,2,2,64,1536]{4,3,2,1,0:T(8,128)(2,1)}, bf16[2,2,2,64,1536]{4,3,2,1,0:T(8,128)(2,1)}, u32[]{:S(2)}, u32[]{:S(2)}) collective-permute-start(bf16[2,2,2,64,1536]{4,3,2,1,0:T(8,128)(2,1)} %dynamic-slice_bitcast_fusion.2), channel_id=1, source_target_pairs={{0,8},{8,0},{16,24},{24,16},{1,9},{9,1},{17,25},{25,17},{2,10},{10... | collective-permute-start | bytes 4718600 | tf_op jit(solution)/shard_map/ppermute | solution.py:285
  856.2 24.0 %collective-permute-start.21 = (bf16[1,2,1,256,512]{4,3,2,1,0:T(8,128)(2,1)S(1)}, bf16[1,2,1,256,512]{4,3,2,1,0:T(8,128)(2,1)S(1)}, u32[]{:S(2)}, u32[]{:S(2)}) collective-permute-start(bf16[1,2,1,256,512]{4,3,2,1,0:T(8,128)(2,1)S(1)} %constant_dynamic-slice_fusion.1), channel_id=1, source_target_pairs={{0,2},{1,3},{2,0},{3,1},{4,6},{5,7},{6,4},{7,5},{8,10},{9,11},{10,... | collective-permute-start | bytes 1572872 | tf_op jit(solution)/shard_map/ppermute | solution.py:285
  883.6 37.0 %collective-permute-start.2 = (bf16[1,2,2,64,1536]{4,3,2,1,0:T(8,128)(2,1)S(1)}, bf16[1,2,2,64,1536]{4,3,2,1,0:T(8,128)(2,1)S(1)}, u32[]{:S(2)}, u32[]{:S(2)}) collective-permute-start(bf16[1,2,2,64,1536]{4,3,2,1,0:T(8,128)(2,1)S(1)} %constant_dynamic-slice_fusion.17), channel_id=1, source_target_pairs={{0,16},{8,24},{16,0},{24,8},{1,17},{9,25},{17,1},{25,9},{2,18},{10... | collective-permute-start | bytes 2359304 | tf_op jit(solution)/shard_map/ppermute | solution.py:285
  892.0 29.1 %collective-permute-start.16 = (bf16[1,1,1,64,2048]{4,3,2,1,0:T(8,128)(2,1)S(1)}, bf16[1,1,1,64,2048]{4,3,2,1,0:T(8,128)(2,1)S(1)}, u32[]{:S(2)}, u32[]{:S(2)}) collective-permute-start(bf16[1,1,1,64,2048]{4,3,2,1,0:T(8,128)(2,1)S(1)} %constant_dynamic-slice_fusion.5), channel_id=1, source_target_pairs={{0,4},{4,0},{1,5},{5,1},{2,6},{6,2},{3,7},{7,3},{8,12},{12,8},{9,1... | collective-permute-start | bytes 786440 | tf_op jit(solution)/shard_map/ppermute | solution.py:285
  893.5 45.3 %collective-permute-start.23 = (bf16[128,512]{1,0:T(8,128)(2,1)S(1)}, bf16[128,512]{1,0:T(8,128)(2,1)S(1)}, u32[]{:S(2)}, u32[]{:S(2)}) collective-permute-start(bf16[128,512]{1,0:T(8,128)(2,1)S(1)} %get-tuple-element.131), channel_id=1, source_target_pairs={{0,1},{1,0},{2,3},{3,2},{4,5},{5,4},{6,7},{7,6},{8,9},{9,8},{10,11... | collective-permute-start | bytes 393224 | tf_op jit(solution)/shard_map/ppermute | solution.py:285
  (73 other events, 863.5 us)

commit v2 on v1

v2 whole, which is shorter than its diff:
```python
import functools
import jax, jax.numpy as jnp
from jax import lax
from jax.experimental import pallas as pl
from jax.experimental.pallas import tpu as pltpu
from jax.sharding import PartitionSpec as P
HD = 64
NN = (((1,), (0,)), ((), ()))
NT = (((1,), (1,)), ((), ()))
def dot(a, b, dims):
    return lax.dot_general(a, b, dims, preferred_element_type=jnp.float32)

def head_mask(values, head, heads):
    if heads == 1:
        return values
    lane = lax.broadcasted_iota(jnp.int32, values.shape, 1)
    return jnp.where(lane // HD == head, values, jnp.zeros_like(values))


def flash_forward(x_ref, o_ref, ot_ref, lse_ref, qm, kf, vt, sb, acc, mrow, done):
    nf, nr, fl, pt, width = x_ref.shape
    lw = width // 3
    nh = lw // HD
    tok = nr * pt
    frames = nf * fl
    blk = 2 * tok
    nblk = frames // 2
    def load(f, _):
        part = x_ref[f // fl, :, f % fl].reshape(tok, width)
        rows = pl.ds(pl.multiple_of(f * tok, tok), tok)
        q = part[:, :lw] * jnp.bfloat16(HD ** -0.5)
        for h in range(nh):
            qm[h, rows, :] = head_mask(q, h, nh)
        kf[rows, :] = part[:, lw:2 * lw]
        vt[:, rows] = part[:, 2 * lw:].T
        return 0
    lax.fori_loop(0, frames, load, 0)

    def fold(v, op):
        return op(v.reshape(v.shape[0] // 8, 8, v.shape[1]), axis=0)

    def stage(cur, nxt, grow):
        zero8 = jnp.zeros((8, blk), jnp.float32)
        if nxt is not None:
            na, nhd, ns = nxt
            n0 = pl.multiple_of(na * blk, blk)
            n1 = pl.multiple_of(na * blk + tok, tok)
            ncols = pl.ds(n0, blk)
            s0 = dot(kf[pl.ds(n0, tok), :], qm[nhd, ncols, :], NT)
            s1 = dot(kf[pl.ds(n1, tok), :], qm[nhd, pl.ds(n1, tok), :], NT)
            sb[ns, pl.ds(n0, tok), :] = s0
            sb[ns, pl.ds(n1, tok), tok:] = s1
            m0 = fold(s0, jnp.max)
            mm = jnp.concatenate([m0[:, :tok], jnp.maximum(m0[:, tok:], fold(s1, jnp.max))], axis=1)
        else:
            mm = zero8
        if cur is not None:
            ca, chd, cs = cur
            hs = slice(chd * HD, (chd + 1) * HD)
            c0 = pl.multiple_of(ca * blk, blk)
            c1 = pl.multiple_of(ca * blk + tok, tok)
            m = mrow[cs]
            p0 = jnp.exp(sb[cs, pl.ds(c0, tok), :] - m)
            p1 = jnp.exp(sb[cs, pl.ds(c1, tok), tok:] - m[:, tok:])
            l0 = fold(p0, jnp.sum)
            ll = jnp.concatenate([l0[:, :tok], l0[:, tok:] + fold(p1, jnp.sum)], axis=1)
            a0 = dot(vt[hs, pl.ds(c0, tok)], p0.astype(jnp.bfloat16), NN)
            a1 = dot(vt[hs, pl.ds(c1, tok)], p1.astype(jnp.bfloat16), NN)
            acc[hs, :tok] = a0[:, :tok]
            acc[hs, tok:] = a0[:, tok:] + a1
        else:
            ll = zero8
        def score(b, mm):
            rows = pl.ds(pl.multiple_of(b * blk, blk), blk)
            s = dot(kf[rows, :], qm[nhd, ncols, :], NT)
            sb[ns, rows, :] = s
            return jnp.maximum(mm, fold(s, jnp.max))
        def body(b, carry):
            mm, ll = carry
            if nxt is not None:
                mm = score(b, mm)
            if cur is not None:
                rows = pl.ds(pl.multiple_of(b * blk, blk), blk)
                p = jnp.exp(sb[cs, rows, :] - m)
                ll = ll + fold(p, jnp.sum)
                acc[hs, :] += dot(vt[hs, rows], p.astype(jnp.bfloat16), NN)
            return mm, ll
        trip = nxt[0] if cur is None else cur[0]
        mm, ll = lax.fori_loop(0, trip, body, (mm, ll))
        if grow and nxt is not None:
            mm = score(cur[0], mm)
        if nxt is not None:
            mrow[ns] = jnp.max(mm, axis=0, keepdims=True)
        if cur is not None:
            l = jnp.sum(ll, axis=0, keepdims=True)
            ot = acc[hs, :] / l
            acc[hs, :] = ot
            cols = pl.ds(c0, blk)
            ot_ref[hs, cols] = ot
            lse_ref[chd:chd + 1, cols] = m + jnp.log(l)

    def finish(a):
        o = acc[...].T.astype(jnp.bfloat16)
        for j in range(2):
            f = 2 * a + j
            o_ref[f // fl, :, f % fl] = o[j * tok:(j + 1) * tok].reshape(nr, pt, lw)
        done(a)

    slots = sb.shape[0]
    def q_block(a, last):
        par = (a * nh) % slots if nh % slots else 0
        for h in range(nh):
            cs = (par + h) % slots
            cur = (a, h, cs)
            ns = (par + h + 1) % slots
            if h + 1 < nh:
                stage(cur, (a, h + 1, ns), False)
            else:
                stage(cur, None if last else (a + 1, 0, ns), True)
        finish(a)
    stage(None, (0, 0, 0), False)
    def step(a, _):
        q_block(a, False)
        return 0
    lax.fori_loop(0, nblk - 1, step, 0)
    q_block(nblk - 1, True)


def rotate_back(t, cos, sin, nh):
    out = []
    for h in range(nh):
        a = t[h * HD:h * HD + HD // 2]
        b = t[h * HD + HD // 2:(h + 1) * HD]
        out += [a * cos + b * sin, b * cos - a * sin]
    return jnp.concatenate(out, axis=0)

def flash_backward(x_ref, go_ref, ot_ref, lse_ref, cos_ref, sin_ref, g_ref, qm, dom, kf, vf, kt, delta, dqt, dka, dva, done):
    nf, nr, fl, pt, width = x_ref.shape
    lw = width // 3
    nh = lw // HD
    tok = nr * pt
    frames = nf * fl
    blk = 2 * tok
    def load(f, _):
        part = x_ref[f // fl, :, f % fl].reshape(tok, width)
        go = go_ref[f // fl, :, f % fl].reshape(tok, lw)
        rows = pl.ds(pl.multiple_of(f * tok, tok), tok)
        q = part[:, :lw] * jnp.bfloat16(HD ** -0.5)
        k = part[:, lw:2 * lw]
        prod = go.T.astype(jnp.float32) * ot_ref[:, rows]
        for h in range(nh):
            qm[h, rows, :] = head_mask(q, h, nh)
            dom[h, rows, :] = head_mask(go, h, nh)
            delta[h:h + 1, rows] = jnp.sum(prod[h * HD:(h + 1) * HD], axis=0, keepdims=True)
        kf[rows, :] = k
        kt[:, rows] = k.T
        vf[rows, :] = part[:, 2 * lw:]
        dqt[:, rows] = jnp.zeros((lw, tok), jnp.float32)
        return 0
    lax.fori_loop(0, frames, load, 0)

    def work(k0, kn, q0, qn):
        rows, cols = pl.ds(k0, kn), pl.ds(q0, qn)
        dv, dk = [], []
        for h in range(nh):
            hs = slice(h * HD, (h + 1) * HD)
            qh, dh = qm[h, cols, :], dom[h, cols, :]
            p = jnp.exp(dot(kf[rows, :], qh, NT) - lse_ref[h:h + 1, cols])
            ds = (p * (dot(vf[rows, :], dh, NT) - delta[h:h + 1, cols])).astype(jnp.bfloat16)
            dv.append(dot(p.astype(jnp.bfloat16), dh, NN))
            dk.append(dot(ds, qh, NN))
            dqt[hs, cols] += dot(kt[hs, rows], ds, NN)
        return sum(dk[1:], dk[0]), sum(dv[1:], dv[0])

    def k_block(b, _):
        k0 = pl.multiple_of(b * blk, blk)
        k1 = pl.multiple_of(b * blk + tok, tok)
        dk, dv = work(k0, tok, k0, blk)
        dka[:tok, :] = dk
        dva[:tok, :] = dv
        dk, dv = work(k1, tok, k1, tok)
        dka[tok:, :] = dk
        dva[tok:, :] = dv
        def q_block(a, _):
            dk, dv = work(k0, blk, pl.multiple_of(a * blk, blk), blk)
            dka[...] += dk
            dva[...] += dv
            return 0
        lax.fori_loop(b + 1, frames // 2, q_block, 0)
        cols = pl.ds(k0, blk)
        dk = rotate_back(dka[...].T, cos_ref[:, cols], sin_ref[:, cols], nh).T.astype(jnp.bfloat16)
        dv = dva[...].astype(jnp.bfloat16)
        dq = rotate_back(dqt[:, cols] * HD ** -0.5, cos_ref[:, cols], sin_ref[:, cols], nh).T.astype(jnp.bfloat16)
        for j in range(2):
            f = 2 * b + j
            for n, part in enumerate((dq, dk, dv)):
                g_ref[f // fl, :, f % fl, :, n * lw:(n + 1) * lw] = part[j * tok:(j + 1) * tok].reshape(nr, pt, lw)
        done(b)
        return 0
    lax.fori_loop(0, frames // 2, k_block, 0)


ALL = ("clip", "frame", "row")
B16, F32 = jnp.bfloat16, jnp.float32


def rope_angles(frame_pos, patch_pos, grid):
    pair_index = jnp.arange(32)
    is_time = pair_index < 8
    is_height = (pair_index >= 8) & (pair_index < 20)
    exponent = jnp.where(
        is_time,
        pair_index / 8.0,
        jnp.where(is_height, (pair_index - 8) / 12.0, (pair_index - 20) / 12.0),
    ).astype(F32)
    frequency = jnp.power(F32(10000.0), -exponent)
    position = jnp.where(
        is_time[None, :],
        frame_pos[:, None],
        jnp.where(is_height[None, :], (patch_pos // grid)[:, None], (patch_pos % grid)[:, None]),
    ).astype(F32)
    angle = position * frequency[None, :]
    return (jnp.cos(angle), jnp.sin(angle))


def rotate_lanes(t, cos, sin):
    lane = lax.broadcasted_iota(jnp.int32, t.shape, 1)
    half = HD // 2
    lanes = t.shape[1]
    low = (lane % HD) < half
    part = jnp.where(low, pltpu.roll(t, lanes - half, 1), pltpu.roll(t, half, 1))
    return t * cos + part * sin


def stats(v):
    mean = jnp.mean(v, axis=1, keepdims=True)
    centre = v - mean
    inverse = lax.rsqrt(jnp.mean(centre * centre, axis=1, keepdims=True) + 1e-06)
    return centre * inverse, inverse


def qkv_kernel(x_ref, mod_ref, w_hbm, b_ref, cos_ref, sin_ref, o_ref, h_ref, w, sem):
    count, width = x_ref.shape
    hg, _, w3 = o_ref.shape
    lw = w3 // 3
    frames = mod_ref.shape[0]
    pt = count // frames
    copies = [pltpu.make_async_copy(w_hbm.at[:, pl.ds(j * width, width)], w.at[j], sem.at[j]) for j in range(3)]
    for c in copies:
        c.start()
    def one(f, _):
        rows = pl.ds(pl.multiple_of(f * pt, pt), pt)
        n, _inv = stats(x_ref[rows, :].astype(F32))
        h_ref[rows, :] = (n * (1.0 + mod_ref[f, 1:2, :]) + mod_ref[f, 0:1, :]).astype(B16)
        return 0
    lax.fori_loop(0, frames, one, 0)
    step = max(256, lw)
    for j in range(3):
        copies[j].wait()
        for a in range(0, width, step):
            t = dot(h_ref[...], w[j, :, a:a + step], NN) + b_ref[0:1, j * width + a:j * width + a + step]
            for g in range(step // lw):
                v = t[:, g * lw:(g + 1) * lw]
                if j < 2:
                    v = rotate_lanes(v, cos_ref[...], sin_ref[...])
                o_ref[a // lw + g, :, j * lw:(j + 1) * lw] = v.astype(B16)


def qkv_forward(x, mods, w, b, cos, sin, hg, lw):
    count, width = x.shape
    return pl.pallas_call(
        qkv_kernel,
        out_shape=(jax.ShapeDtypeStruct((hg, count, 3 * lw), B16), jax.ShapeDtypeStruct((count, width), B16)),
        in_specs=[pl.BlockSpec(memory_space=pltpu.VMEM)] * 2 + [pl.BlockSpec(memory_space=pl.ANY)]
        + [pl.BlockSpec(memory_space=pltpu.VMEM)] * 3,
        scratch_shapes=[pltpu.VMEM((3, width, width), B16), pltpu.SemaphoreType.DMA((3,))],
        compiler_params=pltpu.CompilerParams(vmem_limit_bytes=48 << 20),
        cost_estimate=pl.CostEstimate(flops=6 * count * width * width, bytes_accessed=10 * count * width + 6 * width * width, transcendentals=0),
        name="qkv",
    )(x, mods, w, b, cos, sin)


def mlp_kernel(a_ref, x_ref, g_ref, mod_ref, wo_ref, bo_ref, wu_ref, bu_ref, wd_ref, bd_ref,
               y_ref, gm_ref, ga_ref, gb_ref, an_ref, h_ref, gd_ref, act_ref, gp_ref, sums_ref, du_ref, db_ref,
               branch, mixed, n2, inv2, down, gh):
    hg, count, lw = a_ref.shape
    width = x_ref.shape[1]
    frames = mod_ref.shape[0]
    pt = count // frames
    step = pl.program_id(0)

    def each(fn):
        def one(f, _):
            fn(f, pl.ds(pl.multiple_of(f * pt, pt), pt))
            return 0
        lax.fori_loop(0, frames, one, 0)

    @pl.when(step == 0)
    def _():
        for g in range(hg):
            an_ref[:, g * lw:(g + 1) * lw] = a_ref[g]
        branch[...] = dot(an_ref[...], wo_ref[...], NN) + bo_ref[...]
        def fn(f, rows):
            m = x_ref[rows, :].astype(F32) + mod_ref[f, 2:3, :] * branch[rows, :]
            n, inv = stats(m)
            mixed[rows, :] = m
            n2[rows, :] = n
            inv2[rows, :] = jnp.broadcast_to(inv, (pt, 128))
            h_ref[rows, :] = (n * (1.0 + mod_ref[f, 4:5, :]) + mod_ref[f, 3:4, :]).astype(B16)
            gd_ref[rows, :] = (g_ref[rows, :].astype(F32) * mod_ref[f, 5:6, :]).astype(B16)
        each(fn)
        down[...] = jnp.zeros_like(down)
        gh[...] = jnp.zeros_like(gh)

    c0 = (2.0 / 3.141592653589793) ** 0.5
    c1 = 0.044715
    h, gd = h_ref[...], gd_ref[...]
    wu, wd = wu_ref[...], wd_ref[...]
    pre = dot(h, wu, NN) + bu_ref[...]
    gact = dot(gd, wd, NT)
    sq = pre * pre
    u = jnp.tanh(pre * (c0 + (c0 * c1) * sq))
    half = 0.5 * (1.0 + u)
    act = (pre * half).astype(B16)
    slope = half + (0.5 * pre) * (1.0 - u * u) * (c0 + (3.0 * c0 * c1) * sq)
    gp = (gact * slope).astype(B16)
    act_ref[...] = act
    gp_ref[...] = gp
    du_ref[...] = jnp.sum(gp.astype(F32), axis=0, keepdims=True)
    down[...] += dot(act, wd, NN)
    gh[...] += dot(gp, wu, NT)

    @pl.when(step == pl.num_programs(0) - 1)
    def _():
        db_ref[...] = jnp.zeros_like(db_ref)
        def fn(f, rows):
            g = g_ref[rows, :].astype(F32)
            d = down[rows, :] + bd_ref[...]
            y_ref[rows, :] = (mixed[rows, :] + mod_ref[f, 5:6, :] * d).astype(B16)
            ghf = gh[rows, :]
            n = n2[rows, :]
            t = ghf * (1.0 + mod_ref[f, 4:5, :])
            back = t - jnp.mean(t, axis=1, keepdims=True) - n * jnp.mean(t * n, axis=1, keepdims=True)
            gm = g + inv2[rows, 0:1] * back
            gm_ref[rows, :] = gm
            gbr = (gm * mod_ref[f, 2:3, :]).astype(B16)
            gb_ref[rows, :] = gbr
            s = lambda v: jnp.sum(v, axis=0, keepdims=True)
            sums_ref[f] = jnp.concatenate([s(gm * branch[rows, :]), s(ghf), s(ghf * n), s(g * d)], axis=0)
            db_ref[...] += jnp.concatenate([s(gbr.astype(F32)), s(gd_ref[rows, :].astype(F32))], axis=0)
        each(fn)
        ga = dot(gb_ref[...], wo_ref[...], NT).astype(B16)
        for i in range(hg):
            ga_ref[i] = ga[:, i * lw:(i + 1) * lw]


def mlp(c, attn, x, g, mods, w_out, b_out, w_up, b_up, w_down, b_down):
    _, hg, count, lw = attn.shape
    width = x.shape[1]
    ff = w_up.shape[1]
    frames = mods.shape[0]
    fc = min(512, ff)
    whole = lambda *shape: pl.BlockSpec(shape, lambda j: (0,) * len(shape), pipeline_mode=pl.Buffered(1))
    keep = lambda *shape: pl.BlockSpec(shape, lambda j: (0,) * len(shape))
    cols = lambda m: pl.BlockSpec((m, fc), lambda j: (0, j))
    s = jax.ShapeDtypeStruct
    return pl.pallas_call(
        mlp_kernel,
        grid=(ff // fc,),
        in_specs=[pl.BlockSpec((None, hg, count, lw), lambda j: (c, 0, 0, 0), pipeline_mode=pl.Buffered(1)), whole(count, width), whole(count, width), whole(frames, 6, width),
                  whole(width, width), whole(1, width), cols(width), cols(1),
                  pl.BlockSpec((fc, width), lambda j: (j, 0)), whole(1, width)],
        out_specs=(keep(count, width), keep(count, width), keep(hg, count, lw), keep(count, width), keep(count, width),
                   keep(count, width), keep(count, width), cols(count), cols(count), keep(frames, 4, width), cols(1), keep(2, width)),
        out_shape=(s((count, width), B16), s((count, width), F32), s((hg, count, lw), B16), s((count, width), B16),
                   s((count, width), B16), s((count, width), B16), s((count, width), B16), s((count, ff), B16),
                   s((count, ff), B16), s((frames, 4, width), F32), s((1, ff), F32), s((2, width), F32)),
        scratch_shapes=[pltpu.VMEM((count, width), F32)] * 3 + [pltpu.VMEM((count, 128), F32)]
        + [pltpu.VMEM((count, width), F32)] * 2,
        compiler_params=pltpu.CompilerParams(vmem_limit_bytes=60 << 20, dimension_semantics=("arbitrary",)),
        cost_estimate=pl.CostEstimate(flops=2 * count * width * (2 * width + 4 * ff), bytes_accessed=4 * width * ff + 40 * count * width, transcendentals=count * ff),
        name="mlp",
    )(attn, x, g, mods, w_out, b_out, w_up, b_up, w_down, b_down)


def qkv_back_kernel(gp_ref, x_ref, gm_ref, mod_ref, w_ref, o_ref, sums_ref, db_ref, full, gh):
    hg, count, w3 = gp_ref.shape
    lw = w3 // 3
    width = x_ref.shape[1]
    frames = mod_ref.shape[0]
    pt = count // frames
    for j in range(3):
        for g in range(hg):
            full[:, j * width + g * lw:j * width + (g + 1) * lw] = gp_ref[g, :, j * lw:(j + 1) * lw]
    gh[...] = dot(full[...], w_ref[...], NT)
    db_ref[...] = jnp.sum(full[...].astype(F32), axis=0, keepdims=True)
    def one(f, _):
        rows = pl.ds(pl.multiple_of(f * pt, pt), pt)
        n, inv = stats(x_ref[rows, :].astype(F32))
        ghf = gh[rows, :]
        t = ghf * (1.0 + mod_ref[f, 1:2, :])
        back = t - jnp.mean(t, axis=1, keepdims=True) - n * jnp.mean(t * n, axis=1, keepdims=True)
        o_ref[rows, :] = gm_ref[rows, :] + inv * back
        s = lambda v: jnp.sum(v, axis=0, keepdims=True)
        sums_ref[f] = jnp.concatenate([s(ghf), s(ghf * n)], axis=0)
        return 0
    lax.fori_loop(0, frames, one, 0)


def qkv_back(c, gproj, x, gmixed, mods, w):
    _, hg, count, w3 = gproj.shape
    width = x.shape[1]
    frames = mods.shape[0]
    s = jax.ShapeDtypeStruct
    whole = lambda *shape: pl.BlockSpec(shape, lambda i: (0,) * len(shape))
    return pl.pallas_call(
        qkv_back_kernel,
        grid=(1,),
        in_specs=[pl.BlockSpec((None, hg, count, w3), lambda i: (c, 0, 0, 0)), whole(count, width), whole(count, width),
                  whole(frames, 6, width), whole(width, 3 * width)],
        out_specs=(whole(count, width), whole(frames, 2, width), whole(1, 3 * width)),
        out_shape=(s((count, width), F32), s((frames, 2, width), F32), s((1, 3 * width), F32)),
        scratch_shapes=[pltpu.VMEM((count, 3 * width), B16), pltpu.VMEM((count, width), F32)],
        compiler_params=pltpu.CompilerParams(vmem_limit_bytes=48 << 20),
        cost_estimate=pl.CostEstimate(flops=6 * count * width * width, bytes_accessed=16 * count * width + 6 * width * width, transcendentals=0),
        name="qkv_back",
    )(gproj, x, gmixed, mods, w)


TN = (((0,), (0,)), ((), ()))


def outer_kernel(half_ref, *refs, clips, packed, received):
    a_refs, b_refs = refs[:clips], refs[clips:2 * clips]
    o_ref = refs[-1]
    total = None
    for a_ref, b_ref in zip(a_refs, b_refs):
        b = jnp.concatenate([b_ref[i] for i in range(packed)], axis=1) if packed else b_ref[...]
        part = dot(a_ref[...], b, TN)
        total = part if total is None else total + part
    if received:
        total = total + refs[2 * clips][...].astype(F32)
    o_ref[...] = total.astype(B16)


def outer(a_list, b_list, half, got=None):
    clips = len(a_list)
    count, rows = a_list[0].shape
    grouped = not isinstance(b_list, (list, tuple))
    if grouped:
        _, groups, _, w3 = b_list.shape
        packed = max(1, 128 * 3 // w3)
        ch = groups // 2 * w3
        cb, rb = packed * w3, rows
        b_specs = [pl.BlockSpec((None, packed, count, w3), lambda i, j, h, c=c: (c, h[0] * (groups // 2 // packed) + j, 0, 0)) for c in range(clips)]
        b_list = [b_list] * clips
    else:
        packed = 0
        ch = b_list[0].shape[1] // 2
        rb = min(rows, 1024)
        cb = min(ch, 512)
        b_specs = [pl.BlockSpec((count, cb), lambda i, j, h: (0, h[0] * (ch // cb) + j))] * clips
    out = pl.BlockSpec((rb, cb), lambda i, j, h: (i, j))
    return pl.pallas_call(
        functools.partial(outer_kernel, clips=clips, packed=packed, received=got is not None),
        grid_spec=pltpu.PrefetchScalarGridSpec(
            num_scalar_prefetch=1, grid=(rows // rb, ch // cb),
            in_specs=[pl.BlockSpec((count, rb), lambda i, j, h: (0, i))] * clips + b_specs + ([out] if got is not None else []),
            out_specs=out),
        out_shape=jax.ShapeDtypeStruct((rows, ch), B16),
        compiler_params=pltpu.CompilerParams(vmem_limit_bytes=40 << 20, dimension_semantics=("arbitrary", "arbitrary")),
        cost_estimate=pl.CostEstimate(flops=2 * clips * count * rows * ch, bytes_accessed=2 * clips * count * (rows + ch) + 2 * rows * ch, transcendentals=0),
        name="outer",
    )(half, *a_list, *b_list, *([got] if got is not None else []))


MESH = pl.DeviceIdType.MESH


class Plane:
    def __init__(self):
        self.nf, self.nr = lax.axis_size("frame"), lax.axis_size("row")
        self.f, self.r = lax.axis_index("frame"), lax.axis_index("row")
        self.size = self.nf * self.nr
        self.me = self.f * self.nr + self.r

    def peer(self, k):
        p = lax.rem(self.me + k, self.size)
        return p, p // self.nr, lax.rem(p, self.nr)


def greet(plane, with_clips):
    barrier = pltpu.get_barrier_semaphore()
    count = plane.size - 1
    for k in range(1, plane.size):
        _, f, r = plane.peer(k)
        pl.semaphore_signal(barrier, inc=1, device_id={"frame": f, "row": r}, device_id_type=MESH)
    if with_clips:
        nc = lax.axis_size("clip")
        c = lax.axis_index("clip")
        for k in range(1, nc):
            pl.semaphore_signal(barrier, inc=1, device_id={"clip": lax.rem(c + k, nc)}, device_id_type=MESH)
        count += nc - 1
    pl.semaphore_wait(barrier, count)


def remote(src, dst, send, recv, device):
    return pltpu.make_async_remote_copy(src_ref=src, dst_ref=dst, send_sem=send, recv_sem=recv, device_id=device, device_id_type=MESH)


def send_blocks(plane, i, a, buf, out, send, recv, local):
    fl = buf.shape[3]
    fh, at = 2 * a // fl, lax.rem(2 * a, fl)
    for r in range(plane.nr):
        src = buf.at[i, fh, r, pl.ds(at, 2)]
        dst = out.at[i, plane.me, pl.ds(at, 2)]
        own = jnp.logical_and(fh == plane.f, r == plane.r)
        dest = fh * plane.nr + r
        k = lax.rem(dest - plane.me + plane.size, plane.size)
        @pl.when(own)
        def _():
            pltpu.make_async_copy(src, dst, local.at[i]).start()
        @pl.when(jnp.logical_not(own))
        def _():
            remote(src, dst, send.at[i, k], recv.at[i, k], {"frame": fh, "row": r}).start()


def wait_blocks(plane, calls, buf, out, send, recv, local):
    for i in range(calls):
        pltpu.make_async_copy(buf.at[i, plane.f, plane.r], out.at[i, plane.me], local.at[i]).wait()
        for k in range(1, plane.size):
            p, f, r = plane.peer(k)
            copy = remote(buf.at[i, f, r], out.at[i, plane.me], send.at[i, k], recv.at[i, k], {"frame": f, "row": r})
            copy.wait_send()
            copy.wait_recv()


def fwd_all_kernel(*refs, calls):
    plane = Plane()
    x_send = refs[:calls]
    x_out, a_out, ot_ref, lse_ref = refs[calls:calls + 4]
    xv, ob, qm, kf, vt, sb, acc, mrow, xs, xr, xl, os, orr, ol, save = refs[calls + 4:]
    greet(plane, False)
    for i in range(calls):
        pltpu.make_async_copy(x_send[i].at[plane.me], xv.at[i, plane.f, plane.r], xl.at[i]).start()
        for k in range(1, plane.size):
            p, f, r = plane.peer(k)
            remote(x_send[i].at[p], xv.at[i, plane.f, plane.r], xs.at[i, k], xr.at[i, k], {"frame": f, "row": r}).start()

    def arrive(i, what):
        for k in range(1, plane.size):
            p, f, r = plane.peer(k)
            copy = remote(x_send[0].at[p], xv.at[i, plane.f, plane.r], xs.at[i, k], xr.at[i, k], {"frame": f, "row": r})
            copy.wait_recv() if what else copy.wait_send()

    def call(i, _):
        pltpu.make_async_copy(x_send[0].at[plane.me], xv.at[i, plane.f, plane.r], xl.at[i]).wait()
        arrive(i, True)
        pltpu.make_async_copy(xv.at[i], x_out.at[i], save.at[i]).start()
        flash_forward(xv.at[i], ob.at[i], ot_ref.at[i], lse_ref.at[i], qm, kf, vt, sb, acc, mrow,
                      lambda a: send_blocks(plane, i, a, ob, a_out, os, orr, ol))
        return 0
    lax.fori_loop(0, calls, call, 0)
    for i in range(calls):
        arrive(i, False)
        pltpu.make_async_copy(xv.at[i], x_out.at[i], save.at[i]).wait()
    wait_blocks(plane, calls, ob, a_out, os, orr, ol)


def attention_forward(sends, lead, lw):
    calls = len(sends)
    nf, nr, fl, pt = lead
    group = nf * nr
    nh = lw // HD
    seq = nf * nr * fl * pt
    blk = 2 * nr * pt
    hbm, vmem = pl.BlockSpec(memory_space=pl.ANY), pl.BlockSpec(memory_space=pltpu.VMEM)
    s, v, dma = jax.ShapeDtypeStruct, pltpu.VMEM, pltpu.SemaphoreType.DMA
    return pl.pallas_call(
        functools.partial(fwd_all_kernel, calls=calls),
        in_specs=[hbm] * calls,
        out_specs=(hbm, hbm, vmem, vmem),
        out_shape=(s((calls,) + lead + (3 * lw,), B16), s((calls, group, fl, pt, lw), B16),
                   s((calls, lw, seq), F32), s((calls, nh, seq), F32)),
        scratch_shapes=[v((calls,) + lead + (3 * lw,), B16), v((calls,) + lead + (lw,), B16), v((nh, seq, lw), B16),
                        v((seq, lw), B16), v((lw, seq), B16), v((2, seq, blk), F32), v((lw, blk), F32), v((2, 1, blk), F32),
                        dma((calls, group)), dma((calls, group)), dma((calls,)), dma((calls, group)), dma((calls, group)),
                        dma((calls,)), dma((calls,))],
        compiler_params=pltpu.CompilerParams(vmem_limit_bytes=56 << 20, collective_id=0, has_side_effects=True),
        cost_estimate=pl.CostEstimate(flops=calls * seq * seq * lw * 2, bytes_accessed=calls * seq * lw * 24, transcendentals=calls * seq * seq * nh // 2),
        name="attention_forward",
    )(*sends)


class Sum:
    def __init__(self, plane, plane_first, part, out, cols, out_cols, v1, s1, v2, s2, v3, sems):
        self.plane, self.plane_first, self.part, self.out = plane, plane_first, part, out
        self.cols, self.out_cols = cols, out_cols
        self.v1, self.s1, self.v2, self.s2, self.v3, self.sems = v1, s1, v2, s2, v3, sems
        self.bit = lax.rem(plane.r, 2)

    def place(self, stage):
        plane = self.plane
        if (stage == 1) == self.plane_first:
            half = plane.nr // 2
            return plane.nf * half, plane.f * half + plane.r // 2, lambda p: {"frame": p // half, "row": lax.rem(p, half) * 2 + self.bit}
        return lax.axis_size("clip"), lax.axis_index("clip"), lambda p: {"clip": p}

    def block(self, stage, p):
        if stage == 2:
            return self.s1.at[p]
        cols = pl.ds(*self.cols)
        return self.part.at[:, p, :, cols] if self.plane_first else self.part.at[p, :, :, cols]

    def copies(self, stage):
        count, me, device = self.place(stage)
        dst = self.v1 if stage == 1 else self.v2
        base = 0 if stage == 1 else self.v1.shape[0]
        out = []
        for k in range(1, count):
            p = lax.rem(me + k, count)
            out.append(remote(self.block(stage, p), dst.at[me], self.sems.at[0, base + k], self.sems.at[1, base + k], device(p)))
        return out, pltpu.make_async_copy(self.block(stage, me), dst.at[me], self.sems.at[0, base])

    def start(self, stage):
        copies, own = self.copies(stage)
        for c in copies:
            c.start()
        own.start()

    def wait(self, stage):
        copies, own = self.copies(stage)
        for c in copies:
            c.wait()
        own.wait()

    def middle(self):
        def one(j, _):
            total = self.v1[0, j].astype(F32)
            for c in range(1, self.v1.shape[0]):
                total = total + self.v1[c, j].astype(F32)
            self.s1[j] = total.astype(B16)
            return 0
        lax.fori_loop(0, self.s1.shape[0], one, 0)
        self.start(2)

    def third(self):
        return remote(self.s2.at[1 - self.bit], self.v3, self.sems.at[0, self.sems.shape[1] - 1], self.sems.at[1, self.sems.shape[1] - 1],
                      {"row": self.plane.r + 1 - 2 * self.bit})

    def columns(self, b):
        first, size = self.cols
        return pl.ds(b * self.out_cols + first, size)

    def last(self):
        total = self.v2[0].astype(F32)
        for c in range(1, self.v2.shape[0]):
            total = total + self.v2[c].astype(F32)
        per = self.s2.shape[1]
        self.s2[0] = total[:per]
        self.s2[1] = total[per:]
        self.third().start()
        for b in range(2):
            @pl.when(self.bit == b)
            def _():
                self.out[:, self.columns(b)] = self.s2[b]

    def close(self):
        self.third().wait()
        for b in range(2):
            @pl.when(self.bit == b)
            def _():
                self.out[:, self.columns(1 - b)] = self.v3[...]


def sum_plan(parts, orders):
    scratch, outs, jobs = [], [], []
    for n, (part, order) in enumerate(zip(parts, orders)):
        nc, np_, two, ch = part.shape
        outs.append(jax.ShapeDtypeStruct((two // 2, 2 * ch), F32))
        for plane_first, first, cols in order:
            n1, n2 = (np_, nc) if plane_first else (nc, np_)
            scratch += [pltpu.VMEM((n1, n2, two, cols), B16), pltpu.VMEM((n2, two, cols), B16), pltpu.VMEM((n2, two, cols), B16),
                        pltpu.VMEM((2, two // 2, cols), F32), pltpu.VMEM((two // 2, cols), F32),
                        pltpu.SemaphoreType.DMA((2, n1 + n2 + 1))]
            jobs.append((n, plane_first, first, cols))
    return scratch, outs, jobs


def make_sums(plane, jobs, parts, outs, scratch):
    return [Sum(plane, plane_first, parts[n], outs[n], (first, cols), parts[n].shape[3], *scratch[6 * i:6 * i + 6])
            for i, (n, plane_first, first, cols) in enumerate(jobs)]


def sums_kernel(*refs, count, jobs):
    plane = Plane()
    sums = make_sums(plane, jobs, refs[:count], refs[count:2 * count], refs[2 * count:])
    greet(plane, True)
    for s in sums:
        s.start(1)
    for s in sums:
        s.wait(1)
        s.middle()
    for s in sums:
        s.wait(2)
        s.last()
    for s in sums:
        s.close()


def scatter_sums(parts, orders, collective_id):
    scratch, outs, jobs = sum_plan(parts, orders)
    return pl.pallas_call(
        functools.partial(sums_kernel, count=len(parts), jobs=jobs),
        in_specs=[pl.BlockSpec(memory_space=pl.ANY)] * len(parts),
        out_specs=[pl.BlockSpec(memory_space=pltpu.VMEM)] * len(parts),
        out_shape=outs,
        scratch_shapes=scratch,
        compiler_params=pltpu.CompilerParams(vmem_limit_bytes=48 << 20, collective_id=collective_id, has_side_effects=True),
        cost_estimate=pl.CostEstimate(flops=0, bytes_accessed=sum(2 * p.size for p in parts) * 40, transcendentals=0),
        name="scatter_sums",
    )(*parts)


def bwd_all_kernel(*refs, calls, count, jobs):
    plane = Plane()
    x_in, go_in, ot_in, lse_ref, cos_ref, sin_ref = refs[:6]
    go_send = refs[6:5 + calls]
    at = 5 + calls
    parts = refs[at:at + count]
    at += count
    gx_out = refs[at]
    outs = refs[at + 1:at + 1 + count]
    at += 1 + count
    xv, gov, otv, gb, qm, dom, kf, vf, kt, delta, dqt, dka, dva, loads, gs, gr, gl, xs, xr, xl = refs[at:at + 20]
    sums = make_sums(plane, jobs, parts, outs, refs[at + 20:])
    greet(plane, True)
    load = [pltpu.make_async_copy(go_in, gov.at[0], gl.at[0])]
    for i in range(calls):
        load += [pltpu.make_async_copy(x_in.at[i], xv.at[i], loads.at[0, i]), pltpu.make_async_copy(ot_in.at[i], otv.at[i], loads.at[1, i])]
    for c in load:
        c.start()
    def go_copy(i, k, src):
        p, f, r = plane.peer(k)
        return remote(src.at[p], gov.at[i, plane.f, plane.r], gs.at[i, k], gr.at[i, k], {"frame": f, "row": r})
    for i in range(1, calls):
        pltpu.make_async_copy(go_send[i - 1].at[plane.me], gov.at[i, plane.f, plane.r], gl.at[i]).start()
        for k in range(1, plane.size):
            go_copy(i, k, go_send[i - 1]).start()
    for s in sums:
        s.start(1)

    def call(i, _):
        pltpu.make_async_copy(x_in.at[i], xv.at[i], loads.at[0, i]).wait()
        pltpu.make_async_copy(ot_in.at[i], otv.at[i], loads.at[1, i]).wait()
        if calls > 1:
            @pl.when(i > 0)
            def _():
                pltpu.make_async_copy(go_send[0].at[plane.me], gov.at[i, plane.f, plane.r], gl.at[i]).wait()
                for k in range(1, plane.size):
                    go_copy(i, k, go_send[0]).wait_recv()
        @pl.when(i == 0)
        def _():
            pltpu.make_async_copy(go_in, gov.at[0], gl.at[0]).wait()
        def block_done(b):
            send_blocks(plane, i, b, gb, gx_out, xs, xr, xl)
            @pl.when(jnp.logical_and(i == calls - 1, b == 3))
            def _():
                for s in sums:
                    s.wait(1)
                    s.middle()
        flash_backward(xv.at[i], gov.at[i], otv.at[i], lse_ref.at[i], cos_ref, sin_ref, gb.at[i],
                       qm, dom, kf, vf, kt, delta, dqt, dka, dva, block_done)
        return 0
    lax.fori_loop(0, calls, call, 0)
    for i in range(1, calls):
        for k in range(1, plane.size):
            go_copy(i, k, go_send[i - 1]).wait_send()
    for s in sums:
        s.wait(2)
        s.last()
    for s in sums:
        s.close()
    wait_blocks(plane, calls, gb, gx_out, xs, xr, xl)


def attention_backward(x, go, go_sends, ot, lse, cos, sin, parts, orders):
    calls, nf, nr, fl, pt, w3 = x.shape
    lead = (nf, nr, fl, pt)
    lw = w3 // 3
    group = nf * nr
    nh = lw // HD
    seq = nf * nr * fl * pt
    blk = 2 * nr * pt
    hbm, vmem = pl.BlockSpec(memory_space=pl.ANY), pl.BlockSpec(memory_space=pltpu.VMEM)
    s, v, dma = jax.ShapeDtypeStruct, pltpu.VMEM, pltpu.SemaphoreType.DMA
    scratch, outs, jobs = sum_plan(parts, orders)
    return pl.pallas_call(
        functools.partial(bwd_all_kernel, calls=calls, count=len(parts), jobs=jobs),
        in_specs=[hbm, hbm, hbm, vmem, vmem, vmem] + [hbm] * (len(go_sends) + len(parts)),
        out_specs=[hbm] + [vmem] * len(parts),
        out_shape=[s((calls, group, fl, pt, w3), B16)] + outs,
        scratch_shapes=[v((calls,) + lead + (w3,), B16), v((calls,) + lead + (lw,), B16), v((calls, lw, seq), F32), v((calls,) + lead + (w3,), B16),
                        v((nh, seq, lw), B16), v((nh, seq, lw), B16), v((seq, lw), B16), v((seq, lw), B16), v((lw, seq), B16),
                        v((nh, seq), F32), v((lw, seq), F32), v((blk, lw), F32), v((blk, lw), F32),
                        dma((2, calls)), dma((calls, group)), dma((calls, group)), dma((calls,)), dma((calls, group)), dma((calls, group)), dma((calls,))] + scratch,
        compiler_params=pltpu.CompilerParams(vmem_limit_bytes=61 << 20, collective_id=1, has_side_effects=True),
        cost_estimate=pl.CostEstimate(flops=calls * seq * seq * lw * 5, bytes_accessed=calls * seq * lw * 48, transcendentals=calls * seq * seq * nh // 2),
        name="attention_backward",
    )(x, go, ot, lse, cos, sin, *go_sends, *parts)


def swap(block, axis, bit):
    size = lax.axis_size(axis)
    return lax.ppermute(block, axis, [(i, i ^ bit) for i in range(size)])


def exchange(blocks, axes=("frame", "row")):
    return lax.all_to_all(blocks, axes, 0, 0, tiled=True)


def after(value, *others):
    return lax.optimization_barrier((value,) + others)[0]


def on_device(tokens, context, noise_mod, clean_mod, w_qkv, b_qkv, w_out, b_out, w_up, b_up, w_down, b_down, cotangent):
    frames, patches, clips, width = tokens.shape
    count = frames * patches
    heads = width // HD
    nf, nr = lax.axis_size("frame"), lax.axis_size("row")
    group = nf * nr
    nh = max(1, heads // group)
    lw = nh * HD
    hg = heads // nh
    cs = group // hg
    calls = clips // cs
    grid = round((patches * nr) ** 0.5)
    fi, ri = lax.axis_index("frame"), lax.axis_index("row")

    is_clean = (fi * frames + jnp.arange(frames))[None, :] < context[:, None]
    mods = jnp.where(is_clean[:, :, None, None], clean_mod[None, None], noise_mod.transpose(1, 0, 2, 3))
    full = (clips, frames, patches, width)
    inputs = tokens.transpose(2, 0, 1, 3).reshape(clips, count, width)
    cots = cotangent.transpose(2, 0, 1, 3).reshape(clips, count, width)

    tok = jnp.arange(count)
    cos, sin = rope_angles(fi * frames + tok // patches, ri * patches + tok % patches, grid)
    cos_l = jnp.tile(jnp.concatenate([cos, cos], axis=1), (1, nh))
    sin_l = jnp.tile(jnp.concatenate([-sin, sin], axis=1), (1, nh))
    every = jnp.arange(nf * frames * nr * patches)
    cos_all, sin_all = rope_angles(every // (nr * patches), every % (nr * patches), grid)
    cos_t, sin_t = cos_all.T, sin_all.T
    row_of = lambda v: v.reshape(1, -1)

    lead = (nf, nr, frames, patches)
    h1, sends = [], []
    for c in range(clips):
        o, h = qkv_forward(inputs[c], mods[c], w_qkv, row_of(b_qkv), cos_l, sin_l, hg, lw)
        sends.append(o)
        h1.append(h)
    by_call = lambda v, w: [jnp.concatenate(v[i * cs:(i + 1) * cs], axis=0).reshape(group, frames, patches, w) for i in range(calls)]
    x, attn, ot, lse = attention_forward(by_call(sends, 3 * lw), lead, lw)
    attn = attn.reshape(clips, hg, count, lw)

    outs = [mlp(c, attn, inputs[c], cots[c], mods[c], w_out, row_of(b_out), w_up, row_of(b_up), w_down, row_of(b_down))
            for c in range(clips)]
    y, gmixed, gattn, gbranch, attn_n, h2, gdown, act, gpre, sums2, db_up, db_two = zip(*outs)
    gattn = by_call(gattn, lw)
    go = exchange(gattn[0]).reshape(lead + (lw,))

    mine = jnp.reshape(ri % 2, (1,)).astype(jnp.int32)
    nc = lax.axis_size("clip")
    def summed(*pairs):
        got = [swap(outer(a, b, 1 - mine), "row", 1) for a, b in pairs]
        parts = [outer(a, b, mine, g) for (a, b), g in zip(pairs, got)]
        return [p.reshape(nc, nf * nr // 2, p.shape[0] // (nc * nf * nr // 2), p.shape[1]) for p in parts]
    parts = summed((act, gdown), (h2, gpre), (attn_n, gbranch))
    orders = [[(True, 0, parts[0].shape[3])], [(False, 0, parts[1].shape[3])], [(True, 0, parts[2].shape[3])]]
    gproj, gw_down, gw_up, gw_out = attention_backward(x, go, gattn[1:], ot, lse, cos_t, sin_t, parts, orders)
    gproj = gproj.reshape(clips, hg, count, 3 * lw)
    backs = [qkv_back(c, gproj, inputs[c], gmixed[c], mods[c], w_qkv) for c in range(clips)]
    gtokens, sums1, db_qkv = zip(*backs)
    parts = summed((h1, gproj))
    ch = parts[0].shape[3]
    gw_qkv, = scatter_sums(parts, [[(True, 0, 3 * ch // 4), (False, 3 * ch // 4, ch // 4)]], 2)
    per = gw_qkv.shape[0]
    gw_qkv = gw_qkv.reshape(per, 2, hg // 2, 3, lw).transpose(0, 3, 1, 2, 4).reshape(per, 3 * width)

    gmods = jnp.stack([jnp.concatenate([sums1[c], sums2[c]], axis=1) for c in range(clips)], axis=0)
    clean = is_clean[:, :, None, None]
    noise_part = jnp.where(clean, 0.0, gmods).transpose(1, 0, 2, 3).astype(B16)
    quarter = width // nr
    sent = noise_part.reshape(frames, clips, 6, nr, quarter).transpose(3, 0, 1, 2, 4)
    grad_noise = jnp.sum(exchange(sent, "row").astype(F32), axis=0)
    clean_part = jnp.sum(jnp.where(clean, gmods, 0.0), axis=(0, 1))
    total = lax.axis_size(ALL)
    two = sum(db_two[1:], db_two[0])
    small = jnp.concatenate(
        [v.reshape(total, -1) for v in (sum(db_qkv[1:], db_qkv[0]), two[0], sum(db_up[1:], db_up[0]), two[1])]
        + [clean_part.reshape(6, total, -1).transpose(1, 0, 2).reshape(total, -1)], axis=1)
    small = jnp.sum(exchange(small, ALL), axis=0)
    ends = []
    at = 0
    for size in (3 * width, width, w_up.shape[1], width):
        ends.append(small[at:at + size // total])
        at += size // total
    gb_qkv, gb_out, gb_up, gb_down = ends
    grad_clean = small[at:].reshape(6, -1)
    back = lambda v: jnp.stack(v, axis=0).reshape(full).transpose(1, 2, 0, 3)
    return (back(y), back(gtokens), grad_noise, grad_clean, gw_qkv, gb_qkv, gw_out, gb_out, gw_up, gb_up, gw_down, gb_down)


def solution(mesh):
    token = P("frame", "row", "clip", None)
    rows = P(ALL, None)
    return jax.shard_map(
        on_device,
        mesh=mesh,
        in_specs=(token, P("clip"), P("frame", "clip", None, None)) + (P(),) * 9 + (token,),
        out_specs=(token, token, P("frame", "clip", None, "row"), P(None, ALL), rows, P(ALL), rows, P(ALL), rows, P(ALL), rows, P(ALL)),
        check_vma=False,
    )
```

time: 952 us -> 561 us (0.59)
  Pallas kernels: 200 us -> 472 us
  waiting for transfers between devices: 233 us -> 2.07 us
  local copies, waits for them, and re-layouts: 200 us -> 49.4 us
  matrix products: 150 us -> 0 us
  other arithmetic: 79.6 us -> 17 us
  starting transfers between devices: 76.4 us -> 15.2 us
    pallas_call x4 -> x17, Pallas kernels: 200 us -> 472 us  [the longest x1 161 us: attention_backward(): pl.pallas_call(functools.partial(bwd_all_kernel, calls=calls, count=len(p...]
    dot_general x13 -> x0, matrix products: 150 us -> none  [the longest x8 103 us: dot(): return lax.dot_general(a, b, dims, preferred_element_type=jnp.float32)]
    ppermute x24 -> x4, waiting for transfers between devices: 123 us -> 0.01 us  [swap(): return lax.ppermute(block, axis, [(i, i ^ bit) for i in range(size)])]
    all_to_all x10 -> x3, waiting for transfers between devices: 109 us -> 2.06 us  [exchange(): return lax.all_to_all(blocks, axes, 0, 0, tiled=True)]
    dynamic_slice x6 -> x0, local copies, waits for them, and re-layouts: 53 us -> none  [the longest x4 45.1 us: half_step(): keep = lax.dynamic_index_in_dim(array, mine, dim, keepdims=False)]
    reshape x6 -> x2, local copies, waits for them, and re-layouts: 41.5 us -> 1.19 us  [on_device(): gw_qkv.reshape(per, 2, hg // 2, 3, lw).transpose(0, 3, 1, 2, 4)]
    all_to_all x10 -> x3, starting transfers between devices: 52.4 us -> 14 us  [exchange(): return lax.all_to_all(blocks, axes, 0, 0, tiled=True)]
    convert_element_type x25 -> x0, other arithmetic: 33.7 us -> none  [the longest x20 29.2 us: half_step(): return (keep.astype(F32) + got.astype(F32)).astype(array.dtype)]
  transfers between devices with their start and end apart: 34 -> 7, of which waited for: 10 -> 1; matrix products, arithmetic and copies ran while one was open for 28% -> 6% of each run, Pallas kernels for 21% -> 9%
where the time goes in v2:
time: 561 us; the launch traced here: 557 us
  Pallas kernels  472 us (84%)
  local copies, waits for them, and re-layouts  49.4 us (9%)
  other arithmetic  17 us (3%)
  starting transfers between devices  15.2 us (3%)
    pallas_call x1, Pallas kernels, attention_backward(): pl.pallas_call(functools.partial(bwd_all_kernel, calls=calls, count=len(p...  161 us
    pallas_call x1, Pallas kernels, attention_forward(): pl.pallas_call(functools.partial(fwd_all_kernel, calls=calls), in_specs=[...  110 us
    pallas_call x2, Pallas kernels, mlp(): pl.pallas_call(mlp_kernel, grid=(ff // fc,), in_specs=[pl.BlockSpec((None...  71.5 us
    pallas_call x8, Pallas kernels, outer(): pl.pallas_call(functools.partial(outer_kernel, clips=clips, packed=packed...  49 us
    pallas_call x1, Pallas kernels, scatter_sums(): pl.pallas_call(functools.partial(sums_kernel, count=len(parts), jobs=jobs...  45.5 us
    unnamed x106, local copies, waits for them, and re-layouts  29.5 us
    pallas_call x2, Pallas kernels, qkv_back(): pl.pallas_call(qkv_back_kernel, grid=(1,), in_specs=[pl.BlockSpec((None,...  21.4 us
    all_to_all x3, starting transfers between devices, exchange(): return lax.all_to_all(blocks, axes, 0, 0, tiled=True)  14 us
  transfers between devices with their start and end apart: 7, of which 1 were waited for; matrix products, arithmetic and copies ran while one was open for 6% of the time, Pallas kernels for 9%

profile of v2, /device:TPU:1, one launch (start us, length us, event | category | flops | bytes accessed | tf_op | source)
XLA Modules:
  0.0 556.8 jit_solution(14912897798378945851)
XLA Ops:
  9.6 6.7 %qkv.3 = (bf16[8,512,384]{2,1,0:T(8,128)(2,1)S(1)}, bf16[512,1024]{1,0:T(8,128)(2,1)S(1)}) custom-call(bf16[512,1024]{1,0:T(8,128)(2,1)S(1)} %bitcast.65, f32[8,6,1024]{2,1,0:T(8,128)S(1)} %get-tuple-element.114.mod_ref, bf16[1024,3072]{1,0:T(8,128)(2,1)} %w_ref.3, f32[1,3072]{1,0:T(1,128)S(1)} %bitcast.74, f32[512,128]{1,0:T(8,128)S(1)} %copy.59.cos_ref, ...), custom_call_target="tpu_custom_call" | custom-call | flops 3221225472 | bytes 11534336 | tf_op jit(solution)/shard_map/qkv/pallas_call | solution.py:271
  18.0 6.5 %qkv.2 = (bf16[8,512,384]{2,1,0:T(8,128)(2,1)S(1)}, bf16[512,1024]{1,0:T(8,128)(2,1)S(1)}) custom-call(bf16[512,1024]{1,0:T(8,128)(2,1)S(1)} %bitcast.68, f32[8,6,1024]{2,1,0:T(8,128)S(1)} %get-tuple-element.115.mod_ref, bf16[1024,3072]{1,0:T(8,128)(2,1)} %w_ref.3, f32[1,3072]{1,0:T(1,128)S(1)} %bitcast.75, f32[512,128]{1,0:T(8,128)S(1)} %copy.59.cos_ref, ...), custom_call_target="tpu_custom_call" | custom-call | flops 3221225472 | bytes 11534336 | tf_op jit(solution)/shard_map/qkv/pallas_call | solution.py:271
  26.2 110.1 %attention_forward.1 = (bf16[2,2,4,8,64,384]{5,4,3,2,1,0:T(8,128)(2,1)}, bf16[2,8,8,64,128]{4,3,2,1,0:T(8,128)(2,1)}, f32[2,128,4096]{2,1,0:T(8,128)}, f32[2,2,4096]{2,1,0:T(2,128)}) custom-call(bf16[8,8,64,384]{3,2,1,0:T(8,128)(2,1)} %bitcast.77, bf16[8,8,64,384]{3,2,1,0:T(8,128)(2,1)} %bitcast.76), custom_call_target="tpu_custom_call" | custom-call | flops 8589934592 | bytes 25165824 | tf_op jit(solution)/shard_map/attention_forward/pallas_call | solution.py:579
  136.3 35.9 %mlp.2 = (bf16[512,1024]{1,0:T(8,128)(2,1)}, f32[512,1024]{1,0:T(8,128)}, bf16[8,512,128]{2,1,0:T(8,128)(2,1)}, bf16[512,1024]{1,0:T(8,128)(2,1)}, bf16[512,1024...) custom-call(bf16[2,8,512,128]{3,2,1,0:T(8,128)(2,1)} %bitcast.98, ...), custom_call_target="tpu_custom_call" | custom-call | flops 19327352832 | bytes 37748736 | tf_op jit(solution)/shard_map/mlp/pallas_call | solution.py:367
  172.2 35.6 %mlp.3 = (bf16[512,1024]{1,0:T(8,128)(2,1)}, f32[512,1024]{1,0:T(8,128)}, bf16[8,512,128]{2,1,0:T(8,128)(2,1)}, bf16[512,1024]{1,0:T(8,128)(2,1)}, bf16[512,1024...) custom-call(bf16[2,8,512,128]{3,2,1,0:T(8,128)(2,1)} %bitcast.99, ...), custom_call_target="tpu_custom_call" | custom-call | flops 19327352832 | bytes 37748736 | tf_op jit(solution)/shard_map/mlp/pallas_call | solution.py:367
  212.4 7.7 %outer.10 = bf16[1024,2048]{1,0:T(8,128)(2,1)} custom-call(s32[1]{0:T(128)S(6)} %sub.52.half_ref, bf16[512,1024]{1,0:T(8,128)(2,1)S(1)} %copy-done.31, bf16[512,1024]{1,0:T(8,128)(2,1)S(1)} %copy-done.35, bf16[512,4096]{1,0:T(8,128)(2,1)S(1)} %copy-done.11, bf16[512,4096]{1,0:T(8,128)(2,1)} %get-tuple-element.71.refs_3_), custom_call_target="tpu_custom_call" | custom-call | flops 4294967296 | bytes 10485760 | tf_op jit(solution)/shard_map/outer/pallas_call | solution.py:464
  220.2 8.4 %outer.8 = bf16[4096,512]{1,0:T(8,128)(2,1)} custom-call(s32[1]{0:T(128)S(6)} %sub.52.half_ref, bf16[512,4096]{1,0:T(8,128)(2,1)S(1)} %copy-done.9, bf16[512,4096]{1,0:T(8,128)(2,1)} %get-tuple-element.65.refs_1_, bf16[512,1024]{1,0:T(8,128)(2,1)S(1)} %copy-done.29, bf16[512,1024]{1,0:T(8,128)(2,1)S(1)} %copy-done.33), custom_call_target="tpu_custom_call" | custom-call | flops 4294967296 | bytes 13631488 | tf_op jit(solution)/shard_map/outer/pallas_call | solution.py:464
  231.6 5.3 all-to-all-start
  236.8 2.9 fusion
  248.4 7.2 %outer.11 = bf16[1024,2048]{1,0:T(8,128)(2,1)S(1)} custom-call(s32[1]{0:T(128)} %bitcast.24.half_ref, bf16[512,1024]{1,0:T(8,128)(2,1)S(1)} %copy-done.32, bf16[512,1024]{1,0:T(8,128)(2,1)S(1)} %copy-done.36, bf16[512,4096]{1,0:T(8,128)(2,1)S(1)} %copy-done.12, bf16[512,4096]{1,0:T(8,128)(2,1)} %get-tuple-element.71.refs_3_, ...), custom_call_target="tpu_custom_call" | custom-call | flops 4294967296 | bytes 10485760 | tf_op jit(solution)/shard_map/outer/pallas_call | solution.py:464
  257.6 7.3 %outer.9 = bf16[4096,512]{1,0:T(8,128)(2,1)S(1)} custom-call(s32[1]{0:T(128)} %bitcast.24.half_ref, bf16[512,4096]{1,0:T(8,128)(2,1)S(1)} %copy-done.10, bf16[512,4096]{1,0:T(8,128)(2,1)} %get-tuple-element.65.refs_1_, bf16[512,1024]{1,0:T(8,128)(2,1)S(1)} %copy-done.30, bf16[512,1024]{1,0:T(8,128)(2,1)S(1)} %copy-done.34, ...), custom_call_target="tpu_custom_call" | custom-call | flops 4294967296 | bytes 13631488 | tf_op jit(solution)/shard_map/outer/pallas_call | solution.py:464
  266.9 160.8 %attention_backward.1 = (bf16[2,8,8,64,384]{4,3,2,1,0:T(8,128)(2,1)}, f32[128,1024]{1,0:T(8,128)}, f32[32,4096]{1,0:T(8,128)}, f32[32,1024]{1,0:T(8,128)}) custom-call(bf16[2,2,4,8,64,384]{5,4,3,2,1,0:T(8,128)(2,1)} %get-tuple-element.59.refs_0_, bf16[2,4,8,64,128]{4,3,2,1,0:T(8,128)(2,1)} %bitcast.22.refs_1_, f32[2,128,4096]{2,1,0:T(8,128)} %get-tuple-element.61.refs_2_, ...), custom_call_target="tpu_custom_call" | custom-call | flops 21474836480 | bytes 50331648 | tf_op jit(solution)/shard_map/attention_backward/pallas_call | solution.py:798
  430.6 6.4 %outer.14 = bf16[1024,1536]{1,0:T(8,128)(2,1)} custom-call(s32[1]{0:T(128)S(6)} %sub.52.half_ref, bf16[512,1024]{1,0:T(8,128)(2,1)S(1)} %get-tuple-element.91.refs_0_, bf16[512,1024]{1,0:T(8,128)(2,1)S(1)} %get-tuple-element.92.refs_1_, bf16[2,8,512,384]{3,2,1,0:T(8,128)(2,1)S(1)} %bitcast.60, bf16[2,8,512,384]{3,2,1,0:T(8,128)(2,1)S(1)} %bitcast.61), custom_call_target="tpu_custom_call" | custom-call | flops 3221225472 | bytes 8388608 | tf_op jit(solution)/shard_map/outer/pallas_call | solution.py:464
  437.7 3.0 copy.64
  440.8 3.0 copy.65
  443.8 5.6 %maximum_bitcast_fusion.1 = bf16[8,64,2,1024]{3,2,1,0:T(2,128)(2,1)} fusion(bf16[1,8,64,1024]{3,0,2,1:T(2,128)(2,1)S(1)} %copy.65, bf16[1,8,64,1024]{3,0,2,1:T(2,128)(2,1)S(1)} %copy.64), kind=kLoop, calls=%fused_computation.1 | loop fusion | flops 4194304 | bytes 4194304 | tf_op jit(solution)/shard_map/transpose | solution.py:909
  449.5 10.4 %qkv_back.2 = (f32[512,1024]{1,0:T(8,128)S(1)}, f32[8,2,1024]{2,1,0:T(2,128)S(1)}, f32[1,3072]{1,0:T(1,128)S(1)}) custom-call(bf16[2,8,512,384]{3,2,1,0:T(8,128)(2,1)} %bitcast.56, bf16[512,1024]{1,0:T(8,128)(2,1)S(1)} %bitcast.70, f32[512,1024]{1,0:T(8,128)S(1)} %copy-done.19, f32[8,6,1024]{2,1,0:T(8,128)S(1)} %copy-done.27, bf16[1024,3072]{1,0:T(8,128)(2,1)} %w_ref.3), custom_call_target="tpu_custom_call" | custom-call | flops 3221225472 | bytes 14680064 | tf_op jit(solution)/shard_map/qkv_back/pallas_call | solution.py:416
  460.0 11.1 %qkv_back.3 = (f32[512,1024]{1,0:T(8,128)S(1)}, f32[8,2,1024]{2,1,0:T(2,128)S(1)}, f32[1,3072]{1,0:T(1,128)S(1)}) custom-call(bf16[2,8,512,384]{3,2,1,0:T(8,128)(2,1)} %bitcast.57, bf16[512,1024]{1,0:T(8,128)(2,1)S(1)} %bitcast.67, f32[512,1024]{1,0:T(8,128)S(1)} %copy-done.20, f32[8,6,1024]{2,1,0:T(8,128)S(1)} %copy-done.25, bf16[1024,3072]{1,0:T(8,128)(2,1)} %w_ref.3), custom_call_target="tpu_custom_call" | custom-call | flops 3221225472 | bytes 14680064 | tf_op jit(solution)/shard_map/qkv_back/pallas_call | solution.py:416
  473.7 5.1 all-to-all-start.2
  478.9 3.9 copy.66
  485.0 5.7 %maximum_bitcast_fusion = f32[8,64,2,1024]{3,2,1,0:T(2,128)} fusion(f32[1,8,64,1024]{3,0,2,1:T(1,128)S(1)} %copy.67, f32[1,8,64,1024]{3,0,2,1:T(1,128)S(1)} %copy.66), kind=kLoop, calls=%fused_computation | loop fusion | flops 1048576 | bytes 8388608 | tf_op jit(solution)/shard_map/transpose | solution.py:909
  491.7 3.6 all-to-all-start.1
  500.5 7.0 %outer.15 = bf16[1024,1536]{1,0:T(8,128)(2,1)S(1)} custom-call(s32[1]{0:T(128)} %bitcast.24.half_ref, bf16[512,1024]{1,0:T(8,128)(2,1)S(1)} %get-tuple-element.91.refs_0_, bf16[512,1024]{1,0:T(8,128)(2,1)S(1)} %get-tuple-element.92.refs_1_, bf16[2,8,512,384]{3,2,1,0:T(8,128)(2,1)} %bitcast.58, bf16[2,8,512,384]{3,2,1,0:T(8,128)(2,1)} %bitcast.59, ...), custom_call_target="tpu_custom_call" | custom-call | flops 3221225472 | bytes 8388608 | tf_op jit(solution)/shard_map/outer/pallas_call | solution.py:464
  507.5 45.5 %scatter_sums.1 = f32[32,3072]{1,0:T(8,128)S(1)} custom-call(bf16[4,4,64,1536]{3,2,1,0:T(8,128)(2,1)S(1)} %bitcast.62), custom_call_target="tpu_custom_call" | custom-call | bytes 125829120 | tf_op jit(solution)/shard_map/scatter_sums/pallas_call | solution.py:713
  (167 shorter events, 50.6 us)
Async XLA Ops:
  3.3 14.7 %copy-start.26 = (f32[8,6,1024]{2,1,0:T(8,128)}, f32[8,6,1024]{2,1,0:T(8,128)S(1)}, u32[]{:S(2)}) copy-start(f32[8,6,1024]{2,1,0:T(8,128)S(1)} %get-tuple-element.115.mod_ref) | copy-start | bytes 589828
  7.4 10.6 %copy-start.17 = (bf16[1,8,64,1024]{3,2,1,0:T(8,128)(2,1)}, bf16[1,8,64,1024]{3,2,1,0:T(8,128)(2,1)S(1)}, u32[]{:S(2)}) copy-start(bf16[1,8,64,1024]{3,2,1,0:T(8,128)(2,1)S(1)} %get-tuple-element.113) | copy-start | bytes 3145732
  220.1 28.2 %collective-permute-start.1 = (bf16[1024,2048]{1,0:T(8,128)(2,1)}, bf16[1024,2048]{1,0:T(8,128)(2,1)}, u32[]{:S(2)}, u32[]{:S(2)}) collective-permute-start(bf16[1024,2048]{1,0:T(8,128)(2,1)} %outer.10), channel_id=1, source_target_pairs={{0,1},{1,0},{2,3},{3,2},{4,5},{5,4},{6,7},{7,6},{8,9},{9,8},{10,11... | collective-permute-start | bytes 12582920 | tf_op jit(solution)/shard_map/ppermute | solution.py:815
  220.1 9.0 %copy-start.1 = (bf16[512,1024]{1,0:T(8,128)(2,1)S(1)}, bf16[512,1024]{1,0:T(8,128)(2,1)}, u32[]{:S(2)}) copy-start(bf16[512,1024]{1,0:T(8,128)(2,1)} %get-tuple-element.74.refs_2_) | copy-start | bytes 3145732
  220.1 9.0 %copy-start.3 = (bf16[512,1024]{1,0:T(8,128)(2,1)S(1)}, bf16[512,1024]{1,0:T(8,128)(2,1)}, u32[]{:S(2)}) copy-start(bf16[512,1024]{1,0:T(8,128)(2,1)} %get-tuple-element.72.refs_0_) | copy-start | bytes 3145732
  220.1 9.0 %copy-start.5 = (bf16[512,1024]{1,0:T(8,128)(2,1)S(1)}, bf16[512,1024]{1,0:T(8,128)(2,1)}, u32[]{:S(2)}) copy-start(bf16[512,1024]{1,0:T(8,128)(2,1)} %get-tuple-element.75.refs_3_) | copy-start | bytes 3145732
  228.6 29.0 %collective-permute-start = (bf16[4096,512]{1,0:T(8,128)(2,1)}, bf16[4096,512]{1,0:T(8,128)(2,1)}, u32[]{:S(2)}, u32[]{:S(2)}) collective-permute-start(bf16[4096,512]{1,0:T(8,128)(2,1)} %outer.8), channel_id=1, source_target_pairs={{0,1},{1,0},{2,3},{3,2},{4,5},{5,4},{6,7},{7,6},{8,9},{9,8},{10,11... | collective-permute-start | bytes 12582920 | tf_op jit(solution)/shard_map/ppermute | solution.py:815
  231.5 8.2 %collective-permute-start.2 = (bf16[1024,512]{1,0:T(8,128)(2,1)}, bf16[1024,512]{1,0:T(8,128)(2,1)}, u32[]{:S(2)}, u32[]{:S(2)}) collective-permute-start(bf16[1024,512]{1,0:T(8,128)(2,1)} %outer.12), channel_id=1, source_target_pairs={{0,1},{1,0},{2,3},{3,2},{4,5},{5,4},{6,7},{7,6},{8,9},{9,8},{10,11... | collective-permute-start | bytes 3145736 | tf_op jit(solution)/shard_map/ppermute | solution.py:815
  231.6 35.4 %all-to-all-start = ((bf16[8,8,64,128]{3,2,1,0:T(8,128)(2,1)}), bf16[8,8,64,128]{3,2,1,0:T(8,128)(2,1)}, u32[]{:S(2)}, u32[]{:S(2)}) async-start(bf16[8,8,64,128]{3,2,1,0:T(8,128)(2,1)} %bitcast.83), calls=%async_computation | async-start | bytes 2097152 | tf_op jit(solution)/shard_map/all_to_all | solution.py:819
  248.3 9.3 %copy-start.10 = (bf16[512,4096]{1,0:T(8,128)(2,1)S(1)}, bf16[512,4096]{1,0:T(8,128)(2,1)}, u32[]{:S(2)}) copy-start(bf16[512,4096]{1,0:T(8,128)(2,1)} %get-tuple-element.64.refs_0_) | copy-start | bytes 12582916
  248.3 9.3 %copy-start.30 = (bf16[512,1024]{1,0:T(8,128)(2,1)S(1)}, bf16[512,1024]{1,0:T(8,128)(2,1)}, u32[]{:S(2)}) copy-start(bf16[512,1024]{1,0:T(8,128)(2,1)} %get-tuple-element.66.refs_2_) | copy-start | bytes 3145732
  248.3 9.3 %copy-start.34 = (bf16[512,1024]{1,0:T(8,128)(2,1)S(1)}, bf16[512,1024]{1,0:T(8,128)(2,1)}, u32[]{:S(2)}) copy-start(bf16[512,1024]{1,0:T(8,128)(2,1)} %get-tuple-element.67.refs_3_) | copy-start | bytes 3145732
  436.9 63.5 %collective-permute-start.3 = (bf16[1024,1536]{1,0:T(8,128)(2,1)}, bf16[1024,1536]{1,0:T(8,128)(2,1)}, u32[]{:S(2)}, u32[]{:S(2)}) collective-permute-start(bf16[1024,1536]{1,0:T(8,128)(2,1)} %outer.14), channel_id=1, source_target_pairs={{0,1},{1,0},{2,3},{3,2},{4,5},{5,4},{6,7},{7,6},{8,9},{9,8},{10,11... | collective-permute-start | bytes 9437192 | tf_op jit(solution)/shard_map/ppermute | solution.py:815
  449.4 10.4 %copy-start.43 = (f32[8,4,1024]{2,1,0:T(4,128)S(1)}, f32[8,4,1024]{2,1,0:T(4,128)}, u32[]{:S(2)}) copy-start(f32[8,4,1024]{2,1,0:T(4,128)} %get-tuple-element.82) | copy-start | bytes 393220
  449.5 10.5 %copy-start.16 = (bf16[1,8,64,1024]{3,2,1,0:T(8,128)(2,1)S(1)}, bf16[1,8,64,1024]{3,2,1,0:T(8,128)(2,1)}, u32[]{:S(2)}) copy-start(bf16[1,8,64,1024]{3,2,1,0:T(8,128)(2,1)} %copy-done.15) | copy-start | bytes 3145732
  449.5 10.5 %copy-start.20 = (f32[512,1024]{1,0:T(8,128)S(1)}, f32[512,1024]{1,0:T(8,128)}, u32[]{:S(2)}) copy-start(f32[512,1024]{1,0:T(8,128)} %get-tuple-element.79.gm_ref) | copy-start | bytes 6291460
  449.5 10.5 %copy-start.25 = (f32[8,6,1024]{2,1,0:T(8,128)S(1)}, f32[8,6,1024]{2,1,0:T(8,128)}, u32[]{:S(2)}) copy-start(f32[8,6,1024]{2,1,0:T(8,128)} %copy-done.24) | copy-start | bytes 589828
  459.8 11.2 %copy-start.21 = (f32[512,1024]{1,0:T(8,128)}, f32[512,1024]{1,0:T(8,128)S(1)}, u32[]{:S(2)}) copy-start(f32[512,1024]{1,0:T(8,128)S(1)} %get-tuple-element.78) | copy-start | bytes 6291460
  460.0 12.4 %copy-start.44 = (f32[8,4,1024]{2,1,0:T(4,128)S(1)}, f32[8,4,1024]{2,1,0:T(4,128)}, u32[]{:S(2)}) copy-start(f32[8,4,1024]{2,1,0:T(4,128)} %get-tuple-element.84) | copy-start | bytes 393220
  473.7 17.9 %all-to-all-start.2 = ((f32[32,1,480]{2,1,0:T(1,128)}), f32[32,1,480]{2,1,0:T(1,128)S(1)}, u32[]{:S(2)}, u32[]{:S(2)}) async-start(f32[32,1,480]{2,1,0:T(1,128)} %copy.72), calls=%async_computation.2 | async-start | bytes 131072 | tf_op jit(solution)/shard_map/all_to_all | solution.py:819
  491.7 8.1 %all-to-all-start.1 = ((bf16[4,8,2,6,256]{4,1,3,2,0:T(8,128)(2,1)}), bf16[4,8,2,6,256]{4,1,3,2,0:T(8,128)(2,1)S(1)}, u32[]{:S(2)}, u32[]{:S(2)}) async-start(bf16[4,8,2,6,256]{4,1,3,2,0:T(8,128)(2,1)} %copy.69), calls=%async_computation.1 | async-start | bytes 393216 | tf_op jit(solution)/shard_map/all_to_all | solution.py:819
  507.4 46.9 %copy-start.45 = (f32[32,1024]{1,0:T(8,128)S(1)}, f32[32,1024]{1,0:T(8,128)}, u32[]{:S(2)}) copy-start(f32[32,1024]{1,0:T(8,128)} %get-tuple-element.147) | copy-start | bytes 393220
  507.5 47.5 %copy-start.42 = (f32[32,4096]{1,0:T(8,128)S(1)}, f32[32,4096]{1,0:T(8,128)}, u32[]{:S(2)}) copy-start(f32[32,4096]{1,0:T(8,128)} %get-tuple-element.149) | copy-start | bytes 1572868
  507.5 48.3 %copy-start.41 = (f32[128,1024]{1,0:T(8,128)S(1)}, f32[128,1024]{1,0:T(8,128)}, u32[]{:S(2)}) copy-start(f32[128,1024]{1,0:T(8,128)} %get-tuple-element.151) | copy-start | bytes 1572868
  (33 other events, 123.8 us)

commit v3 on v2

--- a/solution.py
+++ b/solution.py
@@ -246,8 +246,10 @@
     frames = mod_ref.shape[0]
     pt = count // frames
     copies = [pltpu.make_async_copy(w_hbm.at[:, pl.ds(j * width, width)], w.at[j], sem.at[j]) for j in range(3)]
-    for c in copies:
-        c.start()
+    @pl.when(pl.program_id(0) == 0)
+    def _():
+        for c in copies:
+            c.start()
     def one(f, _):
         rows = pl.ds(pl.multiple_of(f * pt, pt), pt)
         n, _inv = stats(x_ref[rows, :].astype(F32))
@@ -256,7 +258,9 @@
     lax.fori_loop(0, frames, one, 0)
     step = max(256, lw)
     for j in range(3):
-        copies[j].wait()
+        @pl.when(pl.program_id(0) == 0)
+        def _():
+            copies[j].wait()
         for a in range(0, width, step):
             t = dot(h_ref[...], w[j, :, a:a + step], NN) + b_ref[0:1, j * width + a:j * width + a + step]
             for g in range(step // lw):
@@ -267,211 +271,24 @@
 
 
 def qkv_forward(x, mods, w, b, cos, sin, hg, lw):
-    count, width = x.shape
+    clips, count, width = x.shape
+    frames = mods.shape[1]
+    one = lambda *shape: pl.BlockSpec((None,) + shape, lambda c: (c,) + (0,) * len(shape))
+    same = lambda *shape: pl.BlockSpec(shape, lambda c: (0,) * len(shape))
     return pl.pallas_call(
         qkv_kernel,
-        out_shape=(jax.ShapeDtypeStruct((hg, count, 3 * lw), B16), jax.ShapeDtypeStruct((count, width), B16)),
-        in_specs=[pl.BlockSpec(memory_space=pltpu.VMEM)] * 2 + [pl.BlockSpec(memory_space=pl.ANY)]
-        + [pl.BlockSpec(memory_space=pltpu.VMEM)] * 3,
+        grid=(clips,),
+        in_specs=[one(count, width), one(frames, 6, width), pl.BlockSpec(memory_space=pl.ANY), same(1, 3 * width), same(count, lw), same(count, lw)],
+        out_specs=(one(hg, count, 3 * lw), one(count, width)),
+        out_shape=(jax.ShapeDtypeStruct((clips, hg, count, 3 * lw), B16), jax.ShapeDtypeStruct((clips, count, width), B16)),
         scratch_shapes=[pltpu.VMEM((3, width, width), B16), pltpu.SemaphoreType.DMA((3,))],
-        compiler_params=pltpu.CompilerParams(vmem_limit_bytes=48 << 20),
-        cost_estimate=pl.CostEstimate(flops=6 * count * width * width, bytes_accessed=10 * count * width + 6 * width * width, transcendentals=0),
+        compiler_params=pltpu.CompilerParams(vmem_limit_bytes=48 << 20, dimension_semantics=("arbitrary",)),
+        cost_estimate=pl.CostEstimate(flops=6 * clips * count * width * width, bytes_accessed=clips * 10 * count * width + 6 * width * width, transcendentals=0),
         name="qkv",
     )(x, mods, w, b, cos, sin)
 
 
-def mlp_kernel(a_ref, x_ref, g_ref, mod_ref, wo_ref, bo_ref, wu_ref, bu_ref, wd_ref, bd_ref,
-               y_ref, gm_ref, ga_ref, gb_ref, an_ref, h_ref, gd_ref, act_ref, gp_ref, sums_ref, du_ref, db_ref,
-               branch, mixed, n2, inv2, down, gh):
-    hg, count, lw = a_ref.shape
-    width = x_ref.shape[1]
-    frames = mod_ref.shape[0]
-    pt = count // frames
-    step = pl.program_id(0)
-
-    def each(fn):
-        def one(f, _):
-            fn(f, pl.ds(pl.multiple_of(f * pt, pt), pt))
-            return 0
-        lax.fori_loop(0, frames, one, 0)
-
-    @pl.when(step == 0)
-    def _():
-        for g in range(hg):
-            an_ref[:, g * lw:(g + 1) * lw] = a_ref[g]
-        branch[...] = dot(an_ref[...], wo_ref[...], NN) + bo_ref[...]
-        def fn(f, rows):
-            m = x_ref[rows, :].astype(F32) + mod_ref[f, 2:3, :] * branch[rows, :]
-            n, inv = stats(m)
-            mixed[rows, :] = m
-            n2[rows, :] = n
-            inv2[rows, :] = jnp.broadcast_to(inv, (pt, 128))
-            h_ref[rows, :] = (n * (1.0 + mod_ref[f, 4:5, :]) + mod_ref[f, 3:4, :]).astype(B16)
-            gd_ref[rows, :] = (g_ref[rows, :].astype(F32) * mod_ref[f, 5:6, :]).astype(B16)
-        each(fn)
-        down[...] = jnp.zeros_like(down)
-        gh[...] = jnp.zeros_like(gh)
-
-    c0 = (2.0 / 3.141592653589793) ** 0.5
-    c1 = 0.044715
-    h, gd = h_ref[...], gd_ref[...]
-    wu, wd = wu_ref[...], wd_ref[...]
-    pre = dot(h, wu, NN) + bu_ref[...]
-    gact = dot(gd, wd, NT)
-    sq = pre * pre
-    u = jnp.tanh(pre * (c0 + (c0 * c1) * sq))
-    half = 0.5 * (1.0 + u)
-    act = (pre * half).astype(B16)
-    slope = half + (0.5 * pre) * (1.0 - u * u) * (c0 + (3.0 * c0 * c1) * sq)
-    gp = (gact * slope).astype(B16)
-    act_ref[...] = act
-    gp_ref[...] = gp
-    du_ref[...] = jnp.sum(gp.astype(F32), axis=0, keepdims=True)
-    down[...] += dot(act, wd, NN)
-    gh[...] += dot(gp, wu, NT)
-
-    @pl.when(step == pl.num_programs(0) - 1)
-    def _():
-        db_ref[...] = jnp.zeros_like(db_ref)
-        def fn(f, rows):
-            g = g_ref[rows, :].astype(F32)
-            d = down[rows, :] + bd_ref[...]
-            y_ref[rows, :] = (mixed[rows, :] + mod_ref[f, 5:6, :] * d).astype(B16)
-            ghf = gh[rows, :]
-            n = n2[rows, :]
-            t = ghf * (1.0 + mod_ref[f, 4:5, :])
-            back = t - jnp.mean(t, axis=1, keepdims=True) - n * jnp.mean(t * n, axis=1, keepdims=True)
-            gm = g + inv2[rows, 0:1] * back
-            gm_ref[rows, :] = gm
-            gbr = (gm * mod_ref[f, 2:3, :]).astype(B16)
-            gb_ref[rows, :] = gbr
-            s = lambda v: jnp.sum(v, axis=0, keepdims=True)
-            sums_ref[f] = jnp.concatenate([s(gm * branch[rows, :]), s(ghf), s(ghf * n), s(g * d)], axis=0)
-            db_ref[...] += jnp.concatenate([s(gbr.astype(F32)), s(gd_ref[rows, :].astype(F32))], axis=0)
-        each(fn)
-        ga = dot(gb_ref[...], wo_ref[...], NT).astype(B16)
-        for i in range(hg):
-            ga_ref[i] = ga[:, i * lw:(i + 1) * lw]
-
-
-def mlp(c, attn, x, g, mods, w_out, b_out, w_up, b_up, w_down, b_down):
-    _, hg, count, lw = attn.shape
-    width = x.shape[1]
-    ff = w_up.shape[1]
-    frames = mods.shape[0]
-    fc = min(512, ff)
-    whole = lambda *shape: pl.BlockSpec(shape, lambda j: (0,) * len(shape), pipeline_mode=pl.Buffered(1))
-    keep = lambda *shape: pl.BlockSpec(shape, lambda j: (0,) * len(shape))
-    cols = lambda m: pl.BlockSpec((m, fc), lambda j: (0, j))
-    s = jax.ShapeDtypeStruct
-    return pl.pallas_call(
-        mlp_kernel,
-        grid=(ff // fc,),
-        in_specs=[pl.BlockSpec((None, hg, count, lw), lambda j: (c, 0, 0, 0), pipeline_mode=pl.Buffered(1)), whole(count, width), whole(count, width), whole(frames, 6, width),
-                  whole(width, width), whole(1, width), cols(width), cols(1),
-                  pl.BlockSpec((fc, width), lambda j: (j, 0)), whole(1, width)],
-        out_specs=(keep(count, width), keep(count, width), keep(hg, count, lw), keep(count, width), keep(count, width),
-                   keep(count, width), keep(count, width), cols(count), cols(count), keep(frames, 4, width), cols(1), keep(2, width)),
-        out_shape=(s((count, width), B16), s((count, width), F32), s((hg, count, lw), B16), s((count, width), B16),
-                   s((count, width), B16), s((count, width), B16), s((count, width), B16), s((count, ff), B16),
-                   s((count, ff), B16), s((frames, 4, width), F32), s((1, ff), F32), s((2, width), F32)),
-        scratch_shapes=[pltpu.VMEM((count, width), F32)] * 3 + [pltpu.VMEM((count, 128), F32)]
-        + [pltpu.VMEM((count, width), F32)] * 2,
-        compiler_params=pltpu.CompilerParams(vmem_limit_bytes=60 << 20, dimension_semantics=("arbitrary",)),
-        cost_estimate=pl.CostEstimate(flops=2 * count * width * (2 * width + 4 * ff), bytes_accessed=4 * width * ff + 40 * count * width, transcendentals=count * ff),
-        name="mlp",
-    )(attn, x, g, mods, w_out, b_out, w_up, b_up, w_down, b_down)
-
-
-def qkv_back_kernel(gp_ref, x_ref, gm_ref, mod_ref, w_ref, o_ref, sums_ref, db_ref, full, gh):
-    hg, count, w3 = gp_ref.shape
-    lw = w3 // 3
-    width = x_ref.shape[1]
-    frames = mod_ref.shape[0]
-    pt = count // frames
-    for j in range(3):
-        for g in range(hg):
-            full[:, j * width + g * lw:j * width + (g + 1) * lw] = gp_ref[g, :, j * lw:(j + 1) * lw]
-    gh[...] = dot(full[...], w_ref[...], NT)
-    db_ref[...] = jnp.sum(full[...].astype(F32), axis=0, keepdims=True)
-    def one(f, _):
-        rows = pl.ds(pl.multiple_of(f * pt, pt), pt)
-        n, inv = stats(x_ref[rows, :].astype(F32))
-        ghf = gh[rows, :]
-        t = ghf * (1.0 + mod_ref[f, 1:2, :])
-        back = t - jnp.mean(t, axis=1, keepdims=True) - n * jnp.mean(t * n, axis=1, keepdims=True)
-        o_ref[rows, :] = gm_ref[rows, :] + inv * back
-        s = lambda v: jnp.sum(v, axis=0, keepdims=True)
-        sums_ref[f] = jnp.concatenate([s(ghf), s(ghf * n)], axis=0)
-        return 0
-    lax.fori_loop(0, frames, one, 0)
-
-
-def qkv_back(c, gproj, x, gmixed, mods, w):
-    _, hg, count, w3 = gproj.shape
-    width = x.shape[1]
-    frames = mods.shape[0]
-    s = jax.ShapeDtypeStruct
-    whole = lambda *shape: pl.BlockSpec(shape, lambda i: (0,) * len(shape))
-    return pl.pallas_call(
-        qkv_back_kernel,
-        grid=(1,),
-        in_specs=[pl.BlockSpec((None, hg, count, w3), lambda i: (c, 0, 0, 0)), whole(count, width), whole(count, width),
-                  whole(frames, 6, width), whole(width, 3 * width)],
-        out_specs=(whole(count, width), whole(frames, 2, width), whole(1, 3 * width)),
-        out_shape=(s((count, width), F32), s((frames, 2, width), F32), s((1, 3 * width), F32)),
-        scratch_shapes=[pltpu.VMEM((count, 3 * width), B16), pltpu.VMEM((count, width), F32)],
-        compiler_params=pltpu.CompilerParams(vmem_limit_bytes=48 << 20),
-        cost_estimate=pl.CostEstimate(flops=6 * count * width * width, bytes_accessed=16 * count * width + 6 * width * width, transcendentals=0),
-        name="qkv_back",
-    )(gproj, x, gmixed, mods, w)
-
-
 TN = (((0,), (0,)), ((), ()))
-
-
-def outer_kernel(half_ref, *refs, clips, packed, received):
-    a_refs, b_refs = refs[:clips], refs[clips:2 * clips]
-    o_ref = refs[-1]
-    total = None
-    for a_ref, b_ref in zip(a_refs, b_refs):
-        b = jnp.concatenate([b_ref[i] for i in range(packed)], axis=1) if packed else b_ref[...]
-        part = dot(a_ref[...], b, TN)
-        total = part if total is None else total + part
-    if received:
-        total = total + refs[2 * clips][...].astype(F32)
-    o_ref[...] = total.astype(B16)
-
-
-def outer(a_list, b_list, half, got=None):
-    clips = len(a_list)
-    count, rows = a_list[0].shape
-    grouped = not isinstance(b_list, (list, tuple))
-    if grouped:
-        _, groups, _, w3 = b_list.shape
-        packed = max(1, 128 * 3 // w3)
-        ch = groups // 2 * w3
-        cb, rb = packed * w3, rows
-        b_specs = [pl.BlockSpec((None, packed, count, w3), lambda i, j, h, c=c: (c, h[0] * (groups // 2 // packed) + j, 0, 0)) for c in range(clips)]
-        b_list = [b_list] * clips
-    else:
-        packed = 0
-        ch = b_list[0].shape[1] // 2
-        rb = min(rows, 1024)
-        cb = min(ch, 512)
-        b_specs = [pl.BlockSpec((count, cb), lambda i, j, h: (0, h[0] * (ch // cb) + j))] * clips
-    out = pl.BlockSpec((rb, cb), lambda i, j, h: (i, j))
-    return pl.pallas_call(
-        functools.partial(outer_kernel, clips=clips, packed=packed, received=got is not None),
-        grid_spec=pltpu.PrefetchScalarGridSpec(
-            num_scalar_prefetch=1, grid=(rows // rb, ch // cb),
-            in_specs=[pl.BlockSpec((count, rb), lambda i, j, h: (0, i))] * clips + b_specs + ([out] if got is not None else []),
-            out_specs=out),
-        out_shape=jax.ShapeDtypeStruct((rows, ch), B16),
-        compiler_params=pltpu.CompilerParams(vmem_limit_bytes=40 << 20, dimension_semantics=("arbitrary", "arbitrary")),
-        cost_estimate=pl.CostEstimate(flops=2 * clips * count * rows * ch, bytes_accessed=2 * clips * count * (rows + ch) + 2 * rows * ch, transcendentals=0),
-        name="outer",
-    )(half, *a_list, *b_list, *([got] if got is not None else []))
 
 
 MESH = pl.DeviceIdType.MESH
@@ -537,24 +354,23 @@
 
 def fwd_all_kernel(*refs, calls):
     plane = Plane()
-    x_send = refs[:calls]
-    x_out, a_out, ot_ref, lse_ref = refs[calls:calls + 4]
-    xv, ob, qm, kf, vt, sb, acc, mrow, xs, xr, xl, os, orr, ol, save = refs[calls + 4:]
+    x_send, x_out, a_out, ot_ref, lse_ref = refs[:5]
+    xv, ob, qm, kf, vt, sb, acc, mrow, xs, xr, xl, os, orr, ol, save = refs[5:]
     greet(plane, False)
     for i in range(calls):
-        pltpu.make_async_copy(x_send[i].at[plane.me], xv.at[i, plane.f, plane.r], xl.at[i]).start()
+        pltpu.make_async_copy(x_send.at[i, plane.me], xv.at[i, plane.f, plane.r], xl.at[i]).start()
         for k in range(1, plane.size):
             p, f, r = plane.peer(k)
-            remote(x_send[i].at[p], xv.at[i, plane.f, plane.r], xs.at[i, k], xr.at[i, k], {"frame": f, "row": r}).start()
+            remote(x_send.at[i, p], xv.at[i, plane.f, plane.r], xs.at[i, k], xr.at[i, k], {"frame": f, "row": r}).start()
 
     def arrive(i, what):
         for k in range(1, plane.size):
             p, f, r = plane.peer(k)
-            copy = remote(x_send[0].at[p], xv.at[i, plane.f, plane.r], xs.at[i, k], xr.at[i, k], {"frame": f, "row": r})
+            copy = remote(x_send.at[i, p], xv.at[i, plane.f, plane.r], xs.at[i, k], xr.at[i, k], {"frame": f, "row": r})
             copy.wait_recv() if what else copy.wait_send()
 
     def call(i, _):
-        pltpu.make_async_copy(x_send[0].at[plane.me], xv.at[i, plane.f, plane.r], xl.at[i]).wait()
+        pltpu.make_async_copy(x_send.at[i, plane.me], xv.at[i, plane.f, plane.r], xl.at[i]).wait()
         arrive(i, True)
         pltpu.make_async_copy(xv.at[i], x_out.at[i], save.at[i]).start()
         flash_forward(xv.at[i], ob.at[i], ot_ref.at[i], lse_ref.at[i], qm, kf, vt, sb, acc, mrow,
@@ -568,7 +384,7 @@
 
 
 def attention_forward(sends, lead, lw):
-    calls = len(sends)
+    calls = sends.shape[0]
     nf, nr, fl, pt = lead
     group = nf * nr
     nh = lw // HD
@@ -578,7 +394,7 @@
     s, v, dma = jax.ShapeDtypeStruct, pltpu.VMEM, pltpu.SemaphoreType.DMA
     return pl.pallas_call(
         functools.partial(fwd_all_kernel, calls=calls),
-        in_specs=[hbm] * calls,
+        in_specs=[hbm],
         out_specs=(hbm, hbm, vmem, vmem),
         out_shape=(s((calls,) + lead + (3 * lw,), B16), s((calls, group, fl, pt, lw), B16),
                    s((calls, lw, seq), F32), s((calls, nh, seq), F32)),
@@ -589,7 +405,7 @@
         compiler_params=pltpu.CompilerParams(vmem_limit_bytes=56 << 20, collective_id=0, has_side_effects=True),
         cost_estimate=pl.CostEstimate(flops=calls * seq * seq * lw * 2, bytes_accessed=calls * seq * lw * 24, transcendentals=calls * seq * seq * nh // 2),
         name="attention_forward",
-    )(*sends)
+    )(sends)
 
 
 class Sum:
@@ -690,36 +506,6 @@
 def make_sums(plane, jobs, parts, outs, scratch):
     return [Sum(plane, plane_first, parts[n], outs[n], (first, cols), parts[n].shape[3], *scratch[6 * i:6 * i + 6])
             for i, (n, plane_first, first, cols) in enumerate(jobs)]
-
-
-def sums_kernel(*refs, count, jobs):
-    plane = Plane()
-    sums = make_sums(plane, jobs, refs[:count], refs[count:2 * count], refs[2 * count:])
-    greet(plane, True)
-    for s in sums:
-        s.start(1)
-    for s in sums:
-        s.wait(1)
-        s.middle()
-    for s in sums:
-        s.wait(2)
-        s.last()
-    for s in sums:
-        s.close()
-
-
-def scatter_sums(parts, orders, collective_id):
-    scratch, outs, jobs = sum_plan(parts, orders)
-    return pl.pallas_call(
-        functools.partial(sums_kernel, count=len(parts), jobs=jobs),
-        in_specs=[pl.BlockSpec(memory_space=pl.ANY)] * len(parts),
-        out_specs=[pl.BlockSpec(memory_space=pltpu.VMEM)] * len(parts),
-        out_shape=outs,
-        scratch_shapes=scratch,
-        compiler_params=pltpu.CompilerParams(vmem_limit_bytes=48 << 20, collective_id=collective_id, has_side_effects=True),
-        cost_estimate=pl.CostEstimate(flops=0, bytes_accessed=sum(2 * p.size for p in parts) * 40, transcendentals=0),
-        name="scatter_sums",
-    )(*parts)
 
 
 def bwd_all_kernel(*refs, calls, count, jobs):
@@ -810,17 +596,412 @@
     )(x, go, ot, lse, cos, sin, *go_sends, *parts)
 
 
-def swap(block, axis, bit):
-    size = lax.axis_size(axis)
-    return lax.ppermute(block, axis, [(i, i ^ bit) for i in range(size)])
-
-
-def exchange(blocks, axes=("frame", "row")):
-    return lax.all_to_all(blocks, axes, 0, 0, tiled=True)
-
-
-def after(value, *others):
-    return lax.optimization_barrier((value,) + others)[0]
+def mlp_kernel(a_ref, x_hbm, g_hbm, mod_ref, wo_ref, bo_ref, wu_ref, bu_ref, wd_ref, bd_ref,
+               y_out, gm_out, ga_out, go_out, pd_out, pu_out, po_out, sums_ref, du_ref, db_ref,
+               g, an, branch, mixed, h, gd, down, gh, st, gav, sd, su, rd, ru, kd, ku, pd, pu, *sems, calls):
+    io, od, pair, free, done, gs, gr, gl, oo = sems
+    plane = Plane()
+    bit = lax.rem(plane.r, 2)
+    partner = {"row": plane.r + 1 - 2 * bit}
+    clips, hg, count, lw = a_ref.shape
+    width = an.shape[1]
+    frames = mod_ref.shape[0]
+    pt = clips * count // frames
+    step, steps = pl.program_id(0), pl.num_programs(0)
+    fc = wu_ref.shape[1]
+    slots = rd.shape[0]
+    hw, hf = width // 2, fc // 2
+
+    def each(first, last, fn):
+        def one(f, _):
+            fn(f, pl.ds(pl.multiple_of(f * pt, pt), pt))
+            return 0
+        lax.fori_loop(first, last, one, 0)
+
+    def split(value, size, send, keep):
+        for b in range(2):
+            @pl.when(bit == b)
+            def _():
+                send[...] = value[:, (1 - b) * size:(2 - b) * size].astype(B16)
+                keep[...] = value[:, b * size:(b + 1) * size]
+
+    @pl.when(step == 0)
+    def _():
+        loads = [pltpu.make_async_copy(x_hbm, h, io.at[0]), pltpu.make_async_copy(g_hbm, g.at[pl.ds(0, clips * count)], io.at[1])]
+        for c in loads:
+            c.start()
+        greet(plane, False)
+        for c in range(clips):
+            for i in range(hg):
+                an[c * count:(c + 1) * count, i * lw:(i + 1) * lw] = a_ref[c, i]
+        branch[...] = dot(an[:clips * count, :], wo_ref[...], NN) + bo_ref[...]
+        for c in loads:
+            c.wait()
+        def fn(f, rows):
+            m = h[rows, :].astype(F32) + mod_ref[f, 2:3, :] * branch[rows, :]
+            mean = jnp.mean(m, axis=1, keepdims=True)
+            centre = m - mean
+            inv = lax.rsqrt(jnp.mean(centre * centre, axis=1, keepdims=True) + 1e-06)
+            mixed[rows, :] = m
+            st[rows, :128] = jnp.broadcast_to(mean, (pt, 128))
+            st[rows, 128:] = jnp.broadcast_to(inv, (pt, 128))
+            h[rows, :] = (centre * inv * (1.0 + mod_ref[f, 4:5, :]) + mod_ref[f, 3:4, :]).astype(B16)
+            gd[rows, :] = (g[rows, :].astype(F32) * mod_ref[f, 5:6, :]).astype(B16)
+        each(0, frames, fn)
+        down[...] = jnp.zeros_like(down)
+        gh[...] = jnp.zeros_like(gh)
+
+    c0 = (2.0 / 3.141592653589793) ** 0.5
+    c1 = 0.044715
+    wu, wd = wu_ref[...], wd_ref[...]
+    wide, tall, bias = None, None, None
+    for c in range(clips):
+        rows = slice(c * count, (c + 1) * count)
+        hr, gr_ = h[rows, :], gd[rows, :]
+        pre = dot(hr, wu, NN) + bu_ref[...]
+        gact = dot(gr_, wd, NT)
+        sq = pre * pre
+        u = jnp.tanh(pre * (c0 + (c0 * c1) * sq))
+        half = 0.5 * (1.0 + u)
+        act = (pre * half).astype(B16)
+        slope = half + (0.5 * pre) * (1.0 - u * u) * (c0 + (3.0 * c0 * c1) * sq)
+        gp = (gact * slope).astype(B16)
+        down[rows, :] += dot(act, wd, NN)
+        gh[rows, :] += dot(gp, wu, NT)
+        d, t, b = dot(act, gr_, TN), dot(hr, gp, TN), jnp.sum(gp.astype(F32), axis=0, keepdims=True)
+        wide = d if wide is None else wide + d
+        tall = t if tall is None else tall + t
+        bias = b if bias is None else bias + b
+    du_ref[...] = bias
+    now, slot = lax.rem(step, 2), lax.rem(step, slots)
+
+    def swaps(j):
+        n, s = lax.rem(j, 2), lax.rem(j, slots)
+        return (remote(sd.at[n], rd.at[s], pair.at[0, n], pair.at[1, s], partner),
+                remote(su.at[n], ru.at[s], pair.at[2, n], pair.at[3, s], partner))
+
+    def stores(j):
+        n = lax.rem(j, 2)
+        return (pltpu.make_async_copy(pd.at[n], pd_out.at[pl.ds(pl.multiple_of(j * fc, fc), fc)], od.at[0, n]),
+                pltpu.make_async_copy(pu.at[n], pu_out.at[:, pl.ds(pl.multiple_of(j * hf, hf), hf)], od.at[1, n]))
+
+    def finish(j):
+        n, s = lax.rem(j, 2), lax.rem(j, slots)
+        @pl.when(j >= 2)
+        def _():
+            for c in stores(j - 2):
+                c.wait()
+        for c in swaps(j):
+            c.wait_recv()
+        pd[n] = (kd[n] + rd[s].astype(F32)).astype(B16)
+        pu[n] = (ku[n] + ru[s].astype(F32)).astype(B16)
+        for c in stores(j):
+            c.start()
+        @pl.when(j + slots < steps)
+        def _():
+            pl.semaphore_signal(free, inc=1, device_id=partner, device_id_type=MESH)
+
+    @pl.when(step >= 2)
+    def _():
+        for c in swaps(step - 2):
+            c.wait_send()
+    split(wide, hw, sd.at[now], kd.at[now])
+    split(tall, hf, su.at[now], ku.at[now])
+    @pl.when(step >= slots)
+    def _():
+        pl.semaphore_wait(free, 1)
+    for c in swaps(step):
+        c.start()
+    @pl.when(step >= 1)
+    def _():
+        finish(step - 1)
+
+    @pl.when(step == steps - 1)
+    def _():
+        db_ref[...] = jnp.zeros_like(db_ref)
+        def fn(f, rows):
+            gf = g[rows, :].astype(F32)
+            d = down[rows, :] + bd_ref[...]
+            m = mixed[rows, :]
+            ghf = gh[rows, :]
+            inv = st[rows, 128:129]
+            n = (m - st[rows, 0:1]) * inv
+            t = ghf * (1.0 + mod_ref[f, 4:5, :])
+            back = t - jnp.mean(t, axis=1, keepdims=True) - n * jnp.mean(t * n, axis=1, keepdims=True)
+            gm = gf + inv * back
+            gbr = (gm * mod_ref[f, 2:3, :]).astype(B16)
+            s = lambda v: jnp.sum(v, axis=0, keepdims=True)
+            sums_ref[f] = jnp.concatenate([s(gm * branch[rows, :]), s(ghf), s(ghf * n), s(gf * d)], axis=0)
+            db_ref[...] += jnp.concatenate([s(gbr.astype(F32)), s(gd[rows, :].astype(F32))], axis=0)
+            mixed[rows, :] = gm
+            h[rows, :] = gbr
+            gd[rows, :] = (m + mod_ref[f, 5:6, :] * d).astype(B16)
+        group = plane.size
+        per_call = clips // calls
+        def go_copies():
+            out = []
+            for k in range(1, group):
+                p, f, r = plane.peer(k)
+                out.append(remote(gav.at[p], go_out.at[plane.f, plane.r], gs.at[k], gr.at[k], {"frame": f, "row": r}))
+            return out, pltpu.make_async_copy(gav.at[plane.me], go_out.at[plane.f, plane.r], gl)
+        def back_out(c):
+            each(c * frames // clips, (c + 1) * frames // clips, fn)
+            ga = dot(h[c * count:(c + 1) * count, :], wo_ref[...], NT).astype(B16)
+            for i in range(hg):
+                gav[c * hg + i] = ga[:, i * lw:(i + 1) * lw]
+        for c in range(per_call):
+            back_out(c)
+        copies, own = go_copies()
+        for c in copies:
+            c.start()
+        own.start()
+        for c in range(per_call, clips):
+            back_out(c)
+        outs = [pltpu.make_async_copy(gd, y_out, oo.at[0]), pltpu.make_async_copy(mixed, gm_out, oo.at[1])]
+        if calls > 1:
+            outs.append(pltpu.make_async_copy(gav.at[pl.ds(group, (calls - 1) * group)], ga_out, oo.at[2]))
+        for c in outs:
+            c.start()
+        finish(step)
+        pl.semaphore_signal(done, inc=1, device_id=partner, device_id_type=MESH)
+        wide_out = dot(an[:clips * count, :], h[...], TN)
+        for b in range(2):
+            @pl.when(bit == b)
+            def _():
+                an[:width, :hw] = wide_out[:, (1 - b) * hw:(2 - b) * hw].astype(B16)
+                down[:width, :hw] = wide_out[:, b * hw:(b + 1) * hw]
+        pl.semaphore_wait(done, 1)
+        ro = g.at[pl.ds(0, width), pl.ds(0, hw)]
+        last = remote(an.at[pl.ds(0, width), pl.ds(0, hw)], ro, pair.at[0, 2], pair.at[1, slots], partner)
+        last.start()
+        last.wait()
+        an[:width, hw:] = (down[:width, :hw] + g[:width, :hw].astype(F32)).astype(B16)
+        outs.append(pltpu.make_async_copy(an.at[pl.ds(0, width), pl.ds(hw, hw)], po_out, oo.at[3]))
+        outs[-1].start()
+        for c in copies:
+            c.wait()
+        own.wait()
+        for c in swaps(step - 1) + swaps(step):
+            c.wait_send()
+        for c in stores(step - 1) + stores(step):
+            c.wait()
+        for c in outs:
+            c.wait()
+
+
+def mlp(attn, x, g, mods, w_out, b_out, w_up, b_up, w_down, b_down, calls, lead):
+    clips, hg, count, lw = attn.shape
+    rows, width = x.shape
+    ff = w_up.shape[1]
+    frames = mods.shape[0]
+    fc = min(512, ff)
+    hw, hf = width // 2, fc // 2
+    nf, nr = lead[:2]
+    group = nf * nr
+    slots = 3
+    tall = max(rows, width)
+    whole = lambda *shape: pl.BlockSpec(shape, lambda j: (0,) * len(shape), pipeline_mode=pl.Buffered(1))
+    keep = lambda *shape: pl.BlockSpec(shape, lambda j: (0,) * len(shape))
+    hbm = pl.BlockSpec(memory_space=pl.ANY)
+    s, v, dma = jax.ShapeDtypeStruct, pltpu.VMEM, pltpu.SemaphoreType.DMA
+    return pl.pallas_call(
+        functools.partial(mlp_kernel, calls=calls),
+        grid=(ff // fc,),
+        in_specs=[whole(clips, hg, count, lw), hbm, hbm, whole(frames, 6, width), whole(width, width), whole(1, width),
+                  pl.BlockSpec((width, fc), lambda j: (0, j)), pl.BlockSpec((1, fc), lambda j: (0, j)),
+                  pl.BlockSpec((fc, width), lambda j: (j, 0)), whole(1, width)],
+        out_specs=[hbm] * 7 + [keep(frames, 4, width), pl.BlockSpec((1, fc), lambda j: (0, j)), keep(2, width)],
+        out_shape=[s((rows, width), B16), s((rows, width), F32), s((max(1, calls - 1) * group, count, lw), B16),
+                   s((nf, nr, count, lw), B16), s((ff, hw), B16), s((width, ff // 2), B16), s((width, hw), B16),
+                   s((frames, 4, width), F32), s((1, ff), F32), s((2, width), F32)],
+        scratch_shapes=[v((tall, width), B16), v((tall, width), B16), v((rows, width), F32), v((rows, width), F32),
+                        v((rows, width), B16), v((rows, width), B16), v((tall, width), F32), v((rows, width), F32), v((rows, 256), F32),
+                        v((clips * hg, count, lw), B16), v((2, fc, hw), B16), v((2, width, hf), B16), v((slots, fc, hw), B16),
+                        v((slots, width, hf), B16), v((2, fc, hw), F32), v((2, width, hf), F32), v((2, fc, hw), B16), v((2, width, hf), B16),
+                        dma((2,)), dma((2, 2)), dma((4, slots + 1)), pltpu.SemaphoreType.REGULAR, pltpu.SemaphoreType.REGULAR,
+                        dma((group,)), dma((group,)), dma, dma((4,))],
+        compiler_params=pltpu.CompilerParams(vmem_limit_bytes=63 << 20, dimension_semantics=("arbitrary",), collective_id=3, has_side_effects=True),
+        cost_estimate=pl.CostEstimate(flops=2 * rows * width * (3 * width + 6 * ff), bytes_accessed=8 * width * ff + 20 * rows * width, transcendentals=rows * ff),
+        name="mlp",
+    )(attn, x, g, mods, w_out, b_out, w_up, b_up, w_down, b_down)
+
+
+def tail_kernel(gp_hbm, h_hbm, w_hbm, x_hbm, gm_hbm, mod_ref, clean_ref, sums2_ref, vec_ref,
+                o_out, gw_ref, noise_ref, vec_out,
+                gp, h, w, x, gm, full, gh, send, got, part, s1s, dbq, nsend, nrecv, vsend, v1, vmid, v2, io, pair, nsem, vsem, oo, *scratch, jobs):
+    plane = Plane()
+    clips, hg, count, w3 = gp_hbm.shape
+    lw = w3 // 3
+    width = w.shape[0]
+    frames = mod_ref.shape[0] // clips
+    pt = count // frames
+    nc, nf, nr = lax.axis_size("clip"), plane.nf, plane.nr
+    group = plane.size
+    bit = lax.rem(plane.r, 2)
+    partner = {"row": plane.r + 1 - 2 * bit}
+    packed = max(1, 128 * 3 // w3)
+    blocks = hg // 2 // packed
+    bw = packed * w3
+    loads = [pltpu.make_async_copy(gp_hbm, gp, io.at[0]), pltpu.make_async_copy(h_hbm, h, io.at[1]),
+             pltpu.make_async_copy(w_hbm, w, io.at[2]), pltpu.make_async_copy(x_hbm, x, io.at[3]), pltpu.make_async_copy(gm_hbm, gm, io.at[4])]
+    for c in loads:
+        c.start()
+    sums = make_sums(plane, jobs, [part], [gw_ref], scratch)
+    greet(plane, True)
+    for c in loads[:2]:
+        c.wait()
+
+    def outer(j):
+        total = None
+        for c in range(clips):
+            b = jnp.concatenate([gp[c, j * packed + i] for i in range(packed)], axis=1)
+            t = dot(h[c], b, TN)
+            total = t if total is None else total + t
+        return total
+
+    def swap(j):
+        return remote(send.at[j], got.at[j], pair.at[0, j], pair.at[1, j], partner)
+    other = 1 - bit
+    for j in range(blocks):
+        send[j] = outer(other * blocks + j).astype(B16)
+        swap(j).start()
+    for s, (_, plane_first, first, cols) in zip(sums, jobs):
+        j = first // bw
+        total = outer(bit * blocks + j)
+        swap(j).wait_recv()
+        total = (total + got[j].astype(F32)).astype(B16)
+        part[:, :, :, first:first + cols] = total.reshape(part.shape[:3] + (cols,))
+        s.start(1)
+
+    for c in loads[2:]:
+        c.wait()
+    dbq[...] = jnp.zeros_like(dbq)
+    for c in range(clips):
+        for j in range(3):
+            for g in range(hg):
+                full[:, j * width + g * lw:j * width + (g + 1) * lw] = gp[c, g, :, j * lw:(j + 1) * lw]
+        gh[...] = dot(full[...], w[...], NT)
+        dbq[...] += jnp.sum(full[...].astype(F32), axis=0, keepdims=True)
+        def one(f, _):
+            rows = pl.ds(pl.multiple_of(f * pt, pt), pt)
+            cf = c * frames + f
+            n, inv = stats(x[c, rows, :].astype(F32))
+            ghf = gh[rows, :]
+            t = ghf * (1.0 + mod_ref[cf, 1:2, :])
+            back = t - jnp.mean(t, axis=1, keepdims=True) - n * jnp.mean(t * n, axis=1, keepdims=True)
+            gm[c, rows, :] = gm[c, rows, :] + inv * back
+            s = lambda v: jnp.sum(v, axis=0, keepdims=True)
+            s1s[cf, 0:2, :] = jnp.concatenate([s(ghf), s(ghf * n)], axis=0)
+            s1s[cf, 2:6, :] = sums2_ref[cf]
+            return 0
+        lax.fori_loop(0, frames, one, 0)
+        pltpu.make_async_copy(gm.at[c], o_out.at[c], oo.at[c]).start()
+        for s in (sums[1:2] if c < clips - 1 else sums[2 if clips > 1 else 1:3]):
+            s.wait(1)
+            s.middle()
+
+    quarter = width // nr
+    vsend[...] = jnp.zeros_like(vsend)
+    def gather(cf, total):
+        both = s1s[cf, 0:6, :]
+        keep = clean_ref[cf]
+        noise = jnp.where(keep > 0.5, jnp.zeros_like(both), both)
+        for q in range(nr):
+            nsend[q, cf] = noise[:, q * quarter:(q + 1) * quarter].astype(B16)
+        return total + (both - noise)
+    clean_sum = lax.fori_loop(0, clips * frames, gather, jnp.zeros((6, width), F32))
+    def ncopies():
+        out = []
+        for k in range(1, nr):
+            q = lax.rem(plane.r + k, nr)
+            out.append(remote(nsend.at[q], nrecv.at[plane.r], nsem.at[0, k], nsem.at[1, k], {"row": q}))
+        return out
+    for c in ncopies():
+        c.start()
+    vsend[:6, :] = clean_sum
+    vsend[6:9, :] = jnp.concatenate([dbq[:, j * width:(j + 1) * width] for j in range(3)], axis=0)
+    vsend[9:9 + vec_ref.shape[0], :] = vec_ref[...]
+    def vcopies(stage):
+        out = []
+        if stage == 1:
+            for k in range(1, group):
+                p, f, r = plane.peer(k)
+                out.append(remote(vsend, v1.at[plane.me], vsem.at[0, k], vsem.at[1, k], {"frame": f, "row": r}))
+        else:
+            c = lax.axis_index("clip")
+            for k in range(1, nc):
+                out.append(remote(vmid, v2.at[c], vsem.at[0, group + k], vsem.at[1, group + k], {"clip": lax.rem(c + k, nc)}))
+        return out
+    for c in vcopies(1):
+        c.start()
+    for s in sums[:1] + sums[3:]:
+        s.wait(1)
+        s.middle()
+    for c in vcopies(1):
+        c.wait()
+    total = vsend[...]
+    for k in range(1, group):
+        p, _, _ = plane.peer(k)
+        total = total + v1[p]
+    vmid[...] = total
+    for c in vcopies(2):
+        c.start()
+    for c in ncopies():
+        c.wait()
+    def add_noise(cf, _):
+        total = nsend[plane.r, cf].astype(F32)
+        for k in range(1, nr):
+            total = total + nrecv[lax.rem(plane.r + k, nr), cf].astype(F32)
+        noise_ref[cf] = total
+        return 0
+    lax.fori_loop(0, clips * frames, add_noise, 0)
+    for s in sums:
+        s.wait(2)
+        s.last()
+    for c in vcopies(2):
+        c.wait()
+    total = vmid[...]
+    for k in range(1, nc):
+        total = total + v2[lax.rem(lax.axis_index("clip") + k, nc)]
+    vec_out[...] = total
+    for s in sums:
+        s.close()
+    for j in range(blocks):
+        swap(j).wait_send()
+    for c in range(clips):
+        pltpu.make_async_copy(gm.at[c], o_out.at[c], oo.at[c]).wait()
+
+
+def tail(gproj, h1, w_qkv, x, gmixed, mods, clean, sums2, vec):
+    clips, hg, count, w3 = gproj.shape
+    lw = w3 // 3
+    width = x.shape[2]
+    nc, nf, nr = (lax.axis_size(a) for a in ALL)
+    group = nf * nr
+    frames = mods.shape[0]
+    two = width // (nc * nf * nr // 2)
+    packed = max(1, 128 * 3 // w3)
+    blocks, bw = hg // 2 // packed, packed * w3
+    vrows = -(-(9 + vec.shape[0]) // 8) * 8
+    hbm, vmem = pl.BlockSpec(memory_space=pl.ANY), pl.BlockSpec(memory_space=pltpu.VMEM)
+    s, v, dma = jax.ShapeDtypeStruct, pltpu.VMEM, pltpu.SemaphoreType.DMA
+    shape = jax.ShapeDtypeStruct((nc, nf * nr // 2, two, blocks * bw), B16)
+    order = [(False if j == 0 else True, j * bw, bw) for j in range(blocks)]
+    scratch, outs, jobs = sum_plan([shape], [order])
+    return pl.pallas_call(
+        functools.partial(tail_kernel, jobs=jobs),
+        in_specs=[hbm] * 5 + [vmem] * 4,
+        out_specs=[hbm, vmem, vmem, vmem],
+        out_shape=[s((clips, count, width), F32)] + outs + [s((frames, 6, width // nr), F32), s((vrows, width), F32)],
+        scratch_shapes=[v((clips, hg, count, w3), B16), v((clips, count, width), B16), v((width, 3 * width), B16), v((clips, count, width), B16),
+                        v((clips, count, width), F32), v((count, 3 * width), B16), v((count, width), F32), v((blocks, width, bw), B16),
+                        v((blocks, width, bw), B16), v(shape.shape, B16), v((frames, 8, width), F32), v((1, 3 * width), F32),
+                        v((nr, frames, 6, width // nr), B16), v((nr, frames, 6, width // nr), B16), v((vrows, width), F32), v((group, vrows, width), F32),
+                        v((vrows, width), F32), v((nc, vrows, width), F32), dma((5,)), dma((2, blocks)), dma((2, nr)), dma((2, group + nc)), dma((clips,))] + scratch,
+        compiler_params=pltpu.CompilerParams(vmem_limit_bytes=62 << 20, collective_id=2, has_side_effects=True),
+        cost_estimate=pl.CostEstimate(flops=12 * clips * count * width * width, bytes_accessed=40 * clips * count * width, transcendentals=0),
+        name="tail",
+    )(gproj, h1, w_qkv, x, gmixed, mods, clean, sums2, vec)
 
 
 def on_device(tokens, context, noise_mod, clean_mod, w_qkv, b_qkv, w_out, b_out, w_up, b_up, w_down, b_down, cotangent):
@@ -853,60 +1034,41 @@
     row_of = lambda v: v.reshape(1, -1)
 
     lead = (nf, nr, frames, patches)
-    h1, sends = [], []
-    for c in range(clips):
-        o, h = qkv_forward(inputs[c], mods[c], w_qkv, row_of(b_qkv), cos_l, sin_l, hg, lw)
-        sends.append(o)
-        h1.append(h)
-    by_call = lambda v, w: [jnp.concatenate(v[i * cs:(i + 1) * cs], axis=0).reshape(group, frames, patches, w) for i in range(calls)]
-    x, attn, ot, lse = attention_forward(by_call(sends, 3 * lw), lead, lw)
+    sends, h1 = qkv_forward(inputs, mods, w_qkv, row_of(b_qkv), cos_l, sin_l, hg, lw)
+    x, attn, ot, lse = attention_forward(sends.reshape(calls, group, frames, patches, 3 * lw), lead, lw)
     attn = attn.reshape(clips, hg, count, lw)
 
-    outs = [mlp(c, attn, inputs[c], cots[c], mods[c], w_out, row_of(b_out), w_up, row_of(b_up), w_down, row_of(b_down))
-            for c in range(clips)]
-    y, gmixed, gattn, gbranch, attn_n, h2, gdown, act, gpre, sums2, db_up, db_two = zip(*outs)
-    gattn = by_call(gattn, lw)
-    go = exchange(gattn[0]).reshape(lead + (lw,))
-
-    mine = jnp.reshape(ri % 2, (1,)).astype(jnp.int32)
+    rows = clips * count
+    by_frame = mods.reshape(clips * frames, 6, width)
+    y, gmixed, ga, go, part_down, part_up, part_out, sums2, db_up, db_two = mlp(
+        attn, inputs.reshape(rows, width), cots.reshape(rows, width), by_frame,
+        w_out, row_of(b_out), w_up, row_of(b_up), w_down, row_of(b_down), calls, lead)
+    go = go.reshape(lead + (lw,))
+    go_sends = [v for v in ga.reshape((-1, group, frames, patches, lw))][:calls - 1]
+    gmixed = gmixed.reshape(clips, count, width)
+
     nc = lax.axis_size("clip")
-    def summed(*pairs):
-        got = [swap(outer(a, b, 1 - mine), "row", 1) for a, b in pairs]
-        parts = [outer(a, b, mine, g) for (a, b), g in zip(pairs, got)]
-        return [p.reshape(nc, nf * nr // 2, p.shape[0] // (nc * nf * nr // 2), p.shape[1]) for p in parts]
-    parts = summed((act, gdown), (h2, gpre), (attn_n, gbranch))
-    orders = [[(True, 0, parts[0].shape[3])], [(False, 0, parts[1].shape[3])], [(True, 0, parts[2].shape[3])]]
-    gproj, gw_down, gw_up, gw_out = attention_backward(x, go, gattn[1:], ot, lse, cos_t, sin_t, parts, orders)
+    as_blocks = lambda p: p.reshape(nc, nf * nr // 2, p.shape[0] // (nc * nf * nr // 2), p.shape[1])
+    parts = [as_blocks(p) for p in (part_down, part_up, part_out)]
+    orders = [[(True, 0, parts[0].shape[3])], [(False, 0, parts[1].shape[3])], [(False, 0, parts[2].shape[3])]]
+    gproj, gw_down, gw_up, gw_out = attention_backward(x, go, go_sends, ot, lse, cos_t, sin_t, parts, orders)
     gproj = gproj.reshape(clips, hg, count, 3 * lw)
-    backs = [qkv_back(c, gproj, inputs[c], gmixed[c], mods[c], w_qkv) for c in range(clips)]
-    gtokens, sums1, db_qkv = zip(*backs)
-    parts = summed((h1, gproj))
-    ch = parts[0].shape[3]
-    gw_qkv, = scatter_sums(parts, [[(True, 0, 3 * ch // 4), (False, 3 * ch // 4, ch // 4)]], 2)
+    fc = min(512, w_up.shape[1])
+    gw_up = gw_up.reshape(gw_up.shape[0], 2, -1, fc // 2).transpose(0, 2, 1, 3).reshape(gw_up.shape[0], -1)
+    clean = jnp.broadcast_to(is_clean.reshape(-1, 1, 1), (clips * frames, 1, width)).astype(F32)
+    vec = jnp.concatenate([db_up.reshape(-1, width), db_two], axis=0)
+    gtokens, gw_qkv, noise, vec = tail(gproj, h1, w_qkv, inputs, gmixed, by_frame, clean, sums2, vec)
     per = gw_qkv.shape[0]
     gw_qkv = gw_qkv.reshape(per, 2, hg // 2, 3, lw).transpose(0, 3, 1, 2, 4).reshape(per, 3 * width)
-
-    gmods = jnp.stack([jnp.concatenate([sums1[c], sums2[c]], axis=1) for c in range(clips)], axis=0)
-    clean = is_clean[:, :, None, None]
-    noise_part = jnp.where(clean, 0.0, gmods).transpose(1, 0, 2, 3).astype(B16)
-    quarter = width // nr
-    sent = noise_part.reshape(frames, clips, 6, nr, quarter).transpose(3, 0, 1, 2, 4)
-    grad_noise = jnp.sum(exchange(sent, "row").astype(F32), axis=0)
-    clean_part = jnp.sum(jnp.where(clean, gmods, 0.0), axis=(0, 1))
+    grad_noise = noise.reshape(clips, frames, 6, -1).transpose(1, 0, 2, 3)
     total = lax.axis_size(ALL)
-    two = sum(db_two[1:], db_two[0])
-    small = jnp.concatenate(
-        [v.reshape(total, -1) for v in (sum(db_qkv[1:], db_qkv[0]), two[0], sum(db_up[1:], db_up[0]), two[1])]
-        + [clean_part.reshape(6, total, -1).transpose(1, 0, 2).reshape(total, -1)], axis=1)
-    small = jnp.sum(exchange(small, ALL), axis=0)
-    ends = []
-    at = 0
-    for size in (3 * width, width, w_up.shape[1], width):
-        ends.append(small[at:at + size // total])
-        at += size // total
-    gb_qkv, gb_out, gb_up, gb_down = ends
-    grad_clean = small[at:].reshape(6, -1)
-    back = lambda v: jnp.stack(v, axis=0).reshape(full).transpose(1, 2, 0, 3)
+    place = lax.axis_index(ALL)
+    def own(at, size):
+        return lax.dynamic_slice_in_dim(vec[at:at + size].reshape(-1), place * (size * width // total), size * width // total)
+    grad_clean = lax.dynamic_slice_in_dim(vec[:6], place * (width // total), width // total, 1)
+    ff = w_up.shape[1] // width
+    gb_qkv, gb_up, gb_out, gb_down = own(6, 3), own(9, ff), own(9 + ff, 1), own(10 + ff, 1)
+    back = lambda v: v.reshape(full).transpose(1, 2, 0, 3)
     return (back(y), back(gtokens), grad_noise, grad_clean, gw_qkv, gb_qkv, gw_out, gb_out, gw_up, gb_up, gw_down, gb_down)
 
 

time: 561 us -> 487 us (0.87)
  local copies, waits for them, and re-layouts: 49.4 us -> 24.5 us
  Pallas kernels: 472 us -> 448 us
  starting transfers between devices: 15.2 us -> 0 us
  other arithmetic: 17 us -> 6.46 us
    unnamed x106 -> x33, local copies, waits for them, and re-layouts: 29.5 us -> 2.73 us
    pallas_call x15 -> x3, Pallas kernels: 201 us -> 174 us  [the longest x1 93.3 us: mlp(): pl.pallas_call(functools.partial(mlp_kernel, calls=calls), grid=(ff // fc...]
    all_to_all x3 -> x0, starting transfers between devices: 14 us -> none  [exchange(): return lax.all_to_all(blocks, axes, 0, 0, tiled=True)]
    another operation x6 -> x0, local copies, waits for them, and re-layouts: 12.2 us -> none  [the longest x4 12 us: on_device(): back = lambda v: jnp.stack(v, axis=0).reshape(full).transpose(1, 2, 0, 3)]
    reshape x5 -> x6, local copies, waits for them, and re-layouts: 1.06 us -> 12.9 us  [the longest x2 11 us: on_device(): back = lambda v: v.reshape(full).transpose(1, 2, 0, 3)]
    transpose x2 -> x0, other arithmetic: 11.3 us -> none  [on_device(): back = lambda v: jnp.stack(v, axis=0).reshape(full).transpose(1, 2, 0, 3)]
  transfers between devices with their start and end apart: 7 -> 0, of which waited for: 1 -> 0; matrix products, arithmetic and copies ran while one was open for 6% -> 0% of each run, Pallas kernels for 9% -> 0%
where the time goes in v3:
time: 487 us; the launch traced here: 480 us
  Pallas kernels  448 us (92%)
  local copies, waits for them, and re-layouts  24.5 us (5%)
  other arithmetic  6.46 us (1%)
    pallas_call x1, Pallas kernels, attention_backward(): pl.pallas_call(functools.partial(bwd_all_kernel, calls=calls, count=len(p...  163 us
    pallas_call x1, Pallas kernels, attention_forward(): pl.pallas_call(functools.partial(fwd_all_kernel, calls=calls), in_specs=[...  111 us
    pallas_call x1, Pallas kernels, mlp(): pl.pallas_call(functools.partial(mlp_kernel, calls=calls), grid=(ff // fc...  93.3 us
    pallas_call x1, Pallas kernels, tail(): pl.pallas_call(functools.partial(tail_kernel, jobs=jobs), in_specs=[hbm]...  65.2 us
    pallas_call x1, Pallas kernels, qkv_forward(): pl.pallas_call(qkv_kernel, grid=(clips,), in_specs=[one(count, width), on...  15.5 us
    reshape x2, local copies, waits for them, and re-layouts, on_device(): back = lambda v: v.reshape(full).transpose(1, 2, 0, 3)  11 us

profile of v3, /device:TPU:1, one launch (start us, length us, event | category | flops | bytes accessed | tf_op | source)
XLA Modules:
  0.0 480.1 jit_solution(14223858336280576599)
XLA Ops:
  1.4 0.7 fusion.36
  2.2 1.1 bitcast_select_fusion.mod_ref
  3.3 0.6 copy.44
  4.0 15.5 %qkv.1 = (bf16[2,8,512,384]{3,2,1,0:T(8,128)(2,1)}, bf16[2,512,1024]{2,1,0:T(8,128)(2,1)S(1)}) custom-call(bf16[2,512,1024]{2,1,0:T(8,128)(2,1)S(1)} %bitcast.50, f32[2,8,6,1024]{3,2,1,0:T(8,128)S(1)} %bitcast_select_fusion.mod_ref, bf16[1024,3072]{1,0:T(8,128)(2,1)} %w_hbm.3, f32[1,3072]{1,0:T(1,128)S(1)} %bitcast.55, f32[512,128]{1,0:T(8,128)S(1)} %copy.46.cos_ref, ...), custom_call_target="tpu_custom_call" | custom-call | flops 6442450944 | bytes 16777216 | tf_op jit(solution)/shard_map/qkv/pallas_call | solution.py:278
  19.5 110.6 %attention_forward.1 = (bf16[2,2,4,8,64,384]{5,4,3,2,1,0:T(8,128)(2,1)}, bf16[2,8,8,64,128]{4,3,2,1,0:T(8,128)(2,1)}, f32[2,128,4096]{2,1,0:T(8,128)}, f32[2,2,4096]{2,1,0:T(2,128)}) custom-call(bf16[2,8,8,64,384]{4,3,2,1,0:T(8,128)(2,1)} %bitcast.75), custom_call_target="tpu_custom_call" | custom-call | flops 8589934592 | bytes 25165824 | tf_op jit(solution)/shard_map/attention_forward/pallas_call | solution.py:395
  130.2 2.0 copy.49
  132.1 93.3 %mlp.1 = (bf16[1024,1024]{1,0:T(8,128)(2,1)}, f32[1024,1024]{1,0:T(8,128)}, bf16[8,512,128]{2,1,0:T(8,128)(2,1)}, bf16[2,4,512,128]{3,2,1,0:T(8,128)(2,1)}, bf16...) custom-call(bf16[2,8,512,128]{3,2,1,0:T(8,128)(2,1)} %bitcast.79, ...), custom_call_target="tpu_custom_call" | custom-call | flops 57982058496 | bytes 54525952 | tf_op jit(solution)/shard_map/mlp/pallas_call | solution.py:807
  225.5 2.9 fusion
  228.4 163.2 %attention_backward.1 = (bf16[2,8,8,64,384]{4,3,2,1,0:T(8,128)(2,1)}, f32[128,1024]{1,0:T(8,128)}, f32[32,4096]{1,0:T(8,128)}, f32[32,1024]{1,0:T(8,128)}) custom-call(bf16[2,2,4,8,64,384]{5,4,3,2,1,0:T(8,128)(2,1)} %get-tuple-element.39.refs_0_, bf16[2,4,8,64,128]{4,3,2,1,0:T(8,128)(2,1)} %bitcast.81, f32[2,128,4096]{2,1,0:T(8,128)} %get-tuple-element.41.refs_2_, ...), custom_call_target="tpu_custom_call" | custom-call | flops 21474836480 | bytes 50331648 | tf_op jit(solution)/shard_map/attention_backward/pallas_call | solution.py:584
  392.1 0.7 reduce.3
  392.8 0.6 pad_maximum_fusion.2.vec_ref
  393.5 0.7 broadcast_in_dim.139.clean_ref
  394.2 65.2 %tail.1 = (f32[2,512,1024]{2,1,0:T(8,128)}, f32[32,3072]{1,0:T(8,128)}, f32[16,6,256]{2,1,0:T(8,128)}, f32[16,1024]{1,0:T(8,128)}) custom-call(bf16[2,8,512,384]{3,2,1,0:T(8,128)(2,1)} %bitcast.74, bf16[2,512,1024]{2,1,0:T(8,128)(2,1)} %copy-done.3, bf16[1024,3072]{1,0:T(8,128)(2,1)} %w_hbm.3, bf16[2,512,1024]{2,1,0:T(8,128)(2,1)} %bitcast.52, ...), custom_call_target="tpu_custom_call" | custom-call | flops 12884901888 | bytes 41943040 | tf_op jit(solution)/shard_map/tail/pallas_call | solution.py:991
  459.5 7.5 %copy.62 = f32[2,8,64,1024]{3,0,2,1:T(2,128)} copy(f32[2,8,64,1024]{3,2,1,0:T(8,128)} %bitcast.57) | data formatting | bytes 8388608 | tf_op jit(solution)/shard_map/reshape | solution.py:1071
  467.4 0.9 reshape.319
  468.3 0.7 copy.64
  469.0 0.7 constant_dynamic-slice_fusion.2
  470.3 0.6 dynamic_slice.20
  470.9 0.6 fusion.27
  472.1 1.2 copy.55
  473.5 1.2 reshape.322
  474.8 3.5 copy.63
  478.2 0.7 copy.68
  478.9 0.8 copy.69
  (56 shorter events, 3.2 us)
Async XLA Ops:
  0.6 2.7 copy-start.4
  0.7 3.3 copy-start.2
  3.3 16.2 %copy-start.1 = (f32[2,8,6,1024]{3,2,1,0:T(8,128)}, f32[2,8,6,1024]{3,2,1,0:T(8,128)S(1)}, u32[]{:S(2)}) copy-start(f32[2,8,6,1024]{3,2,1,0:T(8,128)S(1)} %bitcast_select_fusion.mod_ref) | copy-start | bytes 1179652
  4.0 15.5 %copy-start = (bf16[2,8,64,1024]{3,2,1,0:T(8,128)(2,1)}, bf16[2,8,64,1024]{3,2,1,0:T(8,128)(2,1)S(1)}, u32[]{:S(2)}) copy-start(bf16[2,8,64,1024]{3,2,1,0:T(8,128)(2,1)S(1)} %copy.44) | copy-start | bytes 6291460
  19.5 110.7 %copy-start.3 = (bf16[2,512,1024]{2,1,0:T(8,128)(2,1)}, bf16[2,512,1024]{2,1,0:T(8,128)(2,1)S(1)}, u32[]{:S(2)}) copy-start(bf16[2,512,1024]{2,1,0:T(8,128)(2,1)S(1)} %get-tuple-element.48.h_hbm) | copy-start | bytes 6291460
  19.5 110.7 %copy-start.5 = (bf16[8,64,2,1024]{3,2,1,0:T(2,128)(2,1)S(1)}, bf16[8,64,2,1024]{3,2,1,0:T(2,128)(2,1)}, u32[]{:S(2)}) copy-start(bf16[8,64,2,1024]{3,2,1,0:T(2,128)(2,1)} %param.25) | copy-start | bytes 6291460
  228.4 163.7 %copy-start.12 = (f32[1,4096]{1,0:T(1,128)S(1)}, f32[1,4096]{1,0:T(1,128)}, u32[]{:S(2)}) copy-start(f32[1,4096]{1,0:T(1,128)} %get-tuple-element.51) | copy-start | bytes 49156
  228.4 164.4 %copy-start.13 = (f32[2,1024]{1,0:T(2,128)S(1)}, f32[2,1024]{1,0:T(2,128)}, u32[]{:S(2)}) copy-start(f32[2,1024]{1,0:T(2,128)} %get-tuple-element.52) | copy-start | bytes 24580
  459.4 7.5 %copy-start.8 = (f32[32,3072]{1,0:T(8,128)S(1)}, f32[32,3072]{1,0:T(8,128)}, u32[]{:S(2)}) copy-start(f32[32,3072]{1,0:T(8,128)} %get-tuple-element.56) | copy-start | bytes 1179652
  459.4 8.8 %copy-start.9 = (f32[16,6,256]{2,1,0:T(8,128)S(1)}, f32[16,6,256]{2,1,0:T(8,128)}, u32[]{:S(2)}) copy-start(f32[16,6,256]{2,1,0:T(8,128)} %get-tuple-element.54) | copy-start | bytes 294916
  459.4 9.5 %copy-start.11 = (f32[16,1024]{1,0:T(8,128)S(1)}, f32[16,1024]{1,0:T(8,128)}, u32[]{:S(2)}) copy-start(f32[16,1024]{1,0:T(8,128)} %get-tuple-element.55) | copy-start | bytes 196612
  467.0 7.8 %copy-start.6 = (bf16[1024,1024]{1,0:T(8,128)(2,1)S(1)}, bf16[1024,1024]{1,0:T(8,128)(2,1)}, u32[]{:S(2)}) copy-start(bf16[1024,1024]{1,0:T(8,128)(2,1)} %get-tuple-element.38) | copy-start | bytes 6291460
  467.4 10.9 %copy-start.10 = (f32[32,1024]{1,0:T(8,128)S(1)}, f32[32,1024]{1,0:T(8,128)}, u32[]{:S(2)}) copy-start(f32[32,1024]{1,0:T(8,128)} %get-tuple-element.93) | copy-start | bytes 393220
  468.3 10.6 %copy-start.7 = (f32[128,1024]{1,0:T(8,128)S(1)}, f32[128,1024]{1,0:T(8,128)}, u32[]{:S(2)}) copy-start(f32[128,1024]{1,0:T(8,128)} %get-tuple-element.97) | copy-start | bytes 1572868

commit v4 on v3

--- a/solution.py
+++ b/solution.py
@@ -17,7 +17,7 @@
     return jnp.where(lane // HD == head, values, jnp.zeros_like(values))
 
 
-def flash_forward(x_ref, o_ref, ot_ref, lse_ref, qm, kf, vt, sb, acc, mrow, done):
+def flash_forward(x_ref, o_ref, ot_ref, lse_ref, qm, kf, vt, sa, sb, acc, ma, mb, done):
     nf, nr, fl, pt, width = x_ref.shape
     lw = width // 3
     nh = lw // HD
@@ -48,8 +48,8 @@
             ncols = pl.ds(n0, blk)
             s0 = dot(kf[pl.ds(n0, tok), :], qm[nhd, ncols, :], NT)
             s1 = dot(kf[pl.ds(n1, tok), :], qm[nhd, pl.ds(n1, tok), :], NT)
-            sb[ns, pl.ds(n0, tok), :] = s0
-            sb[ns, pl.ds(n1, tok), tok:] = s1
+            (sa, sb)[ns][pl.ds(n0, tok), :] = s0
+            (sa, sb)[ns][pl.ds(n1, tok), tok:] = s1
             m0 = fold(s0, jnp.max)
             mm = jnp.concatenate([m0[:, :tok], jnp.maximum(m0[:, tok:], fold(s1, jnp.max))], axis=1)
         else:
@@ -59,9 +59,9 @@
             hs = slice(chd * HD, (chd + 1) * HD)
             c0 = pl.multiple_of(ca * blk, blk)
             c1 = pl.multiple_of(ca * blk + tok, tok)
-            m = mrow[cs]
-            p0 = jnp.exp(sb[cs, pl.ds(c0, tok), :] - m)
-            p1 = jnp.exp(sb[cs, pl.ds(c1, tok), tok:] - m[:, tok:])
+            m = (ma, mb)[cs][...]
+            p0 = jnp.exp((sa, sb)[cs][pl.ds(c0, tok), :] - m)
+            p1 = jnp.exp((sa, sb)[cs][pl.ds(c1, tok), tok:] - m[:, tok:])
             l0 = fold(p0, jnp.sum)
             ll = jnp.concatenate([l0[:, :tok], l0[:, tok:] + fold(p1, jnp.sum)], axis=1)
             a0 = dot(vt[hs, pl.ds(c0, tok)], p0.astype(jnp.bfloat16), NN)
@@ -73,7 +73,7 @@
         def score(b, mm):
             rows = pl.ds(pl.multiple_of(b * blk, blk), blk)
             s = dot(kf[rows, :], qm[nhd, ncols, :], NT)
-            sb[ns, rows, :] = s
+            (sa, sb)[ns][rows, :] = s
             return jnp.maximum(mm, fold(s, jnp.max))
         def body(b, carry):
             mm, ll = carry
@@ -81,7 +81,7 @@
                 mm = score(b, mm)
             if cur is not None:
                 rows = pl.ds(pl.multiple_of(b * blk, blk), blk)
-                p = jnp.exp(sb[cs, rows, :] - m)
+                p = jnp.exp((sa, sb)[cs][rows, :] - m)
                 ll = ll + fold(p, jnp.sum)
                 acc[hs, :] += dot(vt[hs, rows], p.astype(jnp.bfloat16), NN)
             return mm, ll
@@ -90,7 +90,7 @@
         if grow and nxt is not None:
             mm = score(cur[0], mm)
         if nxt is not None:
-            mrow[ns] = jnp.max(mm, axis=0, keepdims=True)
+            (ma, mb)[ns][...] = jnp.max(mm, axis=0, keepdims=True)
         if cur is not None:
             l = jnp.sum(ll, axis=0, keepdims=True)
             ot = acc[hs, :] / l
@@ -106,25 +106,23 @@
             o_ref[f // fl, :, f % fl] = o[j * tok:(j + 1) * tok].reshape(nr, pt, lw)
         done(a)
 
-    slots = sb.shape[0]
-    def q_block(a, last):
-        par = (a * nh) % slots if nh % slots else 0
+    def q_block(a, par, last):
         for h in range(nh):
-            cs = (par + h) % slots
-            cur = (a, h, cs)
-            ns = (par + h + 1) % slots
+            cur, ns = (a, h, (par + h) % 2), (par + h + 1) % 2
             if h + 1 < nh:
                 stage(cur, (a, h + 1, ns), False)
             else:
                 stage(cur, None if last else (a + 1, 0, ns), True)
         finish(a)
     stage(None, (0, 0, 0), False)
-    def step(a, _):
-        q_block(a, False)
+    span = 2 if nh % 2 else 1
+    def step(i, _):
+        for n in range(span):
+            q_block(i * span + n, n % 2, False)
         return 0
-    lax.fori_loop(0, nblk - 1, step, 0)
-    q_block(nblk - 1, True)
-
+    lax.fori_loop(0, nblk // span - 1, step, 0)
+    for n in range(span):
+        q_block(nblk - span + n, n % 2, n == span - 1)
 
 def rotate_back(t, cos, sin, nh):
     out = []
@@ -134,7 +132,7 @@
         out += [a * cos + b * sin, b * cos - a * sin]
     return jnp.concatenate(out, axis=0)
 
-def flash_backward(x_ref, go_ref, ot_ref, lse_ref, cos_ref, sin_ref, g_ref, qm, dom, kf, vf, kt, delta, dqt, dka, dva, done):
+def flash_backward(x_ref, go_ref, ot_ref, lse_ref, cos_ref, sin_ref, gq_ref, gkv_ref, qm, dom, kf, vf, kt, delta, dqt, dka, dva, done_q, done_kv):
     nf, nr, fl, pt, width = x_ref.shape
     lw = width // 3
     nh = lw // HD
@@ -161,18 +159,32 @@
 
     def work(k0, kn, q0, qn):
         rows, cols = pl.ds(k0, kn), pl.ds(q0, qn)
+        k, v = kf[rows, :], vf[rows, :]
+        s = [dot(k, qm[h, cols, :], NT) for h in range(nh)]
+        g = [dot(v, dom[h, cols, :], NT) for h in range(nh)]
         dv, dk = [], []
         for h in range(nh):
             hs = slice(h * HD, (h + 1) * HD)
-            qh, dh = qm[h, cols, :], dom[h, cols, :]
-            p = jnp.exp(dot(kf[rows, :], qh, NT) - lse_ref[h:h + 1, cols])
-            ds = (p * (dot(vf[rows, :], dh, NT) - delta[h:h + 1, cols])).astype(jnp.bfloat16)
-            dv.append(dot(p.astype(jnp.bfloat16), dh, NN))
-            dk.append(dot(ds, qh, NN))
+            p = jnp.exp(s[h] - lse_ref[h:h + 1, cols])
+            ds = (p * (g[h] - delta[h:h + 1, cols])).astype(jnp.bfloat16)
+            dv.append(dot(p.astype(jnp.bfloat16), dom[h, cols, :], NN))
+            dk.append(dot(ds, qm[h, cols, :], NN))
             dqt[hs, cols] += dot(kt[hs, rows], ds, NN)
         return sum(dk[1:], dk[0]), sum(dv[1:], dv[0])
 
-    def k_block(b, _):
+    count = frames // 2
+    half = count // 2
+
+    def store_q(a):
+        cols = pl.ds(pl.multiple_of(a * blk, blk), blk)
+        dq = rotate_back(dqt[:, cols] * HD ** -0.5, cos_ref[:, cols], sin_ref[:, cols], nh).T.astype(jnp.bfloat16)
+        for j in range(2):
+            f = 2 * a + j
+            gq_ref[f // fl, :, f % fl] = dq[j * tok:(j + 1) * tok].reshape(nr, pt, lw)
+        done_q(a)
+
+    def k_block(t, _):
+        b = lax.rem(t + half, count)
         k0 = pl.multiple_of(b * blk, blk)
         k1 = pl.multiple_of(b * blk + tok, tok)
         dk, dv = work(k0, tok, k0, blk)
@@ -181,24 +193,28 @@
         dk, dv = work(k1, tok, k1, tok)
         dka[tok:, :] = dk
         dva[tok:, :] = dv
+        @pl.when(b < half)
+        def _():
+            store_q(b)
         def q_block(a, _):
             dk, dv = work(k0, blk, pl.multiple_of(a * blk, blk), blk)
             dka[...] += dk
             dva[...] += dv
+            @pl.when(t == count - 1)
+            def _():
+                store_q(a)
             return 0
-        lax.fori_loop(b + 1, frames // 2, q_block, 0)
+        lax.fori_loop(b + 1, count, q_block, 0)
         cols = pl.ds(k0, blk)
         dk = rotate_back(dka[...].T, cos_ref[:, cols], sin_ref[:, cols], nh).T.astype(jnp.bfloat16)
         dv = dva[...].astype(jnp.bfloat16)
-        dq = rotate_back(dqt[:, cols] * HD ** -0.5, cos_ref[:, cols], sin_ref[:, cols], nh).T.astype(jnp.bfloat16)
         for j in range(2):
             f = 2 * b + j
-            for n, part in enumerate((dq, dk, dv)):
-                g_ref[f // fl, :, f % fl, :, n * lw:(n + 1) * lw] = part[j * tok:(j + 1) * tok].reshape(nr, pt, lw)
-        done(b)
+            for n, part in enumerate((dk, dv)):
+                gkv_ref[f // fl, :, f % fl, :, n * lw:(n + 1) * lw] = part[j * tok:(j + 1) * tok].reshape(nr, pt, lw)
+        done_kv(t, b)
         return 0
-    lax.fori_loop(0, frames // 2, k_block, 0)
-
+    lax.fori_loop(0, count, k_block, 0)
 
 ALL = ("clip", "frame", "row")
 B16, F32 = jnp.bfloat16, jnp.float32
@@ -355,7 +371,7 @@
 def fwd_all_kernel(*refs, calls):
     plane = Plane()
     x_send, x_out, a_out, ot_ref, lse_ref = refs[:5]
-    xv, ob, qm, kf, vt, sb, acc, mrow, xs, xr, xl, os, orr, ol, save = refs[5:]
+    xv, ob, qm, kf, vt, sa, sb, acc, ma, mb, xs, xr, xl, os, orr, ol, save = refs[5:]
     greet(plane, False)
     for i in range(calls):
         pltpu.make_async_copy(x_send.at[i, plane.me], xv.at[i, plane.f, plane.r], xl.at[i]).start()
@@ -373,7 +389,7 @@
         pltpu.make_async_copy(x_send.at[i, plane.me], xv.at[i, plane.f, plane.r], xl.at[i]).wait()
         arrive(i, True)
         pltpu.make_async_copy(xv.at[i], x_out.at[i], save.at[i]).start()
-        flash_forward(xv.at[i], ob.at[i], ot_ref.at[i], lse_ref.at[i], qm, kf, vt, sb, acc, mrow,
+        flash_forward(xv.at[i], ob.at[i], ot_ref.at[i], lse_ref.at[i], qm, kf, vt, sa, sb, acc, ma, mb,
                       lambda a: send_blocks(plane, i, a, ob, a_out, os, orr, ol))
         return 0
     lax.fori_loop(0, calls, call, 0)
@@ -399,7 +415,7 @@
         out_shape=(s((calls,) + lead + (3 * lw,), B16), s((calls, group, fl, pt, lw), B16),
                    s((calls, lw, seq), F32), s((calls, nh, seq), F32)),
         scratch_shapes=[v((calls,) + lead + (3 * lw,), B16), v((calls,) + lead + (lw,), B16), v((nh, seq, lw), B16),
-                        v((seq, lw), B16), v((lw, seq), B16), v((2, seq, blk), F32), v((lw, blk), F32), v((2, 1, blk), F32),
+                        v((seq, lw), B16), v((lw, seq), B16), v((seq, blk), F32), v((seq, blk), F32), v((lw, blk), F32), v((1, blk), F32), v((1, blk), F32),
                         dma((calls, group)), dma((calls, group)), dma((calls,)), dma((calls, group)), dma((calls, group)),
                         dma((calls,)), dma((calls,))],
         compiler_params=pltpu.CompilerParams(vmem_limit_bytes=56 << 20, collective_id=0, has_side_effects=True),
@@ -438,6 +454,9 @@
             out.append(remote(self.block(stage, p), dst.at[me], self.sems.at[0, base + k], self.sems.at[1, base + k], device(p)))
         return out, pltpu.make_async_copy(self.block(stage, me), dst.at[me], self.sems.at[0, base])
 
+    def fetch(self):
+        return pltpu.make_async_copy(self.part, self.v1, self.sems.at[0, 0])
+
     def start(self, stage):
         copies, own = self.copies(stage)
         for c in copies:
@@ -465,8 +484,7 @@
                       {"row": self.plane.r + 1 - 2 * self.bit})
 
     def columns(self, b):
-        first, size = self.cols
-        return pl.ds(b * self.out_cols + first, size)
+        return pl.ds(b * self.out_cols + self.at, self.cols[1])
 
     def last(self):
         total = self.v2[0].astype(F32)
@@ -490,36 +508,42 @@
 
 
 def sum_plan(parts, orders):
-    scratch, outs, jobs = [], [], []
-    for n, (part, order) in enumerate(zip(parts, orders)):
-        nc, np_, two, ch = part.shape
-        outs.append(jax.ShapeDtypeStruct((two // 2, 2 * ch), F32))
-        for plane_first, first, cols in order:
-            n1, n2 = (np_, nc) if plane_first else (nc, np_)
+    scratch, outs, jobs = [], {}, []
+    for n, (part, (o, half, arrived, pieces)) in enumerate(zip(parts, orders)):
+        two = part.shape[2]
+        outs[o] = jax.ShapeDtypeStruct((two // 2, 2 * half), F32)
+        for plane_first, first, cols, at in pieces:
+            n1, n2 = part.shape[:2]
+            if plane_first and not arrived:
+                n1, n2 = n2, n1
             scratch += [pltpu.VMEM((n1, n2, two, cols), B16), pltpu.VMEM((n2, two, cols), B16), pltpu.VMEM((n2, two, cols), B16),
                         pltpu.VMEM((2, two // 2, cols), F32), pltpu.VMEM((two // 2, cols), F32),
                         pltpu.SemaphoreType.DMA((2, n1 + n2 + 1))]
-            jobs.append((n, plane_first, first, cols))
-    return scratch, outs, jobs
+            jobs.append((n, o, half, arrived, plane_first, first, cols, at))
+    return scratch, [outs[o] for o in sorted(outs)], jobs
 
 
 def make_sums(plane, jobs, parts, outs, scratch):
-    return [Sum(plane, plane_first, parts[n], outs[n], (first, cols), parts[n].shape[3], *scratch[6 * i:6 * i + 6])
-            for i, (n, plane_first, first, cols) in enumerate(jobs)]
-
-
-def bwd_all_kernel(*refs, calls, count, jobs):
+    sums = []
+    for i, (n, o, half, arrived, plane_first, first, cols, at) in enumerate(jobs):
+        s = Sum(plane, plane_first, parts[n], outs[o], (first, cols), half, *scratch[6 * i:6 * i + 6])
+        s.at, s.arrived = at, arrived
+        sums.append(s)
+    return sums
+
+
+def bwd_all_kernel(*refs, calls, count, outputs, jobs):
     plane = Plane()
     x_in, go_in, ot_in, lse_ref, cos_ref, sin_ref = refs[:6]
     go_send = refs[6:5 + calls]
     at = 5 + calls
     parts = refs[at:at + count]
     at += count
-    gx_out = refs[at]
-    outs = refs[at + 1:at + 1 + count]
-    at += 1 + count
-    xv, gov, otv, gb, qm, dom, kf, vf, kt, delta, dqt, dka, dva, loads, gs, gr, gl, xs, xr, xl = refs[at:at + 20]
-    sums = make_sums(plane, jobs, parts, outs, refs[at + 20:])
+    gq_out, gkv_out = refs[at:at + 2]
+    outs = refs[at + 2:at + 2 + outputs]
+    at += 2 + outputs
+    xv, gov, otv, gqb, gkb, qm, dom, kf, vf, kt, delta, dqt, dka, dva, loads, gs, gr, gl, qs, qr, ql, xs, xr, xl = refs[at:at + 24]
+    sums = make_sums(plane, jobs, parts, outs, refs[at + 24:])
     greet(plane, True)
     load = [pltpu.make_async_copy(go_in, gov.at[0], gl.at[0])]
     for i in range(calls):
@@ -533,8 +557,12 @@
         pltpu.make_async_copy(go_send[i - 1].at[plane.me], gov.at[i, plane.f, plane.r], gl.at[i]).start()
         for k in range(1, plane.size):
             go_copy(i, k, go_send[i - 1]).start()
-    for s in sums:
+    early = [s for s in sums if s.arrived]
+    late = [s for s in sums if not s.arrived]
+    for s in late:
         s.start(1)
+    for s in early:
+        s.fetch().start()
 
     def call(i, _):
         pltpu.make_async_copy(x_in.at[i], xv.at[i], loads.at[0, i]).wait()
@@ -548,26 +576,37 @@
         @pl.when(i == 0)
         def _():
             pltpu.make_async_copy(go_in, gov.at[0], gl.at[0]).wait()
-        def block_done(b):
-            send_blocks(plane, i, b, gb, gx_out, xs, xr, xl)
-            @pl.when(jnp.logical_and(i == calls - 1, b == 3))
+        def done_q(a):
+            send_blocks(plane, i, a, gqb, gq_out, qs, qr, ql)
+        def done_kv(t, b):
+            send_blocks(plane, i, b, gkb, gkv_out, xs, xr, xl)
+            @pl.when(jnp.logical_and(i == 0, t == 0))
             def _():
-                for s in sums:
+                for s in early:
+                    s.fetch().wait()
+                    s.middle()
+            @pl.when(jnp.logical_and(i == calls - 1, t == 4))
+            def _():
+                for s in early:
+                    s.wait(2)
+                    s.last()
+                for s in late:
                     s.wait(1)
                     s.middle()
-        flash_backward(xv.at[i], gov.at[i], otv.at[i], lse_ref.at[i], cos_ref, sin_ref, gb.at[i],
-                       qm, dom, kf, vf, kt, delta, dqt, dka, dva, block_done)
+        flash_backward(xv.at[i], gov.at[i], otv.at[i], lse_ref.at[i], cos_ref, sin_ref, gqb.at[i], gkb.at[i],
+                       qm, dom, kf, vf, kt, delta, dqt, dka, dva, done_q, done_kv)
         return 0
     lax.fori_loop(0, calls, call, 0)
     for i in range(1, calls):
         for k in range(1, plane.size):
             go_copy(i, k, go_send[i - 1]).wait_send()
-    for s in sums:
+    for s in late:
         s.wait(2)
         s.last()
     for s in sums:
         s.close()
-    wait_blocks(plane, calls, gb, gx_out, xs, xr, xl)
+    wait_blocks(plane, calls, gqb, gq_out, qs, qr, ql)
+    wait_blocks(plane, calls, gkb, gkv_out, xs, xr, xl)
 
 
 def attention_backward(x, go, go_sends, ot, lse, cos, sin, parts, orders):
@@ -582,14 +621,14 @@
     s, v, dma = jax.ShapeDtypeStruct, pltpu.VMEM, pltpu.SemaphoreType.DMA
     scratch, outs, jobs = sum_plan(parts, orders)
     return pl.pallas_call(
-        functools.partial(bwd_all_kernel, calls=calls, count=len(parts), jobs=jobs),
+        functools.partial(bwd_all_kernel, calls=calls, count=len(parts), outputs=len(outs), jobs=jobs),
         in_specs=[hbm, hbm, hbm, vmem, vmem, vmem] + [hbm] * (len(go_sends) + len(parts)),
-        out_specs=[hbm] + [vmem] * len(parts),
-        out_shape=[s((calls, group, fl, pt, w3), B16)] + outs,
-        scratch_shapes=[v((calls,) + lead + (w3,), B16), v((calls,) + lead + (lw,), B16), v((calls, lw, seq), F32), v((calls,) + lead + (w3,), B16),
+        out_specs=[hbm, hbm] + [vmem] * len(outs),
+        out_shape=[s((calls, group, fl, pt, lw), B16), s((calls, group, fl, pt, 2 * lw), B16)] + outs,
+        scratch_shapes=[v((calls,) + lead + (w3,), B16), v((calls,) + lead + (lw,), B16), v((calls, lw, seq), F32), v((calls,) + lead + (lw,), B16), v((calls,) + lead + (2 * lw,), B16),
                         v((nh, seq, lw), B16), v((nh, seq, lw), B16), v((seq, lw), B16), v((seq, lw), B16), v((lw, seq), B16),
                         v((nh, seq), F32), v((lw, seq), F32), v((blk, lw), F32), v((blk, lw), F32),
-                        dma((2, calls)), dma((calls, group)), dma((calls, group)), dma((calls,)), dma((calls, group)), dma((calls, group)), dma((calls,))] + scratch,
+                        dma((2, calls)), dma((calls, group)), dma((calls, group)), dma((calls,)), dma((calls, group)), dma((calls, group)), dma((calls,)), dma((calls, group)), dma((calls, group)), dma((calls,))] + scratch,
         compiler_params=pltpu.CompilerParams(vmem_limit_bytes=61 << 20, collective_id=1, has_side_effects=True),
         cost_estimate=pl.CostEstimate(flops=calls * seq * seq * lw * 5, bytes_accessed=calls * seq * lw * 48, transcendentals=calls * seq * seq * nh // 2),
         name="attention_backward",
@@ -597,11 +636,16 @@
 
 
 def mlp_kernel(a_ref, x_hbm, g_hbm, mod_ref, wo_ref, bo_ref, wu_ref, bu_ref, wd_ref, bd_ref,
-               y_out, gm_out, ga_out, go_out, pd_out, pu_out, po_out, sums_ref, du_ref, db_ref,
+               y_out, gm_out, ga_out, go_out, pd_out, ugot, vgot, po_out, sums_ref, du_ref, db_ref,
                g, an, branch, mixed, h, gd, down, gh, st, gav, sd, su, rd, ru, kd, ku, pd, pu, *sems, calls):
-    io, od, pair, free, done, gs, gr, gl, oo = sems
+    io, od, pair, free, done, gs, gr, gl, oo, us, ur, vr = sems
     plane = Plane()
+    nc, mc = lax.axis_size("clip"), lax.axis_index("clip")
+    half_row = plane.nr // 2
+    places, mp = plane.nf * half_row, plane.f * half_row + plane.r // 2
+    at_place = lambda p: {"frame": p // half_row, "row": lax.rem(p, half_row) * 2 + bit}
     bit = lax.rem(plane.r, 2)
+    clip_first = ugot.shape[3] // (wu_ref.shape[1] // 2)
     partner = {"row": plane.r + 1 - 2 * bit}
     clips, hg, count, lw = a_ref.shape
     width = an.shape[1]
@@ -630,7 +674,7 @@
         loads = [pltpu.make_async_copy(x_hbm, h, io.at[0]), pltpu.make_async_copy(g_hbm, g.at[pl.ds(0, clips * count)], io.at[1])]
         for c in loads:
             c.start()
-        greet(plane, False)
+        greet(plane, True)
         for c in range(clips):
             for i in range(hg):
                 an[c * count:(c + 1) * count, i * lw:(i + 1) * lw] = a_ref[c, i]
@@ -680,23 +724,36 @@
         return (remote(sd.at[n], rd.at[s], pair.at[0, n], pair.at[1, s], partner),
                 remote(su.at[n], ru.at[s], pair.at[2, n], pair.at[3, s], partner))
 
-    def stores(j):
+    def onward(j, what):
         n = lax.rem(j, 2)
-        return (pltpu.make_async_copy(pd.at[n], pd_out.at[pl.ds(pl.multiple_of(j * fc, fc), fc)], od.at[0, n]),
-                pltpu.make_async_copy(pu.at[n], pu_out.at[:, pl.ds(pl.multiple_of(j * hf, hf), hf)], od.at[1, n]))
+        def do(copy, sent):
+            copy.start() if what == "start" else (copy.wait_send() if sent else copy.wait())
+        do(pltpu.make_async_copy(pd.at[n], pd_out.at[pl.ds(pl.multiple_of(j * fc, fc), fc)], od.at[0, n]), False)
+        @pl.when(j < clip_first)
+        def _():
+            cols = pl.ds(pl.multiple_of(j * hf, hf), hf)
+            do(pltpu.make_async_copy(pu.at[n, mc], ugot.at[mc, :, :, cols], od.at[1, n]), False)
+            for k in range(1, nc):
+                c = lax.rem(mc + k, nc)
+                do(remote(pu.at[n, c], ugot.at[mc, :, :, cols], us.at[n, k], ur.at[mc], {"clip": c}), True)
+        @pl.when(j >= clip_first)
+        def _():
+            cols = pl.ds(pl.multiple_of((j - clip_first) * hf, hf), hf)
+            do(pltpu.make_async_copy(pu.at[n, :, mp], vgot.at[mp, :, :, cols], od.at[1, n]), False)
+            for k in range(1, places):
+                p = lax.rem(mp + k, places)
+                do(remote(pu.at[n, :, p], vgot.at[mp, :, :, cols], us.at[n, k], vr.at[mp], at_place(p)), True)
 
     def finish(j):
         n, s = lax.rem(j, 2), lax.rem(j, slots)
         @pl.when(j >= 2)
         def _():
-            for c in stores(j - 2):
-                c.wait()
+            onward(j - 2, "wait")
         for c in swaps(j):
             c.wait_recv()
         pd[n] = (kd[n] + rd[s].astype(F32)).astype(B16)
-        pu[n] = (ku[n] + ru[s].astype(F32)).astype(B16)
-        for c in stores(j):
-            c.start()
+        pu[n] = (ku[n] + ru[s].astype(F32)).astype(B16).reshape(pu.shape[1:])
+        onward(j, "start")
         @pl.when(j + slots < steps)
         def _():
             pl.semaphore_signal(free, inc=1, device_id=partner, device_id_type=MESH)
@@ -783,8 +840,14 @@
         own.wait()
         for c in swaps(step - 1) + swaps(step):
             c.wait_send()
-        for c in stores(step - 1) + stores(step):
-            c.wait()
+        onward(step - 1, "wait")
+        onward(step, "wait")
+        for k in range(1, places):
+            p = lax.rem(mp + k, places)
+            remote(vgot.at[p], vgot.at[p], us.at[0, 0], vr.at[p], at_place(p)).wait_recv()
+        for k in range(1, nc):
+            c = lax.rem(mc + k, nc)
+            remote(ugot.at[c], ugot.at[c], us.at[0, 0], ur.at[c], {"clip": c}).wait_recv()
         for c in outs:
             c.wait()
 
@@ -799,6 +862,10 @@
     nf, nr = lead[:2]
     group = nf * nr
     slots = 3
+    nc = lax.axis_size("clip")
+    places, steps = group // 2, ff // fc
+    clip_first = max(1, steps // 4)
+    two_u = width // (nc * places)
     tall = max(rows, width)
     whole = lambda *shape: pl.BlockSpec(shape, lambda j: (0,) * len(shape), pipeline_mode=pl.Buffered(1))
     keep = lambda *shape: pl.BlockSpec(shape, lambda j: (0,) * len(shape))
@@ -810,28 +877,28 @@
         in_specs=[whole(clips, hg, count, lw), hbm, hbm, whole(frames, 6, width), whole(width, width), whole(1, width),
                   pl.BlockSpec((width, fc), lambda j: (0, j)), pl.BlockSpec((1, fc), lambda j: (0, j)),
                   pl.BlockSpec((fc, width), lambda j: (j, 0)), whole(1, width)],
-        out_specs=[hbm] * 7 + [keep(frames, 4, width), pl.BlockSpec((1, fc), lambda j: (0, j)), keep(2, width)],
+        out_specs=[hbm] * 8 + [keep(frames, 4, width), pl.BlockSpec((1, fc), lambda j: (0, j)), keep(2, width)],
         out_shape=[s((rows, width), B16), s((rows, width), F32), s((max(1, calls - 1) * group, count, lw), B16),
-                   s((nf, nr, count, lw), B16), s((ff, hw), B16), s((width, ff // 2), B16), s((width, hw), B16),
+                   s((nf, nr, count, lw), B16), s((ff, hw), B16), s((nc, places, two_u, clip_first * hf), B16), s((places, nc, two_u, (steps - clip_first) * hf), B16), s((width, hw), B16),
                    s((frames, 4, width), F32), s((1, ff), F32), s((2, width), F32)],
         scratch_shapes=[v((tall, width), B16), v((tall, width), B16), v((rows, width), F32), v((rows, width), F32),
                         v((rows, width), B16), v((rows, width), B16), v((tall, width), F32), v((rows, width), F32), v((rows, 256), F32),
                         v((clips * hg, count, lw), B16), v((2, fc, hw), B16), v((2, width, hf), B16), v((slots, fc, hw), B16),
-                        v((slots, width, hf), B16), v((2, fc, hw), F32), v((2, width, hf), F32), v((2, fc, hw), B16), v((2, width, hf), B16),
+                        v((slots, width, hf), B16), v((2, fc, hw), F32), v((2, width, hf), F32), v((2, fc, hw), B16), v((2, nc, places, two_u, hf), B16),
                         dma((2,)), dma((2, 2)), dma((4, slots + 1)), pltpu.SemaphoreType.REGULAR, pltpu.SemaphoreType.REGULAR,
-                        dma((group,)), dma((group,)), dma, dma((4,))],
+                        dma((group,)), dma((group,)), dma, dma((4,)), dma((2, max(places, nc))), dma((nc,)), dma((places,))],
         compiler_params=pltpu.CompilerParams(vmem_limit_bytes=63 << 20, dimension_semantics=("arbitrary",), collective_id=3, has_side_effects=True),
         cost_estimate=pl.CostEstimate(flops=2 * rows * width * (3 * width + 6 * ff), bytes_accessed=8 * width * ff + 20 * rows * width, transcendentals=rows * ff),
         name="mlp",
     )(attn, x, g, mods, w_out, b_out, w_up, b_up, w_down, b_down)
 
 
-def tail_kernel(gp_hbm, h_hbm, w_hbm, x_hbm, gm_hbm, mod_ref, clean_ref, sums2_ref, vec_ref,
+def tail_kernel(gq_hbm, gkv_hbm, h_hbm, w_hbm, x_hbm, gm_hbm, mod_ref, clean_ref, sums2_ref, vec_ref,
                 o_out, gw_ref, noise_ref, vec_out,
-                gp, h, w, x, gm, full, gh, send, got, part, s1s, dbq, nsend, nrecv, vsend, v1, vmid, v2, io, pair, nsem, vsem, oo, *scratch, jobs):
+                gq, gkv, h, w, x, gm, full, gh, send, got, part, s1s, dbq, nsend, nrecv, vsend, v1, vmid, v2, io, pair, nsem, vsem, oo, *scratch, jobs):
     plane = Plane()
-    clips, hg, count, w3 = gp_hbm.shape
-    lw = w3 // 3
+    clips, hg, count, lw = gq_hbm.shape
+    w3 = 3 * lw
     width = w.shape[0]
     frames = mod_ref.shape[0] // clips
     pt = count // frames
@@ -842,19 +909,19 @@
     packed = max(1, 128 * 3 // w3)
     blocks = hg // 2 // packed
     bw = packed * w3
-    loads = [pltpu.make_async_copy(gp_hbm, gp, io.at[0]), pltpu.make_async_copy(h_hbm, h, io.at[1]),
+    loads = [pltpu.make_async_copy(gq_hbm, gq, io.at[0]), pltpu.make_async_copy(gkv_hbm, gkv, io.at[5]), pltpu.make_async_copy(h_hbm, h, io.at[1]),
              pltpu.make_async_copy(w_hbm, w, io.at[2]), pltpu.make_async_copy(x_hbm, x, io.at[3]), pltpu.make_async_copy(gm_hbm, gm, io.at[4])]
     for c in loads:
         c.start()
     sums = make_sums(plane, jobs, [part], [gw_ref], scratch)
     greet(plane, True)
-    for c in loads[:2]:
+    for c in loads[:3]:
         c.wait()
 
     def outer(j):
         total = None
         for c in range(clips):
-            b = jnp.concatenate([gp[c, j * packed + i] for i in range(packed)], axis=1)
+            b = jnp.concatenate([v[c, j * packed + i] for i in range(packed) for v in (gq, gkv)], axis=1)
             t = dot(h[c], b, TN)
             total = t if total is None else total + t
         return total
@@ -865,7 +932,8 @@
     for j in range(blocks):
         send[j] = outer(other * blocks + j).astype(B16)
         swap(j).start()
-    for s, (_, plane_first, first, cols) in zip(sums, jobs):
+    for s in sums:
+        first, cols = s.cols
         j = first // bw
         total = outer(bit * blocks + j)
         swap(j).wait_recv()
@@ -873,13 +941,14 @@
         part[:, :, :, first:first + cols] = total.reshape(part.shape[:3] + (cols,))
         s.start(1)
 
-    for c in loads[2:]:
+    for c in loads[3:]:
         c.wait()
     dbq[...] = jnp.zeros_like(dbq)
     for c in range(clips):
-        for j in range(3):
-            for g in range(hg):
-                full[:, j * width + g * lw:j * width + (g + 1) * lw] = gp[c, g, :, j * lw:(j + 1) * lw]
+        for g in range(hg):
+            full[:, g * lw:(g + 1) * lw] = gq[c, g]
+            for j in range(2):
+                full[:, (j + 1) * width + g * lw:(j + 1) * width + (g + 1) * lw] = gkv[c, g, :, j * lw:(j + 1) * lw]
         gh[...] = dot(full[...], w[...], NT)
         dbq[...] += jnp.sum(full[...].astype(F32), axis=0, keepdims=True)
         def one(f, _):
@@ -972,9 +1041,9 @@
         pltpu.make_async_copy(gm.at[c], o_out.at[c], oo.at[c]).wait()
 
 
-def tail(gproj, h1, w_qkv, x, gmixed, mods, clean, sums2, vec):
-    clips, hg, count, w3 = gproj.shape
-    lw = w3 // 3
+def tail(gq, gkv, h1, w_qkv, x, gmixed, mods, clean, sums2, vec):
+    clips, hg, count, lw = gq.shape
+    w3 = 3 * lw
     width = x.shape[2]
     nc, nf, nr = (lax.axis_size(a) for a in ALL)
     group = nf * nr
@@ -986,22 +1055,22 @@
     hbm, vmem = pl.BlockSpec(memory_space=pl.ANY), pl.BlockSpec(memory_space=pltpu.VMEM)
     s, v, dma = jax.ShapeDtypeStruct, pltpu.VMEM, pltpu.SemaphoreType.DMA
     shape = jax.ShapeDtypeStruct((nc, nf * nr // 2, two, blocks * bw), B16)
-    order = [(False if j == 0 else True, j * bw, bw) for j in range(blocks)]
-    scratch, outs, jobs = sum_plan([shape], [order])
+    order = [(False if j == 0 else True, j * bw, bw, j * bw) for j in range(blocks)]
+    scratch, outs, jobs = sum_plan([shape], [(0, blocks * bw, False, order)])
     return pl.pallas_call(
         functools.partial(tail_kernel, jobs=jobs),
-        in_specs=[hbm] * 5 + [vmem] * 4,
+        in_specs=[hbm] * 6 + [vmem] * 4,
         out_specs=[hbm, vmem, vmem, vmem],
         out_shape=[s((clips, count, width), F32)] + outs + [s((frames, 6, width // nr), F32), s((vrows, width), F32)],
-        scratch_shapes=[v((clips, hg, count, w3), B16), v((clips, count, width), B16), v((width, 3 * width), B16), v((clips, count, width), B16),
+        scratch_shapes=[v((clips, hg, count, lw), B16), v((clips, hg, count, 2 * lw), B16), v((clips, count, width), B16), v((width, 3 * width), B16), v((clips, count, width), B16),
                         v((clips, count, width), F32), v((count, 3 * width), B16), v((count, width), F32), v((blocks, width, bw), B16),
                         v((blocks, width, bw), B16), v(shape.shape, B16), v((frames, 8, width), F32), v((1, 3 * width), F32),
                         v((nr, frames, 6, width // nr), B16), v((nr, frames, 6, width // nr), B16), v((vrows, width), F32), v((group, vrows, width), F32),
-                        v((vrows, width), F32), v((nc, vrows, width), F32), dma((5,)), dma((2, blocks)), dma((2, nr)), dma((2, group + nc)), dma((clips,))] + scratch,
+                        v((vrows, width), F32), v((nc, vrows, width), F32), dma((6,)), dma((2, blocks)), dma((2, nr)), dma((2, group + nc)), dma((clips,))] + scratch,
         compiler_params=pltpu.CompilerParams(vmem_limit_bytes=62 << 20, collective_id=2, has_side_effects=True),
         cost_estimate=pl.CostEstimate(flops=12 * clips * count * width * width, bytes_accessed=40 * clips * count * width, transcendentals=0),
         name="tail",
-    )(gproj, h1, w_qkv, x, gmixed, mods, clean, sums2, vec)
+    )(gq, gkv, h1, w_qkv, x, gmixed, mods, clean, sums2, vec)
 
 
 def on_device(tokens, context, noise_mod, clean_mod, w_qkv, b_qkv, w_out, b_out, w_up, b_up, w_down, b_down, cotangent):
@@ -1040,7 +1109,7 @@
 
     rows = clips * count
     by_frame = mods.reshape(clips * frames, 6, width)
-    y, gmixed, ga, go, part_down, part_up, part_out, sums2, db_up, db_two = mlp(
+    y, gmixed, ga, go, part_down, got_up, got_up2, part_out, sums2, db_up, db_two = mlp(
         attn, inputs.reshape(rows, width), cots.reshape(rows, width), by_frame,
         w_out, row_of(b_out), w_up, row_of(b_up), w_down, row_of(b_down), calls, lead)
     go = go.reshape(lead + (lw,))
@@ -1048,16 +1117,19 @@
     gmixed = gmixed.reshape(clips, count, width)
 
     nc = lax.axis_size("clip")
-    as_blocks = lambda p: p.reshape(nc, nf * nr // 2, p.shape[0] // (nc * nf * nr // 2), p.shape[1])
-    parts = [as_blocks(p) for p in (part_down, part_up, part_out)]
-    orders = [[(True, 0, parts[0].shape[3])], [(False, 0, parts[1].shape[3])], [(False, 0, parts[2].shape[3])]]
-    gproj, gw_down, gw_up, gw_out = attention_backward(x, go, go_sends, ot, lse, cos_t, sin_t, parts, orders)
-    gproj = gproj.reshape(clips, hg, count, 3 * lw)
+    places = group // 2
+    first, second, hw = got_up.shape[3], got_up2.shape[3], width // 2
+    as_blocks = lambda p: p.reshape(nc, places, p.shape[0] // (nc * places), p.shape[1])
+    parts = [as_blocks(part_down), got_up, got_up2, as_blocks(part_out)]
+    orders = [(0, hw, False, [(False, 0, hw // 2, 0), (True, hw // 2, hw // 2, hw // 2)]), (1, first + second, True, [(False, 0, first, 0)]),
+              (1, first + second, True, [(True, 0, second, first)]), (2, hw, False, [(False, 0, hw, 0)])]
+    gq, gkv, gw_down, gw_up, gw_out = attention_backward(x, go, go_sends, ot, lse, cos_t, sin_t, parts, orders)
+    gq, gkv = gq.reshape(clips, hg, count, lw), gkv.reshape(clips, hg, count, 2 * lw)
     fc = min(512, w_up.shape[1])
     gw_up = gw_up.reshape(gw_up.shape[0], 2, -1, fc // 2).transpose(0, 2, 1, 3).reshape(gw_up.shape[0], -1)
     clean = jnp.broadcast_to(is_clean.reshape(-1, 1, 1), (clips * frames, 1, width)).astype(F32)
     vec = jnp.concatenate([db_up.reshape(-1, width), db_two], axis=0)
-    gtokens, gw_qkv, noise, vec = tail(gproj, h1, w_qkv, inputs, gmixed, by_frame, clean, sums2, vec)
+    gtokens, gw_qkv, noise, vec = tail(gq, gkv, h1, w_qkv, inputs, gmixed, by_frame, clean, sums2, vec)
     per = gw_qkv.shape[0]
     gw_qkv = gw_qkv.reshape(per, 2, hg // 2, 3, lw).transpose(0, 3, 1, 2, 4).reshape(per, 3 * width)
     grad_noise = noise.reshape(clips, frames, 6, -1).transpose(1, 0, 2, 3)

time: 487 us -> 460 us (0.945)
  Pallas kernels: 448 us -> 421 us
    pallas_call x1, Pallas kernels: 163 us -> 138 us  [attention_backward(): pl.pallas_call(functools.partial(bwd_all_kernel, calls=calls, count=len(p...]
    pallas_call x1, Pallas kernels: 93.3 us -> 103 us  [mlp(): pl.pallas_call(functools.partial(mlp_kernel, calls=calls), grid=(ff // fc...]
    pallas_call x1, Pallas kernels: 65.2 us -> 56.7 us  [tail(): pl.pallas_call(functools.partial(tail_kernel, jobs=jobs), in_specs=[hbm]...]
where the time goes in v4:
time: 460 us; the launch traced here: 453 us
  Pallas kernels  421 us (92%)
  local copies, waits for them, and re-layouts  24.5 us (5%)
  other arithmetic  6.46 us (1%)
    pallas_call x1, Pallas kernels, attention_backward(): pl.pallas_call(functools.partial(bwd_all_kernel, calls=calls, count=len(p...  138 us
    pallas_call x1, Pallas kernels, attention_forward(): pl.pallas_call(functools.partial(fwd_all_kernel, calls=calls), in_specs=[...  108 us
    pallas_call x1, Pallas kernels, mlp(): pl.pallas_call(functools.partial(mlp_kernel, calls=calls), grid=(ff // fc...  103 us
    pallas_call x1, Pallas kernels, tail(): pl.pallas_call(functools.partial(tail_kernel, jobs=jobs), in_specs=[hbm]...  56.7 us
    pallas_call x1, Pallas kernels, qkv_forward(): pl.pallas_call(qkv_kernel, grid=(clips,), in_specs=[one(count, width), on...  15.4 us
    reshape x2, local copies, waits for them, and re-layouts, on_device(): back = lambda v: v.reshape(full).transpose(1, 2, 0, 3)  11 us

profile of v4, /device:TPU:1, one launch (start us, length us, event | category | flops | bytes accessed | tf_op | source)
XLA Modules:
  0.0 452.9 jit_solution(5697375894344002402)
XLA Ops:
  1.4 0.7 fusion.36
  2.2 1.1 bitcast_select_fusion.mod_ref
  3.3 0.6 copy.44
  4.0 15.4 %qkv.1 = (bf16[2,8,512,384]{3,2,1,0:T(8,128)(2,1)}, bf16[2,512,1024]{2,1,0:T(8,128)(2,1)S(1)}) custom-call(bf16[2,512,1024]{2,1,0:T(8,128)(2,1)S(1)} %bitcast.50, f32[2,8,6,1024]{3,2,1,0:T(8,128)S(1)} %bitcast_select_fusion.mod_ref, bf16[1024,3072]{1,0:T(8,128)(2,1)} %w_hbm.3, f32[1,3072]{1,0:T(1,128)S(1)} %bitcast.55, f32[512,128]{1,0:T(8,128)S(1)} %copy.46.cos_ref, ...), custom_call_target="tpu_custom_call" | custom-call | flops 6442450944 | bytes 16777216 | tf_op jit(solution)/shard_map/qkv/pallas_call | solution.py:294
  19.5 107.6 %attention_forward.1 = (bf16[2,2,4,8,64,384]{5,4,3,2,1,0:T(8,128)(2,1)}, bf16[2,8,8,64,128]{4,3,2,1,0:T(8,128)(2,1)}, f32[2,128,4096]{2,1,0:T(8,128)}, f32[2,2,4096]{2,1,0:T(2,128)}) custom-call(bf16[2,8,8,64,384]{4,3,2,1,0:T(8,128)(2,1)} %bitcast.74), custom_call_target="tpu_custom_call" | custom-call | flops 8589934592 | bytes 25165824 | tf_op jit(solution)/shard_map/attention_forward/pallas_call | solution.py:411
  127.1 2.0 copy.49
  129.0 102.6 %mlp.1 = (bf16[1024,1024]{1,0:T(8,128)(2,1)}, f32[1024,1024]{1,0:T(8,128)}, bf16[8,512,128]{2,1,0:T(8,128)(2,1)}, bf16[2,4,512,128]{3,2,1,0:T(8,128)(2,1)}, bf16...) custom-call(bf16[2,8,512,128]{3,2,1,0:T(8,128)(2,1)} %bitcast.79, ...), custom_call_target="tpu_custom_call" | custom-call | flops 57982058496 | bytes 54525952 | tf_op jit(solution)/shard_map/mlp/pallas_call | solution.py:874
  231.7 2.9 fusion
  234.6 138.4 %attention_backward.1 = (bf16[2,8,8,64,128]{4,3,2,1,0:T(8,128)(2,1)}, bf16[2,8,8,64,256]{4,3,2,1,0:T(8,128)(2,1)}, f32[128,1024]{1,0:T(8,128)}, f32[32,4096]{1,0:T(8,128)}, f32[32,1024]{1,0:T(8,128)}) custom-call(bf16[2,2,4,8,64,384]{5,4,3,2,1,0:T(8,128)(2,1)} %get-tuple-element.41.refs_0_, bf16[2,4,8,64,128]{4,3,2,1,0:T(8,128)(2,1)} %bitcast.81, ...), custom_call_target="tpu_custom_call" | custom-call | flops 21474836480 | bytes 50331648 | tf_op jit(solution)/shard_map/attention_backward/pallas_call | solution.py:623
  373.5 0.7 reduce.3
  374.2 0.6 pad_maximum_fusion.2.vec_ref
  375.0 0.7 broadcast_in_dim.139.clean_ref
  375.7 56.7 %tail.1 = (f32[2,512,1024]{2,1,0:T(8,128)}, f32[32,3072]{1,0:T(8,128)}, f32[16,6,256]{2,1,0:T(8,128)}, f32[16,1024]{1,0:T(8,128)}) custom-call(bf16[2,8,512,128]{3,2,1,0:T(8,128)(2,1)} %bitcast.78, bf16[2,8,512,256]{3,2,1,0:T(8,128)(2,1)} %bitcast.76, bf16[2,512,1024]{2,1,0:T(8,128)(2,1)} %copy-done.3, bf16[1024,3072]{1,0:T(8,128)(2,1)} %w_hbm.3, ...), custom_call_target="tpu_custom_call" | custom-call | flops 12884901888 | bytes 41943040 | tf_op jit(solution)/shard_map/tail/pallas_call | solution.py:1060
  432.4 7.5 %copy.62 = f32[2,8,64,1024]{3,0,2,1:T(2,128)} copy(f32[2,8,64,1024]{3,2,1,0:T(8,128)} %bitcast.57) | data formatting | bytes 8388608 | tf_op jit(solution)/shard_map/reshape | solution.py:1143
  440.3 0.9 reshape.319
  441.2 0.7 copy.64
  442.0 0.7 constant_dynamic-slice_fusion.2
  443.2 0.6 dynamic_slice.20
  443.8 0.6 fusion.27
  445.0 1.2 copy.55
  446.5 1.2 reshape.322
  447.7 3.5 copy.63
  451.2 0.7 copy.68
  451.9 0.8 copy.69
  (56 shorter events, 3.2 us)
Async XLA Ops:
  0.6 2.7 copy-start.4
  0.7 3.3 copy-start.2
  3.3 16.1 %copy-start.1 = (f32[2,8,6,1024]{3,2,1,0:T(8,128)}, f32[2,8,6,1024]{3,2,1,0:T(8,128)S(1)}, u32[]{:S(2)}) copy-start(f32[2,8,6,1024]{3,2,1,0:T(8,128)S(1)} %bitcast_select_fusion.mod_ref) | copy-start | bytes 1179652
  4.0 15.5 %copy-start = (bf16[2,8,64,1024]{3,2,1,0:T(8,128)(2,1)}, bf16[2,8,64,1024]{3,2,1,0:T(8,128)(2,1)S(1)}, u32[]{:S(2)}) copy-start(bf16[2,8,64,1024]{3,2,1,0:T(8,128)(2,1)S(1)} %copy.44) | copy-start | bytes 6291460
  19.5 107.6 %copy-start.3 = (bf16[2,512,1024]{2,1,0:T(8,128)(2,1)}, bf16[2,512,1024]{2,1,0:T(8,128)(2,1)S(1)}, u32[]{:S(2)}) copy-start(bf16[2,512,1024]{2,1,0:T(8,128)(2,1)S(1)} %get-tuple-element.52.h_hbm) | copy-start | bytes 6291460
  19.5 107.6 %copy-start.5 = (bf16[8,64,2,1024]{3,2,1,0:T(2,128)(2,1)S(1)}, bf16[8,64,2,1024]{3,2,1,0:T(2,128)(2,1)}, u32[]{:S(2)}) copy-start(bf16[8,64,2,1024]{3,2,1,0:T(2,128)(2,1)} %param.25) | copy-start | bytes 6291460
  234.6 139.0 %copy-start.12 = (f32[1,4096]{1,0:T(1,128)S(1)}, f32[1,4096]{1,0:T(1,128)}, u32[]{:S(2)}) copy-start(f32[1,4096]{1,0:T(1,128)} %get-tuple-element.55) | copy-start | bytes 49156
  234.6 139.7 %copy-start.13 = (f32[2,1024]{1,0:T(2,128)S(1)}, f32[2,1024]{1,0:T(2,128)}, u32[]{:S(2)}) copy-start(f32[2,1024]{1,0:T(2,128)} %get-tuple-element.56) | copy-start | bytes 24580
  432.4 7.5 %copy-start.8 = (f32[32,3072]{1,0:T(8,128)S(1)}, f32[32,3072]{1,0:T(8,128)}, u32[]{:S(2)}) copy-start(f32[32,3072]{1,0:T(8,128)} %get-tuple-element.60) | copy-start | bytes 1179652
  432.4 8.8 %copy-start.9 = (f32[16,6,256]{2,1,0:T(8,128)S(1)}, f32[16,6,256]{2,1,0:T(8,128)}, u32[]{:S(2)}) copy-start(f32[16,6,256]{2,1,0:T(8,128)} %get-tuple-element.58) | copy-start | bytes 294916
  432.4 9.5 %copy-start.11 = (f32[16,1024]{1,0:T(8,128)S(1)}, f32[16,1024]{1,0:T(8,128)}, u32[]{:S(2)}) copy-start(f32[16,1024]{1,0:T(8,128)} %get-tuple-element.59) | copy-start | bytes 196612
  439.9 7.8 %copy-start.6 = (bf16[1024,1024]{1,0:T(8,128)(2,1)S(1)}, bf16[1024,1024]{1,0:T(8,128)(2,1)}, u32[]{:S(2)}) copy-start(bf16[1024,1024]{1,0:T(8,128)(2,1)} %get-tuple-element.40) | copy-start | bytes 6291460
  440.3 10.9 %copy-start.10 = (f32[32,1024]{1,0:T(8,128)S(1)}, f32[32,1024]{1,0:T(8,128)}, u32[]{:S(2)}) copy-start(f32[32,1024]{1,0:T(8,128)} %get-tuple-element.97) | copy-start | bytes 393220
  441.2 10.6 %copy-start.7 = (f32[128,1024]{1,0:T(8,128)S(1)}, f32[128,1024]{1,0:T(8,128)}, u32[]{:S(2)}) copy-start(f32[128,1024]{1,0:T(8,128)} %get-tuple-element.101) | copy-start | bytes 1572868

commit v5 on v4

--- a/solution.py
+++ b/solution.py
@@ -483,8 +483,11 @@
         return remote(self.s2.at[1 - self.bit], self.v3, self.sems.at[0, self.sems.shape[1] - 1], self.sems.at[1, self.sems.shape[1] - 1],
                       {"row": self.plane.r + 1 - 2 * self.bit})
 
-    def columns(self, b):
-        return pl.ds(b * self.out_cols + self.at, self.cols[1])
+    def place_columns(self, b, value):
+        size = self.unit
+        for k in range(self.cols[1] // size):
+            to = self.where(b, (self.at + k * size) // size)
+            self.out[:, to:to + size] = value[:, k * size:(k + 1) * size]
 
     def last(self):
         total = self.v2[0].astype(F32)
@@ -497,19 +500,19 @@
         for b in range(2):
             @pl.when(self.bit == b)
             def _():
-                self.out[:, self.columns(b)] = self.s2[b]
+                self.place_columns(b, self.s2[b])
 
     def close(self):
         self.third().wait()
         for b in range(2):
             @pl.when(self.bit == b)
             def _():
-                self.out[:, self.columns(1 - b)] = self.v3[...]
+                self.place_columns(1 - b, self.v3[...])
 
 
 def sum_plan(parts, orders):
     scratch, outs, jobs = [], {}, []
-    for n, (part, (o, half, arrived, pieces)) in enumerate(zip(parts, orders)):
+    for n, (part, (o, half, arrived, pieces, unit, where)) in enumerate(zip(parts, orders)):
         two = part.shape[2]
         outs[o] = jax.ShapeDtypeStruct((two // 2, 2 * half), F32)
         for plane_first, first, cols, at in pieces:
@@ -519,15 +522,15 @@
             scratch += [pltpu.VMEM((n1, n2, two, cols), B16), pltpu.VMEM((n2, two, cols), B16), pltpu.VMEM((n2, two, cols), B16),
                         pltpu.VMEM((2, two // 2, cols), F32), pltpu.VMEM((two // 2, cols), F32),
                         pltpu.SemaphoreType.DMA((2, n1 + n2 + 1))]
-            jobs.append((n, o, half, arrived, plane_first, first, cols, at))
+            jobs.append((n, o, half, arrived, plane_first, first, cols, at, unit, where))
     return scratch, [outs[o] for o in sorted(outs)], jobs
 
 
 def make_sums(plane, jobs, parts, outs, scratch):
     sums = []
-    for i, (n, o, half, arrived, plane_first, first, cols, at) in enumerate(jobs):
+    for i, (n, o, half, arrived, plane_first, first, cols, at, unit, where) in enumerate(jobs):
         s = Sum(plane, plane_first, parts[n], outs[o], (first, cols), half, *scratch[6 * i:6 * i + 6])
-        s.at, s.arrived = at, arrived
+        s.at, s.arrived, s.unit, s.where = at, arrived, unit, where
         sums.append(s)
     return sums
 
@@ -580,19 +583,34 @@
             send_blocks(plane, i, a, gqb, gq_out, qs, qr, ql)
         def done_kv(t, b):
             send_blocks(plane, i, b, gkb, gkv_out, xs, xr, xl)
-            @pl.when(jnp.logical_and(i == 0, t == 0))
+            at = lambda call_, step_: pl.when(jnp.logical_and(i == call_, t == step_))
+            last_call = calls - 1
+            @at(0, 0)
             def _():
                 for s in early:
                     s.fetch().wait()
                     s.middle()
-            @pl.when(jnp.logical_and(i == calls - 1, t == 4))
+            @at(0, 7 if last_call else 3)
+            def _():
+                for s in late:
+                    if s.plane_first:
+                        s.wait(1)
+                        s.middle()
+            @at(last_call, 4)
             def _():
                 for s in early:
                     s.wait(2)
                     s.last()
                 for s in late:
-                    s.wait(1)
-                    s.middle()
+                    if not s.plane_first:
+                        s.wait(1)
+                        s.middle()
+            @at(last_call, 6)
+            def _():
+                for s in late:
+                    if s.plane_first:
+                        s.wait(2)
+                        s.last()
         flash_backward(xv.at[i], gov.at[i], otv.at[i], lse_ref.at[i], cos_ref, sin_ref, gqb.at[i], gkb.at[i],
                        qm, dom, kf, vf, kt, delta, dqt, dka, dva, done_q, done_kv)
         return 0
@@ -601,8 +619,9 @@
         for k in range(1, plane.size):
             go_copy(i, k, go_send[i - 1]).wait_send()
     for s in late:
-        s.wait(2)
-        s.last()
+        if not s.plane_first:
+            s.wait(2)
+            s.last()
     for s in sums:
         s.close()
     wait_blocks(plane, calls, gqb, gq_out, qs, qr, ql)
@@ -636,7 +655,7 @@
 
 
 def mlp_kernel(a_ref, x_hbm, g_hbm, mod_ref, wo_ref, bo_ref, wu_ref, bu_ref, wd_ref, bd_ref,
-               y_out, gm_out, ga_out, go_out, pd_out, ugot, vgot, po_out, sums_ref, du_ref, db_ref,
+               y_out, gm_out, ga_out, go_out, pd_out, ugot, vgot, pu_out, po_out, sums_ref, du_ref, db_ref,
                g, an, branch, mixed, h, gd, down, gh, st, gav, sd, su, rd, ru, kd, ku, pd, pu, *sems, calls):
     io, od, pair, free, done, gs, gr, gl, oo, us, ur, vr = sems
     plane = Plane()
@@ -736,7 +755,12 @@
             for k in range(1, nc):
                 c = lax.rem(mc + k, nc)
                 do(remote(pu.at[n, c], ugot.at[mc, :, :, cols], us.at[n, k], ur.at[mc], {"clip": c}), True)
-        @pl.when(j >= clip_first)
+        tail_at = steps - pu_out.shape[3] // hf
+        @pl.when(j >= tail_at)
+        def _():
+            cols = pl.ds(pl.multiple_of((j - tail_at) * hf, hf), hf)
+            do(pltpu.make_async_copy(pu.at[n], pu_out.at[:, :, :, cols], od.at[1, n]), False)
+        @pl.when(jnp.logical_and(j >= clip_first, j < tail_at))
         def _():
             cols = pl.ds(pl.multiple_of((j - clip_first) * hf, hf), hf)
             do(pltpu.make_async_copy(pu.at[n, :, mp], vgot.at[mp, :, :, cols], od.at[1, n]), False)
@@ -877,9 +901,9 @@
         in_specs=[whole(clips, hg, count, lw), hbm, hbm, whole(frames, 6, width), whole(width, width), whole(1, width),
                   pl.BlockSpec((width, fc), lambda j: (0, j)), pl.BlockSpec((1, fc), lambda j: (0, j)),
                   pl.BlockSpec((fc, width), lambda j: (j, 0)), whole(1, width)],
-        out_specs=[hbm] * 8 + [keep(frames, 4, width), pl.BlockSpec((1, fc), lambda j: (0, j)), keep(2, width)],
+        out_specs=[hbm] * 9 + [keep(frames, 4, width), pl.BlockSpec((1, fc), lambda j: (0, j)), keep(2, width)],
         out_shape=[s((rows, width), B16), s((rows, width), F32), s((max(1, calls - 1) * group, count, lw), B16),
-                   s((nf, nr, count, lw), B16), s((ff, hw), B16), s((nc, places, two_u, clip_first * hf), B16), s((places, nc, two_u, (steps - clip_first) * hf), B16), s((width, hw), B16),
+                   s((nf, nr, count, lw), B16), s((ff, hw), B16), s((nc, places, two_u, clip_first * hf), B16), s((places, nc, two_u, (steps - clip_first - 2) * hf), B16), s((nc, places, two_u, 2 * hf), B16), s((width, hw), B16),
                    s((frames, 4, width), F32), s((1, ff), F32), s((2, width), F32)],
         scratch_shapes=[v((tall, width), B16), v((tall, width), B16), v((rows, width), F32), v((rows, width), F32),
                         v((rows, width), B16), v((rows, width), B16), v((tall, width), F32), v((rows, width), F32), v((rows, 256), F32),
@@ -893,9 +917,9 @@
     )(attn, x, g, mods, w_out, b_out, w_up, b_up, w_down, b_down)
 
 
-def tail_kernel(gq_hbm, gkv_hbm, h_hbm, w_hbm, x_hbm, gm_hbm, mod_ref, clean_ref, sums2_ref, vec_ref,
-                o_out, gw_ref, noise_ref, vec_out,
-                gq, gkv, h, w, x, gm, full, gh, send, got, part, s1s, dbq, nsend, nrecv, vsend, v1, vmid, v2, io, pair, nsem, vsem, oo, *scratch, jobs):
+def tail_kernel(gq_hbm, gkv_hbm, h_hbm, w_hbm, x_hbm, gm_hbm, y_hbm, mod_ref, clean_ref, sums2_ref, vec_ref,
+                o_out, y_out, gw_ref, noise_ref, vec_out,
+                gq, gkv, h, w, x, gm, yv, ob, yb, full, gh, send, got, part, s1s, dbq, nsend, nrecv, vsend, v1, vmid, v2, io, pair, nsem, vsem, oo, *scratch, jobs):
     plane = Plane()
     clips, hg, count, lw = gq_hbm.shape
     w3 = 3 * lw
@@ -910,7 +934,7 @@
     blocks = hg // 2 // packed
     bw = packed * w3
     loads = [pltpu.make_async_copy(gq_hbm, gq, io.at[0]), pltpu.make_async_copy(gkv_hbm, gkv, io.at[5]), pltpu.make_async_copy(h_hbm, h, io.at[1]),
-             pltpu.make_async_copy(w_hbm, w, io.at[2]), pltpu.make_async_copy(x_hbm, x, io.at[3]), pltpu.make_async_copy(gm_hbm, gm, io.at[4])]
+             pltpu.make_async_copy(w_hbm, w, io.at[2]), pltpu.make_async_copy(x_hbm, x, io.at[3]), pltpu.make_async_copy(gm_hbm, gm, io.at[4]), pltpu.make_async_copy(y_hbm, yv, io.at[6])]
     for c in loads:
         c.start()
     sums = make_sums(plane, jobs, [part], [gw_ref], scratch)
@@ -929,10 +953,13 @@
     def swap(j):
         return remote(send.at[j], got.at[j], pair.at[0, j], pair.at[1, j], partner)
     other = 1 - bit
-    for j in range(blocks):
+    def give(j):
         send[j] = outer(other * blocks + j).astype(B16)
         swap(j).start()
-    for s in sums:
+    give(0)
+    for n, s in enumerate(sums):
+        if n + 1 < blocks:
+            give(n + 1)
         first, cols = s.cols
         j = first // bw
         total = outer(bit * blocks + j)
@@ -958,16 +985,20 @@
             ghf = gh[rows, :]
             t = ghf * (1.0 + mod_ref[cf, 1:2, :])
             back = t - jnp.mean(t, axis=1, keepdims=True) - n * jnp.mean(t * n, axis=1, keepdims=True)
-            gm[c, rows, :] = gm[c, rows, :] + inv * back
+            ob[f, :, c, :] = gm[c, rows, :] + inv * back
+            yb[f, :, c, :] = yv[c, rows, :]
             s = lambda v: jnp.sum(v, axis=0, keepdims=True)
             s1s[cf, 0:2, :] = jnp.concatenate([s(ghf), s(ghf * n)], axis=0)
             s1s[cf, 2:6, :] = sums2_ref[cf]
             return 0
         lax.fori_loop(0, frames, one, 0)
-        pltpu.make_async_copy(gm.at[c], o_out.at[c], oo.at[c]).start()
         for s in (sums[1:2] if c < clips - 1 else sums[2 if clips > 1 else 1:3]):
             s.wait(1)
             s.middle()
+
+    results = [pltpu.make_async_copy(ob, o_out, oo.at[0]), pltpu.make_async_copy(yb, y_out, oo.at[1])]
+    for c in results:
+        c.start()
 
     quarter = width // nr
     vsend[...] = jnp.zeros_like(vsend)
@@ -1037,17 +1068,18 @@
         s.close()
     for j in range(blocks):
         swap(j).wait_send()
-    for c in range(clips):
-        pltpu.make_async_copy(gm.at[c], o_out.at[c], oo.at[c]).wait()
-
-
-def tail(gq, gkv, h1, w_qkv, x, gmixed, mods, clean, sums2, vec):
+    for c in results:
+        c.wait()
+
+
+def tail(gq, gkv, h1, w_qkv, x, gmixed, y, mods, clean, sums2, vec):
     clips, hg, count, lw = gq.shape
     w3 = 3 * lw
     width = x.shape[2]
     nc, nf, nr = (lax.axis_size(a) for a in ALL)
     group = nf * nr
     frames = mods.shape[0]
+    fl, pt = frames // clips, count // (frames // clips)
     two = width // (nc * nf * nr // 2)
     packed = max(1, 128 * 3 // w3)
     blocks, bw = hg // 2 // packed, packed * w3
@@ -1056,21 +1088,22 @@
     s, v, dma = jax.ShapeDtypeStruct, pltpu.VMEM, pltpu.SemaphoreType.DMA
     shape = jax.ShapeDtypeStruct((nc, nf * nr // 2, two, blocks * bw), B16)
     order = [(False if j == 0 else True, j * bw, bw, j * bw) for j in range(blocks)]
-    scratch, outs, jobs = sum_plan([shape], [(0, blocks * bw, False, order)])
+    where = lambda b, u: u % 3 * width + (b * (hg // 2) + u // 3) * lw
+    scratch, outs, jobs = sum_plan([shape], [(0, blocks * bw, False, order, lw, where)])
     return pl.pallas_call(
         functools.partial(tail_kernel, jobs=jobs),
-        in_specs=[hbm] * 6 + [vmem] * 4,
-        out_specs=[hbm, vmem, vmem, vmem],
-        out_shape=[s((clips, count, width), F32)] + outs + [s((frames, 6, width // nr), F32), s((vrows, width), F32)],
+        in_specs=[hbm] * 7 + [vmem] * 4,
+        out_specs=[hbm, hbm, vmem, vmem, vmem],
+        out_shape=[s((fl, pt, clips, width), F32), s((fl, pt, clips, width), B16)] + outs + [s((frames, 6, width // nr), F32), s((vrows, width), F32)],
         scratch_shapes=[v((clips, hg, count, lw), B16), v((clips, hg, count, 2 * lw), B16), v((clips, count, width), B16), v((width, 3 * width), B16), v((clips, count, width), B16),
-                        v((clips, count, width), F32), v((count, 3 * width), B16), v((count, width), F32), v((blocks, width, bw), B16),
+                        v((clips, count, width), F32), v((clips, count, width), B16), v((fl, pt, clips, width), F32), v((fl, pt, clips, width), B16), v((count, 3 * width), B16), v((count, width), F32), v((blocks, width, bw), B16),
                         v((blocks, width, bw), B16), v(shape.shape, B16), v((frames, 8, width), F32), v((1, 3 * width), F32),
                         v((nr, frames, 6, width // nr), B16), v((nr, frames, 6, width // nr), B16), v((vrows, width), F32), v((group, vrows, width), F32),
-                        v((vrows, width), F32), v((nc, vrows, width), F32), dma((6,)), dma((2, blocks)), dma((2, nr)), dma((2, group + nc)), dma((clips,))] + scratch,
+                        v((vrows, width), F32), v((nc, vrows, width), F32), dma((7,)), dma((2, blocks)), dma((2, nr)), dma((2, group + nc)), dma((2,))] + scratch,
         compiler_params=pltpu.CompilerParams(vmem_limit_bytes=62 << 20, collective_id=2, has_side_effects=True),
         cost_estimate=pl.CostEstimate(flops=12 * clips * count * width * width, bytes_accessed=40 * clips * count * width, transcendentals=0),
         name="tail",
-    )(gq, gkv, h1, w_qkv, x, gmixed, mods, clean, sums2, vec)
+    )(gq, gkv, h1, w_qkv, x, gmixed, y, mods, clean, sums2, vec)
 
 
 def on_device(tokens, context, noise_mod, clean_mod, w_qkv, b_qkv, w_out, b_out, w_up, b_up, w_down, b_down, cotangent):
@@ -1089,7 +1122,6 @@
 
     is_clean = (fi * frames + jnp.arange(frames))[None, :] < context[:, None]
     mods = jnp.where(is_clean[:, :, None, None], clean_mod[None, None], noise_mod.transpose(1, 0, 2, 3))
-    full = (clips, frames, patches, width)
     inputs = tokens.transpose(2, 0, 1, 3).reshape(clips, count, width)
     cots = cotangent.transpose(2, 0, 1, 3).reshape(clips, count, width)
 
@@ -1109,7 +1141,7 @@
 
     rows = clips * count
     by_frame = mods.reshape(clips * frames, 6, width)
-    y, gmixed, ga, go, part_down, got_up, got_up2, part_out, sums2, db_up, db_two = mlp(
+    y, gmixed, ga, go, part_down, got_up, got_up2, part_up, part_out, sums2, db_up, db_two = mlp(
         attn, inputs.reshape(rows, width), cots.reshape(rows, width), by_frame,
         w_out, row_of(b_out), w_up, row_of(b_up), w_down, row_of(b_down), calls, lead)
     go = go.reshape(lead + (lw,))
@@ -1120,18 +1152,21 @@
     places = group // 2
     first, second, hw = got_up.shape[3], got_up2.shape[3], width // 2
     as_blocks = lambda p: p.reshape(nc, places, p.shape[0] // (nc * places), p.shape[1])
-    parts = [as_blocks(part_down), got_up, got_up2, as_blocks(part_out)]
-    orders = [(0, hw, False, [(False, 0, hw // 2, 0), (True, hw // 2, hw // 2, hw // 2)]), (1, first + second, True, [(False, 0, first, 0)]),
-              (1, first + second, True, [(True, 0, second, first)]), (2, hw, False, [(False, 0, hw, 0)])]
+    parts = [as_blocks(part_down), got_up, got_up2, part_up, as_blocks(part_out)]
+    third, unit = part_up.shape[3], part_up.shape[3] // 2
+    half_up = first + second + third
+    by_half = lambda b, u: b * hw + u * (hw // 2)
+    by_chunk = lambda b, u: (2 * u + b) * unit
+    orders = [(0, hw, False, [(False, 0, hw // 2, 0), (True, hw // 2, hw // 2, hw // 2)], hw // 2, by_half),
+              (1, half_up, True, [(False, 0, first, 0)], unit, by_chunk),
+              (1, half_up, True, [(True, 0, second, first)], unit, by_chunk),
+              (1, half_up, False, [(True, 0, third, first + second)], unit, by_chunk),
+              (2, hw, False, [(False, 0, hw, 0)], hw // 2, by_half)]
     gq, gkv, gw_down, gw_up, gw_out = attention_backward(x, go, go_sends, ot, lse, cos_t, sin_t, parts, orders)
     gq, gkv = gq.reshape(clips, hg, count, lw), gkv.reshape(clips, hg, count, 2 * lw)
-    fc = min(512, w_up.shape[1])
-    gw_up = gw_up.reshape(gw_up.shape[0], 2, -1, fc // 2).transpose(0, 2, 1, 3).reshape(gw_up.shape[0], -1)
     clean = jnp.broadcast_to(is_clean.reshape(-1, 1, 1), (clips * frames, 1, width)).astype(F32)
     vec = jnp.concatenate([db_up.reshape(-1, width), db_two], axis=0)
-    gtokens, gw_qkv, noise, vec = tail(gq, gkv, h1, w_qkv, inputs, gmixed, by_frame, clean, sums2, vec)
-    per = gw_qkv.shape[0]
-    gw_qkv = gw_qkv.reshape(per, 2, hg // 2, 3, lw).transpose(0, 3, 1, 2, 4).reshape(per, 3 * width)
+    gtokens, output, gw_qkv, noise, vec = tail(gq, gkv, h1, w_qkv, inputs, gmixed, y.reshape(clips, count, width), by_frame, clean, sums2, vec)
     grad_noise = noise.reshape(clips, frames, 6, -1).transpose(1, 0, 2, 3)
     total = lax.axis_size(ALL)
     place = lax.axis_index(ALL)
@@ -1140,8 +1175,7 @@
     grad_clean = lax.dynamic_slice_in_dim(vec[:6], place * (width // total), width // total, 1)
     ff = w_up.shape[1] // width
     gb_qkv, gb_up, gb_out, gb_down = own(6, 3), own(9, ff), own(9 + ff, 1), own(10 + ff, 1)
-    back = lambda v: v.reshape(full).transpose(1, 2, 0, 3)
-    return (back(y), back(gtokens), grad_noise, grad_clean, gw_qkv, gb_qkv, gw_out, gb_out, gw_up, gb_up, gw_down, gb_down)
+    return (output, gtokens, grad_noise, grad_clean, gw_qkv, gb_qkv, gw_out, gb_out, gw_up, gb_up, gw_down, gb_down)
 
 
 def solution(mesh):

time: 460 us -> 450 us (0.978)
  Pallas kernels: 421 us -> 412 us
    reshape x5 -> x0, local copies, waits for them, and re-layouts: 13.4 us -> none  [the longest x2 11 us: on_device(): back = lambda v: v.reshape(full).transpose(1, 2, 0, 3)]
    unnamed x33 -> x38, local copies, waits for them, and re-layouts: 2.73 us -> 11.7 us
    pallas_call x1, Pallas kernels: 103 us -> 95.7 us  [mlp(): pl.pallas_call(functools.partial(mlp_kernel, calls=calls), grid=(ff // fc...]
where the time goes in v5:
time: 450 us; the launch traced here: 443 us
  Pallas kernels  412 us (92%)
  local copies, waits for them, and re-layouts  24.6 us (5%)
  other arithmetic  4.81 us (1%)
    pallas_call x1, Pallas kernels, attention_backward(): pl.pallas_call(functools.partial(bwd_all_kernel, calls=calls, count=len(p...  139 us
    pallas_call x1, Pallas kernels, attention_forward(): pl.pallas_call(functools.partial(fwd_all_kernel, calls=calls), in_specs=[...  107 us
    pallas_call x1, Pallas kernels, mlp(): pl.pallas_call(functools.partial(mlp_kernel, calls=calls), grid=(ff // fc...  95.7 us
    pallas_call x1, Pallas kernels, tail(): pl.pallas_call(functools.partial(tail_kernel, jobs=jobs), in_specs=[hbm]...  55.4 us
    pallas_call x1, Pallas kernels, qkv_forward(): pl.pallas_call(qkv_kernel, grid=(clips,), in_specs=[one(count, width), on...  14.7 us
    unnamed x38, local copies, waits for them, and re-layouts  11.7 us

profile of v5, /device:TPU:1, one launch (start us, length us, event | category | flops | bytes accessed | tf_op | source)
XLA Modules:
  0.0 442.6 jit_solution(2955272518196307027)
XLA Ops:
  0.7 2.3 copy.30
  4.0 14.7 %qkv.1 = (bf16[2,8,512,384]{3,2,1,0:T(8,128)(2,1)}, bf16[2,512,1024]{2,1,0:T(8,128)(2,1)S(1)}) custom-call(bf16[2,512,1024]{2,1,0:T(8,128)(2,1)S(1)} %bitcast.37, f32[2,8,6,1024]{3,2,1,0:T(8,128)S(1)} %bitcast_select_fusion.mod_ref, bf16[1024,3072]{1,0:T(8,128)(2,1)} %w_hbm.3, f32[1,3072]{1,0:T(1,128)S(1)} %bitcast.42, f32[512,128]{1,0:T(8,128)S(1)} %copy.32.cos_ref, ...), custom_call_target="tpu_custom_call" | custom-call | flops 6442450944 | bytes 16777216 | tf_op jit(solution)/shard_map/qkv/pallas_call | solution.py:294
  18.8 1.4 copy-done.3
  20.2 106.9 %attention_forward.1 = (bf16[2,2,4,8,64,384]{5,4,3,2,1,0:T(8,128)(2,1)}, bf16[2,8,8,64,128]{4,3,2,1,0:T(8,128)(2,1)}, f32[2,128,4096]{2,1,0:T(8,128)}, f32[2,2,4096]{2,1,0:T(2,128)}) custom-call(bf16[2,8,8,64,384]{4,3,2,1,0:T(8,128)(2,1)} %bitcast.54), custom_call_target="tpu_custom_call" | custom-call | flops 8589934592 | bytes 25165824 | tf_op jit(solution)/shard_map/attention_forward/pallas_call | solution.py:411
  127.1 2.0 copy.35
  129.0 95.7 %mlp.1 = (bf16[1024,1024]{1,0:T(8,128)(2,1)}, f32[1024,1024]{1,0:T(8,128)}, bf16[8,512,128]{2,1,0:T(8,128)(2,1)}, bf16[2,4,512,128]{3,2,1,0:T(8,128)(2,1)}, bf16...) custom-call(bf16[2,8,512,128]{3,2,1,0:T(8,128)(2,1)} %bitcast.60, ...), custom_call_target="tpu_custom_call" | custom-call | flops 57982058496 | bytes 54525952 | tf_op jit(solution)/shard_map/mlp/pallas_call | solution.py:898
  224.8 2.9 fusion
  227.7 139.2 %attention_backward.1 = (bf16[2,8,8,64,128]{4,3,2,1,0:T(8,128)(2,1)}, bf16[2,8,8,64,256]{4,3,2,1,0:T(8,128)(2,1)}, f32[128,1024]{1,0:T(8,128)}, f32[32,4096]{1,0:T(8,128)}, f32[32,1024]{1,0:T(8,128)}) custom-call(bf16[2,2,4,8,64,384]{5,4,3,2,1,0:T(8,128)(2,1)} %get-tuple-element.41.refs_0_, bf16[2,4,8,64,128]{4,3,2,1,0:T(8,128)(2,1)} %bitcast.62, ...), custom_call_target="tpu_custom_call" | custom-call | flops 21474836480 | bytes 50331648 | tf_op jit(solution)/shard_map/attention_backward/pallas_call | solution.py:642
  367.0 0.7 broadcast_in_dim.139.clean_ref
  368.2 0.7 reduce.3
  369.0 0.6 pad_maximum_fusion.2.vec_ref
  369.6 55.4 %tail.1 = (f32[8,64,2,1024]{3,2,1,0:T(2,128)}, bf16[8,64,2,1024]{3,2,1,0:T(2,128)(2,1)}, f32[32,3072]{1,0:T(8,128)}, f32[16,6,256]{2,1,0:T(8,128)}, f32[16,1024]{1,0:T(8,128)}) custom-call(bf16[2,8,512,128]{3,2,1,0:T(8,128)(2,1)} %bitcast.59, bf16[2,8,512,256]{3,2,1,0:T(8,128)(2,1)} %bitcast.56, bf16[2,512,1024]{2,1,0:T(8,128)(2,1)} %copy-done.3, ...), custom_call_target="tpu_custom_call" | custom-call | flops 12884901888 | bytes 41943040 | tf_op jit(solution)/shard_map/tail/pallas_call | solution.py:1093
  425.0 1.6 copy.41
  426.6 0.8 slice.15
  427.4 0.7 constant_dynamic-slice_fusion.2
  428.0 0.8 slice.16
  429.5 0.8 fusion.37
  430.9 0.8 slice_bitcast_fusion
  432.8 4.5 %copy.49 = bf16[8,64,2,1024]{3,2,1,0:T(2,128)(2,1)} copy(bf16[8,64,2,1024]{3,2,1,0:T(2,128)(2,1)} %get-tuple-element.95) | data formatting | bytes 4194304
  437.3 2.0 copy.50
  439.4 0.7 copy.51
  440.1 0.7 copy.52
  440.8 0.8 copy.53
  441.6 0.8 copy.54
  (54 shorter events, 3.9 us)
Async XLA Ops:
  0.6 2.4 copy-start.14
  0.7 2.4 copy-start.8
  0.7 2.4 copy-start.11
  3.0 15.8 %copy-start = (bf16[2,8,64,1024]{3,2,1,0:T(8,128)(2,1)}, bf16[2,8,64,1024]{3,2,1,0:T(8,128)(2,1)S(1)}, u32[]{:S(2)}) copy-start(bf16[2,8,64,1024]{3,2,1,0:T(8,128)(2,1)S(1)} %copy.30) | copy-start | bytes 6291460
  3.0 1.0 copy-start.2
  3.2 15.5 %copy-start.1 = (f32[2,8,6,1024]{3,2,1,0:T(8,128)}, f32[2,8,6,1024]{3,2,1,0:T(8,128)S(1)}, u32[]{:S(2)}) copy-start(f32[2,8,6,1024]{3,2,1,0:T(8,128)S(1)} %bitcast_select_fusion.mod_ref) | copy-start | bytes 1179652
  18.8 1.4 copy-start.3
  20.2 106.9 %copy-start.5 = (bf16[8,64,2,1024]{3,2,1,0:T(2,128)(2,1)S(1)}, bf16[8,64,2,1024]{3,2,1,0:T(2,128)(2,1)}, u32[]{:S(2)}) copy-start(bf16[8,64,2,1024]{3,2,1,0:T(2,128)(2,1)} %param.25) | copy-start | bytes 6291460
  227.7 140.6 %copy-start.12 = (f32[1,4096]{1,0:T(1,128)S(1)}, f32[1,4096]{1,0:T(1,128)}, u32[]{:S(2)}) copy-start(f32[1,4096]{1,0:T(1,128)} %get-tuple-element.58) | copy-start | bytes 49156
  227.7 141.3 %copy-start.13 = (f32[2,1024]{1,0:T(2,128)S(1)}, f32[2,1024]{1,0:T(2,128)}, u32[]{:S(2)}) copy-start(f32[2,1024]{1,0:T(2,128)} %get-tuple-element.59) | copy-start | bytes 24580
  432.8 4.5 %copy-start.4 = (f32[8,64,2,1024]{3,2,1,0:T(2,128)S(1)}, f32[8,64,2,1024]{3,2,1,0:T(2,128)}, u32[]{:S(2)}) copy-start(f32[8,64,2,1024]{3,2,1,0:T(2,128)} %get-tuple-element.96) | copy-start | bytes 12582916
  437.3 2.0 copy-start.9
  437.3 2.8 copy-start.10
  437.3 3.4 copy-start.7
  439.4 2.2 copy-start.6

commit v6 on v5

--- a/solution.py
+++ b/solution.py
@@ -70,23 +70,25 @@
             acc[hs, tok:] = a0[:, tok:] + a1
         else:
             ll = zero8
-        def score(b, mm):
-            rows = pl.ds(pl.multiple_of(b * blk, blk), blk)
+        def score(b, mm, size=1):
+            rows = pl.ds(pl.multiple_of(b * blk, blk), size * blk)
             s = dot(kf[rows, :], qm[nhd, ncols, :], NT)
             (sa, sb)[ns][rows, :] = s
             return jnp.maximum(mm, fold(s, jnp.max))
-        def body(b, carry):
+        def body(b, carry, size=1):
             mm, ll = carry
             if nxt is not None:
-                mm = score(b, mm)
+                mm = score(b, mm, size)
             if cur is not None:
-                rows = pl.ds(pl.multiple_of(b * blk, blk), blk)
+                rows = pl.ds(pl.multiple_of(b * blk, blk), size * blk)
                 p = jnp.exp((sa, sb)[cs][rows, :] - m)
                 ll = ll + fold(p, jnp.sum)
                 acc[hs, :] += dot(vt[hs, rows], p.astype(jnp.bfloat16), NN)
             return mm, ll
         trip = nxt[0] if cur is None else cur[0]
-        mm, ll = lax.fori_loop(0, trip, body, (mm, ll))
+        pairs = trip // 2
+        mm, ll = lax.fori_loop(0, pairs, lambda n, carry: body(2 * n, carry, 2), (mm, ll))
+        mm, ll = lax.fori_loop(2 * pairs, trip, body, (mm, ll))
         if grow and nxt is not None:
             mm = score(cur[0], mm)
         if nxt is not None:
@@ -204,7 +206,19 @@
             def _():
                 store_q(a)
             return 0
-        lax.fori_loop(b + 1, count, q_block, 0)
+        def q_two(n, _):
+            a = b + 1 + 2 * n
+            dk, dv = work(k0, blk, pl.multiple_of(a * blk, blk), 2 * blk)
+            dka[...] += dk
+            dva[...] += dv
+            @pl.when(t == count - 1)
+            def _():
+                store_q(a)
+                store_q(a + 1)
+            return 0
+        todo = (count - 1 - b) // 2
+        lax.fori_loop(0, todo, q_two, 0)
+        lax.fori_loop(b + 1 + 2 * todo, count, q_block, 0)
         cols = pl.ds(k0, blk)
         dk = rotate_back(dka[...].T, cos_ref[:, cols], sin_ref[:, cols], nh).T.astype(jnp.bfloat16)
         dv = dva[...].astype(jnp.bfloat16)
@@ -953,25 +967,29 @@
     def swap(j):
         return remote(send.at[j], got.at[j], pair.at[0, j], pair.at[1, j], partner)
     other = 1 - bit
-    def give(j):
-        send[j] = outer(other * blocks + j).astype(B16)
-        swap(j).start()
-    give(0)
-    for n, s in enumerate(sums):
-        if n + 1 < blocks:
-            give(n + 1)
-        first, cols = s.cols
-        j = first // bw
-        total = outer(bit * blocks + j)
-        swap(j).wait_recv()
-        total = (total + got[j].astype(F32)).astype(B16)
-        part[:, :, :, first:first + cols] = total.reshape(part.shape[:3] + (cols,))
-        s.start(1)
+    def block(n, _):
+        @pl.when(n < blocks)
+        def _():
+            send[n] = outer(other * blocks + n).astype(B16)
+            swap(n).start()
+        @pl.when(n > 0)
+        def _():
+            j = n - 1
+            total = outer(bit * blocks + j)
+            swap(j).wait_recv()
+            total = (total + got[j].astype(F32)).astype(B16)
+            part[:, :, :, pl.ds(pl.multiple_of(j * bw, 128), bw)] = total.reshape(part.shape[:3] + (bw,))
+            for k, s in enumerate(sums):
+                @pl.when(j == k)
+                def _():
+                    s.start(1)
+        return 0
+    lax.fori_loop(0, blocks + 1, block, 0)
 
     for c in loads[3:]:
         c.wait()
     dbq[...] = jnp.zeros_like(dbq)
-    for c in range(clips):
+    def clip_back(c, _):
         for g in range(hg):
             full[:, g * lw:(g + 1) * lw] = gq[c, g]
             for j in range(2):
@@ -985,16 +1003,25 @@
             ghf = gh[rows, :]
             t = ghf * (1.0 + mod_ref[cf, 1:2, :])
             back = t - jnp.mean(t, axis=1, keepdims=True) - n * jnp.mean(t * n, axis=1, keepdims=True)
-            ob[f, :, c, :] = gm[c, rows, :] + inv * back
-            yb[f, :, c, :] = yv[c, rows, :]
+            new, out = gm[c, rows, :] + inv * back, yv[c, rows, :]
+            for m in range(clips):
+                @pl.when(c == m)
+                def _():
+                    ob[f, :, m, :] = new
+                    yb[f, :, m, :] = out
             s = lambda v: jnp.sum(v, axis=0, keepdims=True)
             s1s[cf, 0:2, :] = jnp.concatenate([s(ghf), s(ghf * n)], axis=0)
             s1s[cf, 2:6, :] = sums2_ref[cf]
             return 0
         lax.fori_loop(0, frames, one, 0)
-        for s in (sums[1:2] if c < clips - 1 else sums[2 if clips > 1 else 1:3]):
-            s.wait(1)
-            s.middle()
+        for n in range(clips):
+            @pl.when(c == n)
+            def _():
+                for s in (sums[1:2] if n < clips - 1 else sums[2 if clips > 1 else 1:3]):
+                    s.wait(1)
+                    s.middle()
+        return 0
+    lax.fori_loop(0, clips, clip_back, 0)
 
     results = [pltpu.make_async_copy(ob, o_out, oo.at[0]), pltpu.make_async_copy(yb, y_out, oo.at[1])]
     for c in results:

time: 450 us -> 447 us (level)
  no operation moved by 1% of the time
where the time goes in v6:
time: 447 us; the launch traced here: 439 us
  Pallas kernels  408 us (91%)
  local copies, waits for them, and re-layouts  24.6 us (6%)
  other arithmetic  4.81 us (1%)
    pallas_call x1, Pallas kernels, attention_backward(): pl.pallas_call(functools.partial(bwd_all_kernel, calls=calls, count=len(p...  136 us
    pallas_call x1, Pallas kernels, attention_forward(): pl.pallas_call(functools.partial(fwd_all_kernel, calls=calls), in_specs=[...  106 us
    pallas_call x1, Pallas kernels, mlp(): pl.pallas_call(functools.partial(mlp_kernel, calls=calls), grid=(ff // fc...  95.5 us
    pallas_call x1, Pallas kernels, tail(): pl.pallas_call(functools.partial(tail_kernel, jobs=jobs), in_specs=[hbm]...  55.7 us
    pallas_call x1, Pallas kernels, qkv_forward(): pl.pallas_call(qkv_kernel, grid=(clips,), in_specs=[one(count, width), on...  14.7 us
    unnamed x38, local copies, waits for them, and re-layouts  11.7 us

profile of v6, /device:TPU:1, one launch (start us, length us, event | category | flops | bytes accessed | tf_op | source)
XLA Modules:
  0.0 438.7 jit_solution(10512868686863619301)
XLA Ops:
  0.7 2.3 copy.30
  4.0 14.7 %qkv.1 = (bf16[2,8,512,384]{3,2,1,0:T(8,128)(2,1)}, bf16[2,512,1024]{2,1,0:T(8,128)(2,1)S(1)}) custom-call(bf16[2,512,1024]{2,1,0:T(8,128)(2,1)S(1)} %bitcast.37, f32[2,8,6,1024]{3,2,1,0:T(8,128)S(1)} %bitcast_select_fusion.mod_ref, bf16[1024,3072]{1,0:T(8,128)(2,1)} %w_hbm.3, f32[1,3072]{1,0:T(1,128)S(1)} %bitcast.42, f32[512,128]{1,0:T(8,128)S(1)} %copy.32.cos_ref, ...), custom_call_target="tpu_custom_call" | custom-call | flops 6442450944 | bytes 16777216 | tf_op jit(solution)/shard_map/qkv/pallas_call | solution.py:308
  18.8 1.4 copy-done.3
  20.2 105.9 %attention_forward.1 = (bf16[2,2,4,8,64,384]{5,4,3,2,1,0:T(8,128)(2,1)}, bf16[2,8,8,64,128]{4,3,2,1,0:T(8,128)(2,1)}, f32[2,128,4096]{2,1,0:T(8,128)}, f32[2,2,4096]{2,1,0:T(2,128)}) custom-call(bf16[2,8,8,64,384]{4,3,2,1,0:T(8,128)(2,1)} %bitcast.54), custom_call_target="tpu_custom_call" | custom-call | flops 8589934592 | bytes 25165824 | tf_op jit(solution)/shard_map/attention_forward/pallas_call | solution.py:425
  126.1 2.0 copy.35
  128.0 95.5 %mlp.1 = (bf16[1024,1024]{1,0:T(8,128)(2,1)}, f32[1024,1024]{1,0:T(8,128)}, bf16[8,512,128]{2,1,0:T(8,128)(2,1)}, bf16[2,4,512,128]{3,2,1,0:T(8,128)(2,1)}, bf16...) custom-call(bf16[2,8,512,128]{3,2,1,0:T(8,128)(2,1)} %bitcast.60, ...), custom_call_target="tpu_custom_call" | custom-call | flops 57982058496 | bytes 54525952 | tf_op jit(solution)/shard_map/mlp/pallas_call | solution.py:912
  223.6 2.9 fusion
  226.5 136.0 %attention_backward.1 = (bf16[2,8,8,64,128]{4,3,2,1,0:T(8,128)(2,1)}, bf16[2,8,8,64,256]{4,3,2,1,0:T(8,128)(2,1)}, f32[128,1024]{1,0:T(8,128)}, f32[32,4096]{1,0:T(8,128)}, f32[32,1024]{1,0:T(8,128)}) custom-call(bf16[2,2,4,8,64,384]{5,4,3,2,1,0:T(8,128)(2,1)} %get-tuple-element.41.refs_0_, bf16[2,4,8,64,128]{4,3,2,1,0:T(8,128)(2,1)} %bitcast.62, ...), custom_call_target="tpu_custom_call" | custom-call | flops 21474836480 | bytes 50331648 | tf_op jit(solution)/shard_map/attention_backward/pallas_call | solution.py:656
  362.5 0.7 broadcast_in_dim.139.clean_ref
  363.8 0.7 reduce.3
  364.5 0.6 pad_maximum_fusion.2.vec_ref
  365.1 55.7 %tail.1 = (f32[8,64,2,1024]{3,2,1,0:T(2,128)}, bf16[8,64,2,1024]{3,2,1,0:T(2,128)(2,1)}, f32[32,3072]{1,0:T(8,128)}, f32[16,6,256]{2,1,0:T(8,128)}, f32[16,1024]{1,0:T(8,128)}) custom-call(bf16[2,8,512,128]{3,2,1,0:T(8,128)(2,1)} %bitcast.59, bf16[2,8,512,256]{3,2,1,0:T(8,128)(2,1)} %bitcast.56, bf16[2,512,1024]{2,1,0:T(8,128)(2,1)} %copy-done.3, ...), custom_call_target="tpu_custom_call" | custom-call | flops 12884901888 | bytes 41943040 | tf_op jit(solution)/shard_map/tail/pallas_call | solution.py:1120
  420.9 1.6 copy.41
  422.5 0.8 slice.15
  423.3 0.7 constant_dynamic-slice_fusion.2
  423.9 0.8 slice.16
  425.4 0.8 fusion.37
  426.8 0.8 slice_bitcast_fusion
  428.7 4.5 %copy.49 = bf16[8,64,2,1024]{3,2,1,0:T(2,128)(2,1)} copy(bf16[8,64,2,1024]{3,2,1,0:T(2,128)(2,1)} %get-tuple-element.95) | data formatting | bytes 4194304
  433.3 2.0 copy.50
  435.3 0.7 copy.51
  436.0 0.7 copy.52
  436.7 0.8 copy.53
  437.5 0.8 copy.54
  (54 shorter events, 3.9 us)
Async XLA Ops:
  0.6 2.4 copy-start.14
  0.7 2.4 copy-start.8
  0.7 2.4 copy-start.11
  3.0 15.8 %copy-start = (bf16[2,8,64,1024]{3,2,1,0:T(8,128)(2,1)}, bf16[2,8,64,1024]{3,2,1,0:T(8,128)(2,1)S(1)}, u32[]{:S(2)}) copy-start(bf16[2,8,64,1024]{3,2,1,0:T(8,128)(2,1)S(1)} %copy.30) | copy-start | bytes 6291460
  3.0 1.0 copy-start.2
  3.2 15.5 %copy-start.1 = (f32[2,8,6,1024]{3,2,1,0:T(8,128)}, f32[2,8,6,1024]{3,2,1,0:T(8,128)S(1)}, u32[]{:S(2)}) copy-start(f32[2,8,6,1024]{3,2,1,0:T(8,128)S(1)} %bitcast_select_fusion.mod_ref) | copy-start | bytes 1179652
  18.8 1.4 copy-start.3
  20.2 105.9 %copy-start.5 = (bf16[8,64,2,1024]{3,2,1,0:T(2,128)(2,1)S(1)}, bf16[8,64,2,1024]{3,2,1,0:T(2,128)(2,1)}, u32[]{:S(2)}) copy-start(bf16[8,64,2,1024]{3,2,1,0:T(2,128)(2,1)} %param.25) | copy-start | bytes 6291460
  226.5 137.3 %copy-start.12 = (f32[1,4096]{1,0:T(1,128)S(1)}, f32[1,4096]{1,0:T(1,128)}, u32[]{:S(2)}) copy-start(f32[1,4096]{1,0:T(1,128)} %get-tuple-element.58) | copy-start | bytes 49156
  226.5 138.0 %copy-start.13 = (f32[2,1024]{1,0:T(2,128)S(1)}, f32[2,1024]{1,0:T(2,128)}, u32[]{:S(2)}) copy-start(f32[2,1024]{1,0:T(2,128)} %get-tuple-element.59) | copy-start | bytes 24580
  428.7 4.5 %copy-start.4 = (f32[8,64,2,1024]{3,2,1,0:T(2,128)S(1)}, f32[8,64,2,1024]{3,2,1,0:T(2,128)}, u32[]{:S(2)}) copy-start(f32[8,64,2,1024]{3,2,1,0:T(2,128)} %get-tuple-element.96) | copy-start | bytes 12582916
  433.2 2.0 copy-start.9
  433.2 2.8 copy-start.10
  433.2 3.4 copy-start.7
  435.3 2.2 copy-start.6

commit v7 on v6

--- a/solution.py
+++ b/solution.py
@@ -1079,7 +1079,7 @@
         total = nsend[plane.r, cf].astype(F32)
         for k in range(1, nr):
             total = total + nrecv[lax.rem(plane.r + k, nr), cf].astype(F32)
-        noise_ref[cf] = total
+        noise_ref[lax.rem(cf, frames), cf // frames] = total
         return 0
     lax.fori_loop(0, clips * frames, add_noise, 0)
     for s in sums:
@@ -1121,7 +1121,7 @@
         functools.partial(tail_kernel, jobs=jobs),
         in_specs=[hbm] * 7 + [vmem] * 4,
         out_specs=[hbm, hbm, vmem, vmem, vmem],
-        out_shape=[s((fl, pt, clips, width), F32), s((fl, pt, clips, width), B16)] + outs + [s((frames, 6, width // nr), F32), s((vrows, width), F32)],
+        out_shape=[s((fl, pt, clips, width), F32), s((fl, pt, clips, width), B16)] + outs + [s((fl, clips, 6, width // nr), F32), s((vrows, width), F32)],
         scratch_shapes=[v((clips, hg, count, lw), B16), v((clips, hg, count, 2 * lw), B16), v((clips, count, width), B16), v((width, 3 * width), B16), v((clips, count, width), B16),
                         v((clips, count, width), F32), v((clips, count, width), B16), v((fl, pt, clips, width), F32), v((fl, pt, clips, width), B16), v((count, 3 * width), B16), v((count, width), F32), v((blocks, width, bw), B16),
                         v((blocks, width, bw), B16), v(shape.shape, B16), v((frames, 8, width), F32), v((1, 3 * width), F32),
@@ -1131,6 +1131,24 @@
         cost_estimate=pl.CostEstimate(flops=12 * clips * count * width * width, bytes_accessed=40 * clips * count * width, transcendentals=0),
         name="tail",
     )(gq, gkv, h1, w_qkv, x, gmixed, y, mods, clean, sums2, vec)
+
+
+def head_tables(frames, grid):
+    pair = jnp.arange(32)[:, None]
+    is_time = pair < 8
+    is_height = (pair >= 8) & (pair < 20)
+    exponent = jnp.where(is_time, pair / 8.0, jnp.where(is_height, (pair - 8) / 12.0, (pair - 20) / 12.0)).astype(F32)
+    frequency = jnp.power(F32(10000.0), -exponent)
+    count = max(frames, grid)
+    angle = frequency * jnp.arange(count).astype(F32)[None, :]
+    token = jnp.arange(frames * grid * grid)[None, :]
+    position = jnp.where(is_time, token // (grid * grid), jnp.where(is_height, token // grid % grid, token % grid))
+    def spread(table):
+        out = jnp.broadcast_to(table[:, :1], position.shape)
+        for n in range(1, count):
+            out = jnp.where(position == n, table[:, n:n + 1], out)
+        return out
+    return spread(jnp.cos(angle)), spread(jnp.sin(angle))
 
 
 def on_device(tokens, context, noise_mod, clean_mod, w_qkv, b_qkv, w_out, b_out, w_up, b_up, w_down, b_down, cotangent):
@@ -1156,9 +1174,7 @@
     cos, sin = rope_angles(fi * frames + tok // patches, ri * patches + tok % patches, grid)
     cos_l = jnp.tile(jnp.concatenate([cos, cos], axis=1), (1, nh))
     sin_l = jnp.tile(jnp.concatenate([-sin, sin], axis=1), (1, nh))
-    every = jnp.arange(nf * frames * nr * patches)
-    cos_all, sin_all = rope_angles(every // (nr * patches), every % (nr * patches), grid)
-    cos_t, sin_t = cos_all.T, sin_all.T
+    cos_t, sin_t = head_tables(nf * frames, grid)
     row_of = lambda v: v.reshape(1, -1)
 
     lead = (nf, nr, frames, patches)
@@ -1194,7 +1210,6 @@
     clean = jnp.broadcast_to(is_clean.reshape(-1, 1, 1), (clips * frames, 1, width)).astype(F32)
     vec = jnp.concatenate([db_up.reshape(-1, width), db_two], axis=0)
     gtokens, output, gw_qkv, noise, vec = tail(gq, gkv, h1, w_qkv, inputs, gmixed, y.reshape(clips, count, width), by_frame, clean, sums2, vec)
-    grad_noise = noise.reshape(clips, frames, 6, -1).transpose(1, 0, 2, 3)
     total = lax.axis_size(ALL)
     place = lax.axis_index(ALL)
     def own(at, size):
@@ -1202,7 +1217,7 @@
     grad_clean = lax.dynamic_slice_in_dim(vec[:6], place * (width // total), width // total, 1)
     ff = w_up.shape[1] // width
     gb_qkv, gb_up, gb_out, gb_down = own(6, 3), own(9, ff), own(9 + ff, 1), own(10 + ff, 1)
-    return (output, gtokens, grad_noise, grad_clean, gw_qkv, gb_qkv, gw_out, gb_out, gw_up, gb_up, gw_down, gb_down)
+    return (output, gtokens, noise, grad_clean, gw_qkv, gb_qkv, gw_out, gb_out, gw_up, gb_up, gw_down, gb_down)
 
 
 def solution(mesh):

time: 447 us -> 444 us (level)
    unnamed x38 -> x41, local copies, waits for them, and re-layouts: 11.7 us -> 12.1 us
where the time goes in v7:
time: 444 us; the launch traced here: 436 us
  Pallas kernels  408 us (92%)
  local copies, waits for them, and re-layouts  21.8 us (5%)
  other arithmetic  5.05 us (1%)
    pallas_call x1, Pallas kernels, attention_backward(): pl.pallas_call(functools.partial(bwd_all_kernel, calls=calls, count=len(p...  136 us
    pallas_call x1, Pallas kernels, attention_forward(): pl.pallas_call(functools.partial(fwd_all_kernel, calls=calls), in_specs=[...  106 us
    pallas_call x1, Pallas kernels, mlp(): pl.pallas_call(functools.partial(mlp_kernel, calls=calls), grid=(ff // fc...  95.7 us
    pallas_call x1, Pallas kernels, tail(): pl.pallas_call(functools.partial(tail_kernel, jobs=jobs), in_specs=[hbm]...  55.6 us
    pallas_call x1, Pallas kernels, qkv_forward(): pl.pallas_call(qkv_kernel, grid=(clips,), in_specs=[one(count, width), on...  15 us
    unnamed x41, local copies, waits for them, and re-layouts  12.1 us

profile of v7, /device:TPU:1, one launch (start us, length us, event | category | flops | bytes accessed | tf_op | source)
XLA Modules:
  0.0 436.4 jit_solution(12070708944172880410)
XLA Ops:
  0.9 1.5 select_select_fusion.refs_5_
  2.4 1.5 select_select_fusion.1.refs_4_
  4.9 0.6 copy.30
  5.7 15.0 %qkv.1 = (bf16[2,8,512,384]{3,2,1,0:T(8,128)(2,1)}, bf16[2,512,1024]{2,1,0:T(8,128)(2,1)S(1)}) custom-call(bf16[2,512,1024]{2,1,0:T(8,128)(2,1)S(1)} %bitcast.97, f32[2,8,6,1024]{3,2,1,0:T(8,128)S(1)} %bitcast_select_fusion.mod_ref, bf16[1024,3072]{1,0:T(8,128)(2,1)} %w_hbm.3, f32[1,3072]{1,0:T(1,128)S(1)} %bitcast.102, f32[512,128]{1,0:T(8,128)S(1)} %copy.32.cos_ref, ...), custom_call_target="tpu_custom_call" | custom-call | flops 6442450944 | bytes 16777216 | tf_op jit(solution)/shard_map/qkv/pallas_call | solution.py:308
  20.8 106.0 %attention_forward.1 = (bf16[2,2,4,8,64,384]{5,4,3,2,1,0:T(8,128)(2,1)}, bf16[2,8,8,64,128]{4,3,2,1,0:T(8,128)(2,1)}, f32[2,128,4096]{2,1,0:T(8,128)}, f32[2,2,4096]{2,1,0:T(2,128)}) custom-call(bf16[2,8,8,64,384]{4,3,2,1,0:T(8,128)(2,1)} %bitcast.112), custom_call_target="tpu_custom_call" | custom-call | flops 8589934592 | bytes 25165824 | tf_op jit(solution)/shard_map/attention_forward/pallas_call | solution.py:425
  126.8 2.0 copy.35
  128.8 95.7 %mlp.1 = (bf16[1024,1024]{1,0:T(8,128)(2,1)}, f32[1024,1024]{1,0:T(8,128)}, bf16[8,512,128]{2,1,0:T(8,128)(2,1)}, bf16[2,4,512,128]{3,2,1,0:T(8,128)(2,1)}, bf16...) custom-call(bf16[2,8,512,128]{3,2,1,0:T(8,128)(2,1)} %bitcast.118, ...), custom_call_target="tpu_custom_call" | custom-call | flops 57982058496 | bytes 54525952 | tf_op jit(solution)/shard_map/mlp/pallas_call | solution.py:912
  224.5 136.0 %attention_backward.1 = (bf16[2,8,8,64,128]{4,3,2,1,0:T(8,128)(2,1)}, bf16[2,8,8,64,256]{4,3,2,1,0:T(8,128)(2,1)}, f32[128,1024]{1,0:T(8,128)}, f32[32,4096]{1,0:T(8,128)}, f32[32,1024]{1,0:T(8,128)}) custom-call(bf16[2,2,4,8,64,384]{5,4,3,2,1,0:T(8,128)(2,1)} %get-tuple-element.41.refs_0_, bf16[2,4,8,64,128]{4,3,2,1,0:T(8,128)(2,1)} %bitcast.120, ...), custom_call_target="tpu_custom_call" | custom-call | flops 21474836480 | bytes 50331648 | tf_op jit(solution)/shard_map/attention_backward/pallas_call | solution.py:656
  361.0 0.7 reduce.3
  361.8 0.6 pad_maximum_fusion.2.vec_ref
  362.5 0.7 broadcast_in_dim.427.clean_ref
  363.2 55.6 %tail.1 = (f32[8,64,2,1024]{3,2,1,0:T(2,128)}, bf16[8,64,2,1024]{3,2,1,0:T(2,128)(2,1)}, f32[32,3072]{1,0:T(8,128)}, f32[8,2,6,256]{3,2,1,0:T(8,128)}, f32[16,1024]{1,0:T(8,128)}) custom-call(bf16[2,8,512,128]{3,2,1,0:T(8,128)(2,1)} %bitcast.117, bf16[2,8,512,256]{3,2,1,0:T(8,128)(2,1)} %bitcast.114, bf16[2,512,1024]{2,1,0:T(8,128)(2,1)} %copy-done.3, ...), custom_call_target="tpu_custom_call" | custom-call | flops 12884901888 | bytes 41943040 | tf_op jit(solution)/shard_map/tail/pallas_call | solution.py:1120
  418.8 1.6 copy.36
  420.4 0.8 slice.143
  421.2 0.7 constant_dynamic-slice_fusion.2
  421.8 0.8 slice_bitcast_fusion
  423.2 0.8 slice.144
  424.6 0.8 fusion.46
  426.7 4.5 %copy.47 = bf16[8,64,2,1024]{3,2,1,0:T(2,128)(2,1)} copy(bf16[8,64,2,1024]{3,2,1,0:T(2,128)(2,1)} %get-tuple-element.151) | data formatting | bytes 4194304
  431.2 2.0 copy.48
  433.2 0.7 copy.49
  433.9 0.7 copy.50
  434.6 0.8 copy.51
  435.4 0.8 copy.52
  (61 shorter events, 4.2 us)
Async XLA Ops:
  0.6 4.0 copy-start.15
  0.7 4.1 copy-start.9
  0.7 4.1 copy-start.12
  2.4 2.5 copy-start.5
  4.9 0.9 copy-start.1
  4.9 0.9 copy-start.2
  5.5 15.2 %copy-start = (bf16[2,8,64,1024]{3,2,1,0:T(8,128)(2,1)}, bf16[2,8,64,1024]{3,2,1,0:T(8,128)(2,1)S(1)}, u32[]{:S(2)}) copy-start(bf16[2,8,64,1024]{3,2,1,0:T(8,128)(2,1)S(1)} %copy.30) | copy-start | bytes 6291460
  20.8 106.0 %copy-start.3 = (bf16[2,512,1024]{2,1,0:T(8,128)(2,1)}, bf16[2,512,1024]{2,1,0:T(8,128)(2,1)S(1)}, u32[]{:S(2)}) copy-start(bf16[2,512,1024]{2,1,0:T(8,128)(2,1)S(1)} %get-tuple-element.54.h_hbm) | copy-start | bytes 6291460
  20.8 106.0 %copy-start.6 = (bf16[8,64,2,1024]{3,2,1,0:T(2,128)(2,1)S(1)}, bf16[8,64,2,1024]{3,2,1,0:T(2,128)(2,1)}, u32[]{:S(2)}) copy-start(bf16[8,64,2,1024]{3,2,1,0:T(2,128)(2,1)} %param.25) | copy-start | bytes 6291460
  224.5 136.5 %copy-start.13 = (f32[1,4096]{1,0:T(1,128)S(1)}, f32[1,4096]{1,0:T(1,128)}, u32[]{:S(2)}) copy-start(f32[1,4096]{1,0:T(1,128)} %get-tuple-element.58) | copy-start | bytes 49156
  224.5 137.2 %copy-start.14 = (f32[2,1024]{1,0:T(2,128)S(1)}, f32[2,1024]{1,0:T(2,128)}, u32[]{:S(2)}) copy-start(f32[2,1024]{1,0:T(2,128)} %get-tuple-element.59) | copy-start | bytes 24580
  426.7 4.5 %copy-start.4 = (f32[8,64,2,1024]{3,2,1,0:T(2,128)S(1)}, f32[8,64,2,1024]{3,2,1,0:T(2,128)}, u32[]{:S(2)}) copy-start(f32[8,64,2,1024]{3,2,1,0:T(2,128)} %get-tuple-element.152) | copy-start | bytes 12582916
  431.2 2.0 copy-start.10
  431.2 2.8 copy-start.11
  431.2 3.4 copy-start.8
  433.2 2.2 copy-start.7
